TPU v7x, 256 devices: a whole 4x4x8 slice. The times are simulated.
256 devices in a mesh: sec: 2 (over x_hi), col: 8 (over y, x_lo), elem: 16 (over z, core).
Axes of the slice: x: 4 (x_hi: 2, x_lo: 2; x = x_hi * 2 + x_lo), y: 4, z: 8, core: 2. Of those that a mesh axis runs over, the one named last changes fastest.
Arguments:
- probes: float32 [256, 96, 256], P('col', 'elem'), may hold values from -6 to 6
- jacobian: float32 [2, 96, 7, 256, 256], P('sec', 'elem'), may hold values from -0.0625 to 0.0625
- neighbors: int32 [96, 7], P('elem'), may hold values from 0 to 95, as said below
- stations: int32 [1024], P('elem'), may hold values from 0 to 95, as said below
- obs_weights: float32 [1024, 256], P('elem'), may hold values from -0.75 to 0.75
Outputs:
- hess_probes: float32 [256, 96, 256], P('col', 'elem', 'sec')
- gram: float32 [256, 256], P('col')
Inputs may be any that keep to these rules, and one draw needn't show every extreme that they name: `neighbors`: row e lists the 7 elements e - 3 to e + 3, taken modulo 96, each once, in an order drawn for each row. Station i lies in one of the 6 elements from (i // 64) * 6 on; every element holds one or more stations.
All inputs are finite; a program needn't handle non-finite values.
Results may differ from a plain program's by a relative error of at most 0.0001.
Values sent between devices are 32-bit elements; how exact they have to be, the bound alone decides.
No kernel may reach another device: no remote copies, remote signals or barrier semaphores. Data moves between devices by JAX's collectives and lax.ppermute only.
A program may use at most 64 MiB of HBM per device.

v0:
```python
import jax
import jax.numpy as jnp
from jax import lax
from jax.sharding import PartitionSpec as P

NBRS = 7
STEPS = 2


PRECISE = lax.Precision.HIGHEST


def with_halo(shard, sides, width):
    for axis, dim in sides:
        devices, length = (lax.axis_size(axis), shard.shape[dim])
        up = [(i, (i + 1) % devices) for i in range(devices)]
        down = [(j, i) for i, j in up]
        last = lax.slice_in_dim(shard, length - width, length, axis=dim)
        leading = lax.slice_in_dim(shard, 0, width, axis=dim)
        before = lax.ppermute(last, axis, up)
        after = lax.ppermute(leading, axis, down)
        shard = jnp.concatenate([before, shard, after], axis=dim)
    return shard


def from_behind(value, axis, steps):
    count = lax.axis_size(axis)
    pairs = [(source, (source + steps) % count) for source in range(count)]
    return lax.ppermute(value, axis, pairs)


def from_behind_2(value, axis, steps):
    count = lax.axis_size(axis)
    leading, last = (max(0, -steps), min(count, count - steps))
    return lax.ppermute(value, axis, [(source, source + steps) for source in range(leading, last)])


def tangent_pass(vector, blocks, lookup, radius):
    column_count, elem_count, dof_count = vector.shape
    for repeat in range(STEPS):
        extended = with_halo(vector, (("elem", 1),), radius)
        gathered = jnp.take(extended, lookup, axis=1).reshape(
            column_count, elem_count, NBRS, dof_count
        )
        vector = vector + jnp.einsum("cekI,ekJI->ceJ", gathered, blocks, precision=PRECISE)
    return vector


def adjoint_pass(vector, blocks, scatter_table, radius):
    column_count, elem_count, dof_count = vector.shape
    for repeat in range(STEPS):
        products = jnp.einsum("ceJ,ekJI->cekI", vector, blocks, precision=PRECISE)
        flattened = products.reshape(column_count, elem_count * NBRS, dof_count)
        extended = jnp.einsum("cxI,xy->cyI", flattened, scatter_table, precision=PRECISE)
        left_rim = extended[:, :radius]
        right_rim = extended[:, elem_count + radius :]
        from_right = from_behind(left_rim, "elem", -1)
        from_left = from_behind(right_rim, "elem", 1)
        centre = extended[:, radius : radius + elem_count]
        centre = centre.at[:, :radius].add(from_left)
        centre = centre.at[:, elem_count - radius :].add(from_right)
        vector = vector + centre
    return vector


def observe(vector, station_table, obs_weights):
    sampled = jnp.einsum("se,ceI->csI", station_table, vector, precision=PRECISE)
    readings = jnp.einsum("csI,sI->cs", sampled, obs_weights, precision=PRECISE)
    weighted = readings[:, :, None] * obs_weights[None, :, :]
    return jnp.einsum("csI,se->ceI", weighted, station_table, precision=PRECISE)


def per_device(probes, jacobian, neighbors, stations, obs_weights):
    column_count, elem_count, dof_count = probes.shape
    radius = (NBRS - 1) // 2
    elem_total = elem_count * lax.axis_size("elem")
    first_elem = lax.axis_index("elem") * elem_count
    lookup = ((neighbors - first_elem + radius) % elem_total).reshape(-1)
    ext_ids = jnp.arange(elem_count + 2 * radius, dtype=jnp.int32)
    scatter_table = (lookup[:, None] == ext_ids[None, :]).astype(jnp.float32)
    local_ids = jnp.arange(elem_count, dtype=jnp.int32)
    station_table = ((stations - first_elem)[:, None] == local_ids[None, :]).astype(jnp.float32)
    segment_index = lax.axis_index("sec")
    leading = segment_index == 0
    half_order = dof_count // 2
    blocks = jacobian[0]
    batch_count = 1
    batch_list = [probes]
    rounds = batch_count + 1
    stored = []
    incoming = jnp.zeros_like(batch_list[0])
    for round_number in range(rounds):
        start_vector = batch_list[min(round_number, batch_count - 1)]
        inputs = jnp.where(leading, start_vector, incoming)
        output = tangent_pass(inputs, blocks, lookup, radius)
        stored.append(output)
        if round_number + 1 < rounds:
            incoming = from_behind_2(output, "sec", 1)
    results = []
    returning = jnp.zeros_like(batch_list[0])
    for round_number in range(rounds):
        state_now = jnp.where(
            leading, stored[max(round_number - 1, 0)], stored[min(round_number + 1, rounds - 1)]
        )
        inputs = returning + observe(state_now, station_table, obs_weights)
        output = adjoint_pass(inputs, blocks, scatter_table, radius)
        if round_number >= 1:
            results.append(output)
        if round_number + 1 < rounds:
            returning = from_behind_2(output, "sec", -1)
    hessian_all = results[0]
    upper_half = from_behind_2(hessian_all[:, :, half_order:], "sec", 1)
    hess_local = jnp.where(leading, hessian_all[:, :, :half_order], upper_half)
    probe_half = lax.dynamic_slice_in_dim(probes, segment_index * half_order, half_order, 2)
    scaling = 1.0 / (elem_total * dof_count)
    shard_piece = lax.all_gather(hess_local, "col", axis=0, tiled=True)
    flat_piece = shard_piece.reshape(shard_piece.shape[0], -1)
    partial_gram = jnp.einsum(
        "ax,bx->ab", probe_half.reshape(column_count, -1), flat_piece, precision=PRECISE
    )
    gram = lax.psum(partial_gram, ("sec", "elem")) * scaling
    return (hess_local, gram)


def solution(mesh):
    in_specs = (
        P("col", "elem", None),
        P("sec", "elem", None, None, None),
        P("elem", None),
        P("elem"),
        P("elem", None),
    )
    out_specs = (P("col", "elem", "sec"), P("col", None))
    return jax.shard_map(
        per_device, mesh=mesh, in_specs=in_specs, out_specs=out_specs, check_vma=False
    )
```

profile of v0, /device:TPU:6, one launch (start us, length us, event | category | flops | bytes accessed | tf_op | source)
XLA Modules:
  0.0 337.4 jit_solution(581083055440860766)
XLA Ops:
  0.7 5.3 %collective-permute-start.1 = (f32[32,3,256]{2,0,1:T(8,128)S(1)}, f32[32,3,256]{2,0,1:T(8,128)S(1)}, u32[]{:S(2)}, u32[]{:S(2)}) collective-permute-start(f32[32,3,256]{2,0,1:T(8,128)S(1)} %get-tuple-element.120), channel_id=1, source_target_pairs={{1,0},{2,1},{3,2},{4,3},{5,4},{6,5},{7,6},{8,7},{9,8},{10,9},{11,1... | collective-permute-start | bytes 294920 | tf_op jit(solution)/shard_map/ppermute | solution.py:21
  9.1 12.6 %fusion.61 = f32[32,6,256]{2,0,1:T(8,128)S(1)} fusion(f32[32,6,256]{2,0,1:T(8,128)S(1)} %broadcast_select_fusion.4, f32[32,6,7,256]{3,0,2,1:T(8,128)S(1)} %bitcast.149, f32[1,6,7,256,256]{4,3,2,1,0:T(8,128)} %param.24), kind=kOutput, calls=%fused_computation.44 | convolution fusion | flops 1057013760 | bytes 12779520 | tf_op jit(solution)/shard_map/cekI,ekJI->ceJ/dot_general | solution.py:45
  21.8 3.0 collective-permute-start.3
  28.0 12.7 %fusion.58 = f32[32,6,256]{2,0,1:T(8,128)S(1)} fusion(f32[32,6,256]{2,0,1:T(8,128)S(1)} %fusion.61, f32[32,6,7,256]{3,0,2,1:T(8,128)S(1)} %bitcast.150, f32[1,6,7,256,256]{4,3,2,1,0:T(8,128)} %param.24), kind=kOutput, calls=%fused_computation.43 | convolution fusion | flops 1057013760 | bytes 12779520 | tf_op jit(solution)/shard_map/cekI,ekJI->ceJ/dot_general | solution.py:45
  42.1 7.6 %collective-permute-done.4 = f32[32,6,256]{2,0,1:T(8,128)S(1)} collective-permute-done((f32[32,6,256]{2,0,1:T(8,128)S(1)}, f32[32,6,256]{2,0,1:T(8,128)S(1)}, u32[]{:S(2)}, u32[]{:S(2)}) %collective-permute-start.4) | collective-permute-done | bytes 196640 | tf_op jit(solution)/shard_map/ppermute | solution.py:35
  49.8 2.9 collective-permute-start.6
  55.9 12.6 %fusion.55 = f32[32,6,256]{2,0,1:T(8,128)S(1)} fusion(f32[32,6,256]{2,0,1:T(8,128)S(1)} %broadcast_select_fusion.5, f32[32,6,7,256]{3,0,2,1:T(8,128)S(1)} %bitcast.151, f32[1,6,7,256,256]{4,3,2,1,0:T(8,128)} %param.24), kind=kOutput, calls=%fused_computation.42 | convolution fusion | flops 1057013760 | bytes 12779520 | tf_op jit(solution)/shard_map/cekI,ekJI->ceJ/dot_general | solution.py:45
  68.6 3.0 collective-permute-start.8
  74.7 12.9 %fusion.64 = f32[32,6,256]{2,0,1:T(8,128)S(1)} fusion(f32[32,6,256]{2,0,1:T(8,128)S(1)} %fusion.58, f32[32,6,256]{2,0,1:T(8,128)S(1)} %fusion.55, f32[32,6,7,256]{3,0,2,1:T(8,128)S(1)} %bitcast.148, f32[1,6,7,256,256]{4,3,2,1,0:T(8,128)} %param.24, pred[]{:T(512)S(6)} %eq.16), kind=kOutput, calls=%fused_computation.45 | convolution fusion | flops 1057062912 | bytes 12976129 | tf_op jit(solution)/shard_map/cekI,ekJI->ceJ/dot_general | solution.py:45
  88.6 3.1 fusion.16
  92.7 9.0 %fusion.6 = f32[6,32,7,256]{3,1,2,0:T(8,128)S(1)} fusion(f32[1,6,7,256,256]{4,3,2,1,0:T(8,128)} %param.24, f32[32,6,256,1]{2,1,0,3:T(8,128)S(1)} %bitcast.143), kind=kOutput, calls=%fused_computation.10 | convolution fusion | flops 1056964608 | bytes 12582912 | tf_op jit(solution)/shard_map/ceJ,ekJI->cekI/dot_general | solution.py:52
  103.2 3.0 collective-permute-start.10
  109.6 9.0 %fusion.4 = f32[6,32,7,256]{3,1,2,0:T(8,128)S(1)} fusion(f32[1,6,7,256,256]{4,3,2,1,0:T(8,128)} %param.24, f32[32,6,256,1]{2,1,0,3:T(8,128)S(1)} %fusion.77), kind=kOutput, calls=%fused_computation.8 | convolution fusion | flops 1056964608 | bytes 12582912 | tf_op jit(solution)/shard_map/ceJ,ekJI->cekI/dot_general | solution.py:52
  120.1 3.0 collective-permute-start.12
  123.1 2.6 collective-permute-done.11
  127.9 3.9 %collective-permute-done.13 = f32[32,6,256]{2,1,0:T(8,128)S(1)} collective-permute-done((f32[32,6,256]{2,1,0:T(8,128)S(1)}, f32[32,6,256]{2,1,0:T(8,128)S(1)}, u32[]{:S(2)}, u32[]{:S(2)}) %collective-permute-start.13) | collective-permute-done | bytes 196640 | tf_op jit(solution)/shard_map/ppermute | solution.py:35
  131.8 9.3 %fusion.2 = f32[6,32,7,256]{3,1,2,0:T(8,128)S(1)} fusion(f32[1,6,7,256,256]{4,3,2,1,0:T(8,128)} %param.24, f32[32,6,256,1]{2,1,0,3:T(8,128)S(1)} %fusion.75), kind=kOutput, calls=%fused_computation.6 | convolution fusion | flops 1056964608 | bytes 12582912 | tf_op jit(solution)/shard_map/ceJ,ekJI->cekI/dot_general | solution.py:52
  142.6 3.0 collective-permute-start.15
  145.6 2.6 collective-permute-done.14
  149.0 9.0 %fusion = f32[6,32,7,256]{3,1,2,0:T(8,128)S(1)} fusion(f32[1,6,7,256,256]{4,3,2,1,0:T(8,128)} %param.24, f32[32,6,256,1]{2,1,0,3:T(8,128)S(1)} %fusion.96), kind=kOutput, calls=%fused_computation.4 | convolution fusion | flops 1056964608 | bytes 12582912 | tf_op jit(solution)/shard_map/ceJ,ekJI->cekI/dot_general | solution.py:52
  159.5 3.0 collective-permute-start.17
  167.2 7.6 %collective-permute-done.18 = f32[32,6,128]{2,1,0:T(8,128)S(1)} collective-permute-done((f32[32,6,128]{2,1,0:T(8,128)S(1)}, f32[32,6,128]{2,1,0:T(8,128)S(1)}, u32[]{:S(2)}, u32[]{:S(2)}) %collective-permute-start.18) | collective-permute-done | bytes 98336 | tf_op jit(solution)/shard_map/ppermute | solution.py:35
  174.9 32.1 %all_gather.3 = f32[256,6,128]{2,0,1:T(8,128)S(1)} all-gather(f32[32,6,128]{2,0,1:T(8,128)S(1)} %copy.37), channel_id=1, replica_groups=mesh['sec'=2,'col'=8,'elem'=16] {'col'}, dimensions={0}, use_global_device_ids=true | all-gather | bytes 884736 | tf_op jit(solution)/shard_map/all_gather | solution.py:116
  207.8 128.5 %psum.7 = f32[32,256]{1,0:T(8,128)S(1)} all-reduce(f32[32,256]{1,0:T(8,128)S(1)} %convolution_bitcast_fusion.1), channel_id=1, replica_groups=mesh['sec'=2,'col'=8,'elem'=16] {'sec','elem'}, use_global_device_ids=true, to_apply=%region_0.2 | all-reduce | flops 8192 | bytes 65536 | tf_op jit(solution)/shard_map/psum | solution.py:121
  (98 shorter events, 34.5 us)
Async XLA Ops:
  0.7 7.6 %collective-permute-start = (f32[32,3,256]{2,0,1:T(8,128)S(1)}, f32[32,3,256]{2,0,1:T(8,128)S(1)}, u32[]{:S(2)}, u32[]{:S(2)}) collective-permute-start(f32[32,3,256]{2,0,1:T(8,128)S(1)} %get-tuple-element.119), channel_id=1, source_target_pairs={{0,1},{1,2},{2,3},{3,4},{4,5},{5,6},{6,7},{7,8},{8,9},{9,10},{10,1... | collective-permute-start | bytes 294920 | tf_op jit(solution)/shard_map/ppermute | solution.py:20
  0.7 7.6 %collective-permute-start.1 = (f32[32,3,256]{2,0,1:T(8,128)S(1)}, f32[32,3,256]{2,0,1:T(8,128)S(1)}, u32[]{:S(2)}, u32[]{:S(2)}) collective-permute-start(f32[32,3,256]{2,0,1:T(8,128)S(1)} %get-tuple-element.120), channel_id=1, source_target_pairs={{1,0},{2,1},{3,2},{4,3},{5,4},{6,5},{7,6},{8,7},{9,8},{10,9},{11,1... | collective-permute-start | bytes 294920 | tf_op jit(solution)/shard_map/ppermute | solution.py:21
  21.8 5.3 %collective-permute-start.2 = (f32[32,3,256]{2,0,1:T(8,128)S(1)}, f32[32,3,256]{2,0,1:T(8,128)S(1)}, u32[]{:S(2)}, u32[]{:S(2)}) collective-permute-start(f32[32,3,256]{2,0,1:T(8,128)S(1)} %get-tuple-element.117), channel_id=1, source_target_pairs={{0,1},{1,2},{2,3},{3,4},{4,5},{5,6},{6,7},{7,8},{8,9},{9,10},{10,1... | collective-permute-start | bytes 294920 | tf_op jit(solution)/shard_map/ppermute | solution.py:20
  21.8 5.3 %collective-permute-start.3 = (f32[32,3,256]{2,0,1:T(8,128)S(1)}, f32[32,3,256]{2,0,1:T(8,128)S(1)}, u32[]{:S(2)}, u32[]{:S(2)}) collective-permute-start(f32[32,3,256]{2,0,1:T(8,128)S(1)} %get-tuple-element.118), channel_id=1, source_target_pairs={{1,0},{2,1},{3,2},{4,3},{5,4},{6,5},{7,6},{8,7},{9,8},{10,9},{11,1... | collective-permute-start | bytes 294920 | tf_op jit(solution)/shard_map/ppermute | solution.py:21
  28.0 21.8 %copy-start = (f32[32,6,256]{2,0,1:T(8,128)S(1)}, f32[32,6,256]{2,0,1:T(8,128)}, u32[]{:S(2)}) copy-start(f32[32,6,256]{2,0,1:T(8,128)} %param.23) | copy-start | bytes 589828
  40.6 9.1 %collective-permute-start.4 = (f32[32,6,256]{2,0,1:T(8,128)S(1)}, f32[32,6,256]{2,0,1:T(8,128)S(1)}, u32[]{:S(2)}, u32[]{:S(2)}) collective-permute-start(f32[32,6,256]{2,0,1:T(8,128)S(1)} %fusion.58), channel_id=1, source_target_pairs={{0,128},{1,129},{2,130},{3,131},{4,132},{5,133},{6,134},{7,135},{8... | collective-permute-start | bytes 589832 | tf_op jit(solution)/shard_map/ppermute | solution.py:35
  49.8 5.3 %collective-permute-start.5 = (f32[32,3,256]{2,0,1:T(8,128)S(1)}, f32[32,3,256]{2,0,1:T(8,128)S(1)}, u32[]{:S(2)}, u32[]{:S(2)}) collective-permute-start(f32[32,3,256]{2,0,1:T(8,128)S(1)} %get-tuple-element.115), channel_id=1, source_target_pairs={{0,1},{1,2},{2,3},{3,4},{4,5},{5,6},{6,7},{7,8},{8,9},{9,10},{10,1... | collective-permute-start | bytes 294920 | tf_op jit(solution)/shard_map/ppermute | solution.py:20
  49.8 5.2 %collective-permute-start.6 = (f32[32,3,256]{2,0,1:T(8,128)S(1)}, f32[32,3,256]{2,0,1:T(8,128)S(1)}, u32[]{:S(2)}, u32[]{:S(2)}) collective-permute-start(f32[32,3,256]{2,0,1:T(8,128)S(1)} %get-tuple-element.116), channel_id=1, source_target_pairs={{1,0},{2,1},{3,2},{4,3},{5,4},{6,5},{7,6},{8,7},{9,8},{10,9},{11,1... | collective-permute-start | bytes 294920 | tf_op jit(solution)/shard_map/ppermute | solution.py:21
  55.9 15.7 %copy-start.3 = (s32[64]{0:T(128)S(1)}, s32[64]{0:T(128)}, u32[]{:S(2)}) copy-start(s32[64]{0:T(128)} %param.26) | copy-start | bytes 772
  68.6 5.3 %collective-permute-start.7 = (f32[32,3,256]{2,0,1:T(8,128)S(1)}, f32[32,3,256]{2,0,1:T(8,128)S(1)}, u32[]{:S(2)}, u32[]{:S(2)}) collective-permute-start(f32[32,3,256]{2,0,1:T(8,128)S(1)} %get-tuple-element.113), channel_id=1, source_target_pairs={{0,1},{1,2},{2,3},{3,4},{4,5},{5,6},{6,7},{7,8},{8,9},{9,10},{10,1... | collective-permute-start | bytes 294920 | tf_op jit(solution)/shard_map/ppermute | solution.py:20
  68.6 5.2 %collective-permute-start.8 = (f32[32,3,256]{2,0,1:T(8,128)S(1)}, f32[32,3,256]{2,0,1:T(8,128)S(1)}, u32[]{:S(2)}, u32[]{:S(2)}) collective-permute-start(f32[32,3,256]{2,0,1:T(8,128)S(1)} %get-tuple-element.114), channel_id=1, source_target_pairs={{1,0},{2,1},{3,2},{4,3},{5,4},{6,5},{7,6},{8,7},{9,8},{10,9},{11,1... | collective-permute-start | bytes 294920 | tf_op jit(solution)/shard_map/ppermute | solution.py:21
  87.5 1.0 copy-start.2
  103.2 5.6 %collective-permute-start.9 = (f32[32,3,256]{2,1,0:T(4,128)S(1)}, f32[32,3,256]{2,1,0:T(4,128)S(1)}, u32[]{:S(2)}, u32[]{:S(2)}) collective-permute-start(f32[32,3,256]{2,1,0:T(4,128)S(1)} %get-tuple-element.112), channel_id=1, source_target_pairs={{0,1},{1,2},{2,3},{3,4},{4,5},{5,6},{6,7},{7,8},{8,9},{9,10},{10,1... | collective-permute-start | bytes 294920 | tf_op jit(solution)/shard_map/ppermute | solution.py:29
  103.2 5.9 %collective-permute-start.10 = (f32[32,3,256]{2,1,0:T(4,128)S(1)}, f32[32,3,256]{2,1,0:T(4,128)S(1)}, u32[]{:S(2)}, u32[]{:S(2)}) collective-permute-start(f32[32,3,256]{2,1,0:T(4,128)S(1)} %get-tuple-element.111), channel_id=1, source_target_pairs={{0,15},{1,0},{2,1},{3,2},{4,3},{5,4},{6,5},{7,6},{8,7},{9,8},{10,9... | collective-permute-start | bytes 294920 | tf_op jit(solution)/shard_map/ppermute | solution.py:29
  120.0 5.6 %collective-permute-start.11 = (f32[32,3,256]{2,1,0:T(4,128)S(1)}, f32[32,3,256]{2,1,0:T(4,128)S(1)}, u32[]{:S(2)}, u32[]{:S(2)}) collective-permute-start(f32[32,3,256]{2,1,0:T(4,128)S(1)} %get-tuple-element.110), channel_id=1, source_target_pairs={{0,1},{1,2},{2,3},{3,4},{4,5},{5,6},{6,7},{7,8},{8,9},{9,10},{10,1... | collective-permute-start | bytes 294920 | tf_op jit(solution)/shard_map/ppermute | solution.py:29
  120.1 5.9 %collective-permute-start.12 = (f32[32,3,256]{2,1,0:T(4,128)S(1)}, f32[32,3,256]{2,1,0:T(4,128)S(1)}, u32[]{:S(2)}, u32[]{:S(2)}) collective-permute-start(f32[32,3,256]{2,1,0:T(4,128)S(1)} %get-tuple-element.109), channel_id=1, source_target_pairs={{0,15},{1,0},{2,1},{3,2},{4,3},{5,4},{6,5},{7,6},{8,7},{9,8},{10,9... | collective-permute-start | bytes 294920 | tf_op jit(solution)/shard_map/ppermute | solution.py:29
  126.5 5.3 %collective-permute-start.13 = (f32[32,6,256]{2,1,0:T(8,128)S(1)}, f32[32,6,256]{2,1,0:T(8,128)S(1)}, u32[]{:S(2)}, u32[]{:S(2)}) collective-permute-start(f32[32,6,256]{2,1,0:T(8,128)S(1)} %fusion.76), channel_id=1, source_target_pairs={{128,0},{129,1},{130,2},{131,3},{132,4},{133,5},{134,6},{135,7},{1... | collective-permute-start | bytes 589832 | tf_op jit(solution)/shard_map/ppermute | solution.py:35
  142.5 5.6 %collective-permute-start.14 = (f32[32,3,256]{2,1,0:T(4,128)S(1)}, f32[32,3,256]{2,1,0:T(4,128)S(1)}, u32[]{:S(2)}, u32[]{:S(2)}) collective-permute-start(f32[32,3,256]{2,1,0:T(4,128)S(1)} %get-tuple-element.108), channel_id=1, source_target_pairs={{0,1},{1,2},{2,3},{3,4},{4,5},{5,6},{6,7},{7,8},{8,9},{9,10},{10,1... | collective-permute-start | bytes 294920 | tf_op jit(solution)/shard_map/ppermute | solution.py:29
  142.6 5.9 %collective-permute-start.15 = (f32[32,3,256]{2,1,0:T(4,128)S(1)}, f32[32,3,256]{2,1,0:T(4,128)S(1)}, u32[]{:S(2)}, u32[]{:S(2)}) collective-permute-start(f32[32,3,256]{2,1,0:T(4,128)S(1)} %get-tuple-element.107), channel_id=1, source_target_pairs={{0,15},{1,0},{2,1},{3,2},{4,3},{5,4},{6,5},{7,6},{8,7},{9,8},{10,9... | collective-permute-start | bytes 294920 | tf_op jit(solution)/shard_map/ppermute | solution.py:29
  159.4 5.6 %collective-permute-start.16 = (f32[32,3,256]{2,1,0:T(4,128)S(1)}, f32[32,3,256]{2,1,0:T(4,128)S(1)}, u32[]{:S(2)}, u32[]{:S(2)}) collective-permute-start(f32[32,3,256]{2,1,0:T(4,128)S(1)} %get-tuple-element.106), channel_id=1, source_target_pairs={{0,1},{1,2},{2,3},{3,4},{4,5},{5,6},{6,7},{7,8},{8,9},{9,10},{10,1... | collective-permute-start | bytes 294920 | tf_op jit(solution)/shard_map/ppermute | solution.py:29
  159.5 5.9 %collective-permute-start.17 = (f32[32,3,256]{2,1,0:T(4,128)S(1)}, f32[32,3,256]{2,1,0:T(4,128)S(1)}, u32[]{:S(2)}, u32[]{:S(2)}) collective-permute-start(f32[32,3,256]{2,1,0:T(4,128)S(1)} %get-tuple-element.105), channel_id=1, source_target_pairs={{0,15},{1,0},{2,1},{3,2},{4,3},{5,4},{6,5},{7,6},{8,7},{9,8},{10,9... | collective-permute-start | bytes 294920 | tf_op jit(solution)/shard_map/ppermute | solution.py:29
  165.9 8.9 %collective-permute-start.18 = (f32[32,6,128]{2,1,0:T(8,128)S(1)}, f32[32,6,128]{2,1,0:T(8,128)S(1)}, u32[]{:S(2)}, u32[]{:S(2)}) collective-permute-start(f32[32,6,128]{2,1,0:T(8,128)S(1)} %slice.329), channel_id=1, source_target_pairs={{0,128},{1,129},{2,130},{3,131},{4,132},{5,133},{6,134},{7,135},{8... | collective-permute-start | bytes 294920 | tf_op jit(solution)/shard_map/ppermute | solution.py:35
  174.9 162.1 %copy-start.1 = (f32[32,6,128]{2,0,1:T(8,128)}, f32[32,6,128]{2,0,1:T(8,128)S(1)}, u32[]{:S(2)}) copy-start(f32[32,6,128]{2,0,1:T(8,128)S(1)} %copy.37) | copy-start | bytes 294916
where the time goes:
time: 344 us; the launch traced here: 337 us
  blocking collectives  161 us (47%)
  matrix products  98.4 us (29%)
  waiting for transfers between devices  37.8 us (11%)
  starting transfers between devices  30.4 us (9%)
  local copies, waits for them, and re-layouts  5.62 us (2%)
    psum x1, blocking collectives, per_device(): gram = lax.psum(partial_gram, ('sec', 'elem')) * scaling  129 us
    dot_general x4, matrix products, tangent_pass(): jnp.einsum('cekI,ekJI->ceJ', gathered, blocks, precision=PRECISE)  50.8 us
    dot_general x4, matrix products, adjoint_pass(): products = jnp.einsum('ceJ,ekJI->cekI', vector, blocks, precision=PRECISE)  36.3 us
    all_gather x1, blocking collectives, per_device(): shard_piece = lax.all_gather(hess_local, 'col', axis=0, tiled=True)  32.1 us
    ppermute x3, waiting for transfers between devices, from_behind_2(): lax.ppermute(value, axis, [(source, source + steps) for source in range(l...  19.1 us
    ppermute x4, starting transfers between devices, with_halo(): after = lax.ppermute(leading, axis, down)  14.2 us
    ppermute x8, starting transfers between devices, from_behind(): return lax.ppermute(value, axis, pairs)  11.9 us
    ppermute x8, waiting for transfers between devices, from_behind(): return lax.ppermute(value, axis, pairs)  10.4 us
  transfers between devices with their start and end apart: 19, of which 11 were waited for; matrix products, arithmetic and copies ran while one was open for 1% of the time, Pallas kernels for 0%

commit v1 on v0

v1 whole, which is shorter than its diff:
```python
import functools

import jax
import jax.numpy as jnp
from jax import lax
from jax.experimental import pallas as pl
from jax.experimental.pallas import tpu as pltpu
from jax.sharding import PartitionSpec as P

NBRS = 7
RADIUS = 3
STEPS = 2
PRECISE = lax.Precision.HIGHEST
BF16 = jnp.bfloat16
F32 = jnp.float32
NN = (((1,), (0,)), ((), ()))
NT = (((1,), (1,)), ((), ()))

IN_VMEM = pl.BlockSpec(memory_space=pltpu.VMEM)
IN_SMEM = pl.BlockSpec(memory_space=pltpu.SMEM)
IN_HBM = pl.BlockSpec(memory_space=pltpu.HBM)


def call(body, name, outs, in_specs, scratch=(), vmem=4 << 20, flops=10**8, moved=10**6):
    single = not isinstance(outs, tuple)
    return pl.pallas_call(
        body,
        name=name,
        out_shape=outs,
        in_specs=in_specs,
        out_specs=IN_VMEM if single else (IN_VMEM,) * len(outs),
        scratch_shapes=list(scratch),
        compiler_params=pltpu.CompilerParams(vmem_limit_bytes=vmem),
        cost_estimate=pl.CostEstimate(flops=flops, bytes_accessed=moved, transcendentals=0),
    )


def vmem(shape, dtype=F32):
    return pltpu.VMEM(shape, dtype)


def split(value):
    high = value.astype(BF16)
    low = (value - high.astype(F32)).astype(BF16)
    return high, low


def store_split(pair_ref, slot, value):
    rows = value.shape[0]
    high, low = split(value)
    pair_ref[slot, :rows] = high
    pair_ref[slot, rows:] = low


def product(pair_ref, slot, high_ref, low_ref, block, dims):
    rows = pair_ref.shape[1] // 2
    both = lax.dot_general(pair_ref[slot], high_ref[block], dims, preferred_element_type=F32)
    rest = lax.dot_general(
        pair_ref[slot, :rows], low_ref[block], dims, preferred_element_type=F32
    )
    return both[:rows] + both[rows:] + rest


def odd_device():
    return lax.rem(lax.axis_index("elem"), 2) == 1


def prepare_body(elem_total, nbr_ref, jac_ref, high_ref, low_ref, buffer, sems):
    elems = buffer.shape[0]
    copies = [
        pltpu.make_async_copy(jac_ref.at[0, e], buffer.at[e], sems.at[e]) for e in range(elems)
    ]
    for copy in copies:
        copy.start()
    first = lax.axis_index("elem") * elems
    odd = odd_device()
    for e in range(elems):
        copies[e].wait()

        def one(k, carry, e=e):
            offset = lax.rem(nbr_ref[e, k] - (first + e) + RADIUS + elem_total, elem_total)
            slot = e * NBRS + offset
            slot = jnp.where(odd, elems * NBRS - 1 - slot, slot)
            high, low = split(buffer[e, k])
            high_ref[slot] = high
            low_ref[slot] = low
            return carry

        lax.fori_loop(0, NBRS, one, 0)


def mirror_body(field_ref, out_ref):
    elems = field_ref.shape[0]
    odd = odd_device()
    for u in range(elems):
        out_ref[u] = field_ref[jnp.where(odd, elems - 1 - u, u)]


def tangent_local_body(field_ref, high_ref, low_ref, total_ref, pair_ref):
    elems = field_ref.shape[0]
    for e in range(elems):
        store_split(pair_ref, e, field_ref[e])
    for e in range(elems):
        total = field_ref[e]
        for m in range(max(0, e - RADIUS), min(elems, e + RADIUS + 1)):
            total += product(pair_ref, m, high_ref, low_ref, e * NBRS + m - e + RADIUS, NT)
        total_ref[e] = total


def tangent_edge_body(total_ref, outer_ref, inner_ref, high_ref, low_ref, field_ref, pair_ref):
    elems = total_ref.shape[0]
    for i in range(RADIUS):
        store_split(pair_ref, i, outer_ref[i])
        store_split(pair_ref, RADIUS + i, inner_ref[i])
    for e in range(elems):
        total = total_ref[e]
        for m in range(e - RADIUS, e + RADIUS + 1):
            if m < 0:
                slot = -1 - m
            elif m >= elems:
                slot = RADIUS + (elems + RADIUS - 1 - m)
            else:
                continue
            total += product(pair_ref, slot, high_ref, low_ref, e * NBRS + m - e + RADIUS, NT)
        field_ref[e] = total


def edge_products(pair_ref, high_ref, low_ref, outer_ref, inner_ref, elems):
    for i in range(RADIUS):
        for ref, m in ((outer_ref, -1 - i), (inner_ref, elems + RADIUS - 1 - i)):
            total = None
            for e in range(max(0, m - RADIUS), min(elems, m + RADIUS + 1)):
                term = product(pair_ref, e, high_ref, low_ref, e * NBRS + m - e + RADIUS, NN)
                total = term if total is None else total + term
            ref[i] = total


def observe_body(
    state0_ref, state1_ref, stations_ref, weights_ref, high_ref, low_ref,
    seen_ref, readings_ref, outer_ref, inner_ref, pair_ref, state_ref,
):
    elems, cols, dofs = state0_ref.shape
    count = weights_ref.shape[0]
    section = lax.axis_index("sec")

    @pl.when(section == 0)
    def _():
        state_ref[...] = state0_ref[...]

    @pl.when(section != 0)
    def _():
        state_ref[...] = state1_ref[...]

    flat = state_ref[...].reshape(elems * cols, dofs)
    weights = weights_ref[...]
    raw = lax.dot_general(flat, weights, NT, precision=PRECISE, preferred_element_type=F32)
    local = stations_ref[...] - lax.axis_index("elem") * elems
    odd = odd_device()
    readings = jnp.zeros((cols, count), F32)
    for u in range(elems):
        here = local == jnp.where(odd, elems - 1 - u, u)
        part = jnp.where(here, raw[u * cols : (u + 1) * cols], 0.0)
        readings += part
        seen = lax.dot_general(part, weights, NN, precision=PRECISE, preferred_element_type=F32)
        seen_ref[u] = seen
        store_split(pair_ref, u, seen)
    readings_ref[...] = readings
    edge_products(pair_ref, high_ref, low_ref, outer_ref, inner_ref, elems)


def adjoint_local_body(field_ref, high_ref, low_ref, total_ref, pair_ref):
    elems = field_ref.shape[0]
    for e in range(elems):
        store_split(pair_ref, e, field_ref[e])
    for m in range(elems):
        total = field_ref[m]
        for e in range(max(0, m - RADIUS), min(elems, m + RADIUS + 1)):
            total += product(pair_ref, e, high_ref, low_ref, e * NBRS + m - e + RADIUS, NN)
        total_ref[m] = total


def adjoint_edge_body(
    total_ref, outer_in_ref, inner_in_ref, high_ref, low_ref,
    field_ref, outer_ref, inner_ref, pair_ref,
):
    elems = total_ref.shape[0]
    for i in range(RADIUS):
        for u, ref in ((i, outer_in_ref), (RADIUS + i, inner_in_ref)):
            value = total_ref[u] + ref[i]
            field_ref[u] = value
            store_split(pair_ref, u, value)
    edge_products(pair_ref, high_ref, low_ref, outer_ref, inner_ref, elems)


def adjoint_join_body(total_ref, outer_in_ref, inner_in_ref, field_ref):
    for i in range(RADIUS):
        field_ref[i] = total_ref[i] + outer_in_ref[i]
        field_ref[RADIUS + i] = total_ref[RADIUS + i] + inner_in_ref[i]


def add_edge_body(
    seen_ref, back_ref, high_ref, low_ref, field_ref, outer_ref, inner_ref, pair_ref
):
    elems = seen_ref.shape[0]
    for u in range(elems):
        value = seen_ref[u] + back_ref[u]
        field_ref[u] = value
        store_split(pair_ref, u, value)
    edge_products(pair_ref, high_ref, low_ref, outer_ref, inner_ref, elems)


def finish_body(total_ref, outer_in_ref, inner_in_ref, lower_ref, upper_ref):
    elems, cols, dofs = total_ref.shape
    half = dofs // 2
    odd = odd_device()
    for u in range(elems):
        ref = outer_in_ref if u < RADIUS else inner_in_ref
        value = total_ref[u] + ref[u % RADIUS]
        place = jnp.where(odd, elems - 1 - u, u)
        lower_ref[place] = value[:, :half]
        upper_ref[place] = value[:, half:]


def gram_body(stack_ref, out_ref):
    own = lax.axis_index("col")
    cols = stack_ref.shape[1]
    mine = stack_ref[0]
    blocks = [stack_ref[jnp.bitwise_xor(own, j)] for j in range(stack_ref.shape[0])]
    every = jnp.concatenate(blocks, axis=0)
    out_ref[...] = lax.dot_general(
        mine, every, NT, precision=PRECISE, preferred_element_type=F32
    )


def swap(value, axis, distance):
    count = lax.axis_size(axis)
    return lax.ppermute(value, axis, [(i, i ^ distance) for i in range(count)])


def exchange(outer, inner):
    count = lax.axis_size("elem")
    on_chip = [(i, i ^ 1) for i in range(count)]
    off_chip = [(i, (i + (1 if i % 2 else -1)) % count) for i in range(count)]
    inner_in = lax.ppermute(inner, "elem", on_chip)
    outer_in = lax.ppermute(outer, "elem", off_chip)
    return outer_in, inner_in


def per_device(probes, jacobian, neighbors, stations, obs_weights):
    cols, elems, dofs = probes.shape
    elem_total = elems * lax.axis_size("elem")
    blocks = elems * NBRS
    field = vmem((elems, cols, dofs))
    edge = vmem((RADIUS, cols, dofs))
    half = vmem((elems, cols, dofs // 2))
    pair = pltpu.VMEM((elems, 2 * cols, dofs), BF16)
    count = obs_weights.shape[0]

    prepare = call(
        functools.partial(prepare_body, elem_total), "prepare",
        (vmem((blocks, dofs, dofs), BF16),) * 2, [IN_SMEM, IN_HBM],
        (pltpu.VMEM((elems, NBRS, dofs, dofs), F32), pltpu.SemaphoreType.DMA((elems,))),
        vmem=16 << 20, moved=2 * 10**7,
    )
    mirror = call(mirror_body, "mirror", field, [IN_VMEM])
    tangent_local = call(
        tangent_local_body, "tangent_local", field, [IN_VMEM] * 3, (pair,), flops=2 * 10**9
    )
    tangent_edge = call(
        tangent_edge_body, "tangent_edge", field, [IN_VMEM] * 5, (pair,), flops=10**9
    )
    observe = call(
        observe_body, "observe", (field, vmem((cols, count)), edge, edge), [IN_VMEM] * 6,
        (pair, pltpu.VMEM((elems, cols, dofs), F32)), flops=10**9,
    )
    adjoint_local = call(
        adjoint_local_body, "adjoint_local", field, [IN_VMEM] * 3, (pair,), flops=2 * 10**9
    )
    adjoint_edge = call(
        adjoint_edge_body, "adjoint_edge", (field, edge, edge), [IN_VMEM] * 5, (pair,),
        flops=10**9,
    )
    adjoint_join = call(adjoint_join_body, "adjoint_join", field, [IN_VMEM] * 3)
    add_edge = call(
        add_edge_body, "add_edge", (field, edge, edge), [IN_VMEM] * 4, (pair,), flops=10**9
    )
    finish = call(finish_body, "finish", (half, half), [IN_VMEM] * 3)
    col_count = lax.axis_size("col")
    gram_part = call(gram_body, "gram_part", vmem((cols, cols * col_count)), [IN_VMEM])

    def tangent(value, high, low):
        for _ in range(STEPS):
            outer_in, inner_in = exchange(value[:RADIUS], value[RADIUS:])
            total = tangent_local(value, high, low)
            value = tangent_edge(total, outer_in, inner_in, high, low)
        return value

    def adjoint(value, outer, inner, high, low):
        for step in range(STEPS):
            outer_in, inner_in = exchange(outer, inner)
            total = adjoint_local(value, high, low)
            if step + 1 < STEPS:
                value, outer, inner = adjoint_edge(total, outer_in, inner_in, high, low)
        return total, outer_in, inner_in

    section = lax.axis_index("sec")
    high, low = prepare(neighbors, jacobian)
    start = mirror(jnp.transpose(probes, (1, 0, 2)))
    state0 = tangent(start, high, low)
    incoming = lax.ppermute(state0, "sec", [(0, 1)])
    state1 = tangent(incoming, high, low)
    seen, readings, outer, inner = observe(
        state0, state1, stations.reshape(1, count), obs_weights, high, low
    )
    joined = adjoint_join(*adjoint(seen, outer, inner, high, low))
    back = lax.ppermute(joined, "sec", [(1, 0)])
    value, outer, inner = add_edge(seen, back, high, low)
    lower, upper = finish(*adjoint(value, outer, inner, high, low))
    upper = lax.ppermute(upper, "sec", [(0, 1)])
    hess = jnp.transpose(jnp.where(section == 0, lower, upper), (1, 0, 2))

    stack = readings[None]
    distance = 1
    while distance < col_count:
        stack = jnp.concatenate([stack, swap(stack, "col", distance)], axis=0)
        distance *= 2
    gram = gram_part(stack)
    distance = 1
    while distance < lax.axis_size("elem"):
        gram = gram + swap(gram, "elem", distance)
        distance *= 2
    gram = gram + swap(gram, "sec", 1)
    return hess, gram * (1.0 / (elem_total * dofs))


def solution(mesh):
    in_specs = (
        P("col", "elem", None),
        P("sec", "elem", None, None, None),
        P("elem", None),
        P("elem"),
        P("elem", None),
    )
    out_specs = (P("col", "elem", "sec"), P("col", None))
    return jax.shard_map(
        per_device, mesh=mesh, in_specs=in_specs, out_specs=out_specs, check_vma=False
    )
```

time: 344 us -> 113 us (0.33)
  the two profiles are of different devices: /device:TPU:6 before, /device:TPU:16 now
where the time goes in v1:
time: 113 us; the launch traced here: 111 us
  waiting for transfers between devices  43.8 us (39%)
  starting transfers between devices  28.5 us (25%)
  Pallas kernels  25.8 us (23%)
  local copies, waits for them, and re-layouts  11 us (10%)
  other arithmetic  1.32 us (1%)
    ppermute x8, waiting for transfers between devices, swap(): return lax.ppermute(value, axis, [(i, i ^ distance) for i in range(count)])  19.3 us
    ppermute x8, waiting for transfers between devices, exchange(): outer_in = lax.ppermute(outer, 'elem', off_chip)  19 us
    unnamed x18, local copies, waits for them, and re-layouts  10.9 us
    ppermute x8, starting transfers between devices, exchange(): outer_in = lax.ppermute(outer, 'elem', off_chip)  10.5 us
    ppermute x8, starting transfers between devices, swap(): return lax.ppermute(value, axis, [(i, i ^ distance) for i in range(count)])  9.67 us
    pallas_call x4, Pallas kernels, tangent(): total = tangent_local(value, high, low)  9.63 us
    pallas_call x4, Pallas kernels, adjoint(): total = adjoint_local(value, high, low)  5.39 us
    ppermute x1, starting transfers between devices, per_device(): incoming = lax.ppermute(state0, 'sec', [(0, 1)])  4.95 us
  transfers between devices with their start and end apart: 27, of which 15 were waited for; matrix products, arithmetic and copies ran while one was open for 1% of the time, Pallas kernels for 18%

profile of v1, /device:TPU:16, one launch (start us, length us, event | category | flops | bytes accessed | tf_op | source)
XLA Modules:
  0.0 111.3 jit_solution(4659356493557597696)
XLA Ops:
  1.6 5.4 %collective-permute-start = (f32[3,32,256]{2,1,0:T(8,128)S(1)}, f32[3,32,256]{2,1,0:T(8,128)S(1)}, u32[]{:S(2)}, u32[]{:S(2)}) collective-permute-start(f32[3,32,256]{2,1,0:T(8,128)S(1)} %get-tuple-element.43), channel_id=1, source_target_pairs={{0,15},{1,2},{2,1},{3,4},{4,3},{5,6},{6,5},{7,8},{8,7},{9,10},{10,... | collective-permute-start | bytes 294920 | tf_op jit(solution)/shard_map/ppermute | solution.py:245
  7.0 4.1 %copy-done.4 = f32[1,6,7,256,256]{4,3,2,1,0:T(8,128)S(1)} copy-done((f32[1,6,7,256,256]{4,3,2,1,0:T(8,128)S(1)}, f32[1,6,7,256,256]{4,3,2,1,0:T(8,128)}, u32[]{:S(2)}) %copy-start.4) | copy-done | bytes 11010072
  11.8 3.4 %prepare.1 = (bf16[42,256,256]{2,1,0:T(8,128)(2,1)S(1)}, bf16[42,256,256]{2,1,0:T(8,128)(2,1)S(1)}) custom-call(s32[6,7]{1,0:T(8,128)S(1)} %copy-done.7, f32[1,6,7,256,256]{4,3,2,1,0:T(8,128)S(1)} %copy-done.4), custom_call_target="tpu_custom_call" | custom-call | flops 100000000 | bytes 20000000 | tf_op jit(solution)/shard_map/prepare/pallas_call | solution.py:307
  15.2 2.4 %tangent_local.4.total_ref = f32[6,32,256]{2,1,0:T(8,128)S(1)} custom-call(f32[6,32,256]{2,1,0:T(8,128)S(1)} %mirror.1.field_ref, bf16[42,256,256]{2,1,0:T(8,128)(2,1)S(1)} %get-tuple-element.19.high_ref, bf16[42,256,256]{2,1,0:T(8,128)(2,1)S(1)} %get-tuple-element.20.low_ref), custom_call_target="tpu_custom_call" | custom-call | flops 2000000000 | bytes 1000000 | tf_op jit(solution)/shard_map/tangent_local/pallas_call | solution.py:294
  19.9 2.4 %tangent_local.5.total_ref = f32[6,32,256]{2,1,0:T(8,128)S(1)} custom-call(f32[6,32,256]{2,1,0:T(8,128)S(1)} %tangent_edge.4.field_ref, bf16[42,256,256]{2,1,0:T(8,128)(2,1)S(1)} %get-tuple-element.19.high_ref, bf16[42,256,256]{2,1,0:T(8,128)(2,1)S(1)} %get-tuple-element.20.low_ref), custom_call_target="tpu_custom_call" | custom-call | flops 2000000000 | bytes 1000000 | tf_op jit(solution)/shard_map/tangent_local/pallas_call | solution.py:294
  22.3 1.7 %collective-permute-done.2.outer_ref = f32[3,32,256]{2,1,0:T(8,128)S(1)} collective-permute-done((f32[3,32,256]{2,1,0:T(8,128)S(1)}, f32[3,32,256]{2,1,0:T(8,128)S(1)}, u32[]{:S(2)}, u32[]{:S(2)}) %collective-permute-start.2) | collective-permute-done | bytes 98336 | tf_op jit(solution)/shard_map/ppermute | solution.py:245
  25.1 4.9 %collective-permute-start.4 = (f32[6,32,256]{2,1,0:T(8,128)S(1)}, f32[6,32,256]{2,1,0:T(8,128)S(1)}, u32[]{:S(2)}, u32[]{:S(2)}) collective-permute-start(f32[6,32,256]{2,1,0:T(8,128)S(1)} %tangent_edge.5.state0_ref), channel_id=1, source_target_pairs={{0,128},{1,129},{2,130},{3,131},{4,132},{5,133},{6,134},{7,135},{8... | collective-permute-start | bytes 589832 | tf_op jit(solution)/shard_map/ppermute | solution.py:310
  30.0 3.9 %collective-permute-done.4.field_ref = f32[6,32,256]{2,1,0:T(8,128)S(1)} collective-permute-done((f32[6,32,256]{2,1,0:T(8,128)S(1)}, f32[6,32,256]{2,1,0:T(8,128)S(1)}, u32[]{:S(2)}, u32[]{:S(2)}) %collective-permute-start.4) | collective-permute-done | bytes 196640 | tf_op jit(solution)/shard_map/ppermute | solution.py:310
  33.9 1.7 %collective-permute-start.5 = (f32[3,32,256]{2,1,0:T(8,128)S(1)}, f32[3,32,256]{2,1,0:T(8,128)S(1)}, u32[]{:S(2)}, u32[]{:S(2)}) collective-permute-start(f32[3,32,256]{2,1,0:T(8,128)S(1)} %get-tuple-element.39), channel_id=1, source_target_pairs={{0,15},{1,2},{2,1},{3,4},{4,3},{5,6},{6,5},{7,8},{8,7},{9,10},{10,... | collective-permute-start | bytes 294920 | tf_op jit(solution)/shard_map/ppermute | solution.py:245
  35.7 2.4 %tangent_local.6.total_ref = f32[6,32,256]{2,1,0:T(8,128)S(1)} custom-call(f32[6,32,256]{2,1,0:T(8,128)S(1)} %collective-permute-done.4.field_ref, bf16[42,256,256]{2,1,0:T(8,128)(2,1)S(1)} %get-tuple-element.19.high_ref, bf16[42,256,256]{2,1,0:T(8,128)(2,1)S(1)} %get-tuple-element.20.low_ref), custom_call_target="tpu_custom_call" | custom-call | flops 2000000000 | bytes 1000000 | tf_op jit(solution)/shard_map/tangent_local/pallas_call | solution.py:294
  42.1 2.4 %tangent_local.7.total_ref = f32[6,32,256]{2,1,0:T(8,128)S(1)} custom-call(f32[6,32,256]{2,1,0:T(8,128)S(1)} %tangent_edge.6.field_ref, bf16[42,256,256]{2,1,0:T(8,128)(2,1)S(1)} %get-tuple-element.19.high_ref, bf16[42,256,256]{2,1,0:T(8,128)(2,1)S(1)} %get-tuple-element.20.low_ref), custom_call_target="tpu_custom_call" | custom-call | flops 2000000000 | bytes 1000000 | tf_op jit(solution)/shard_map/tangent_local/pallas_call | solution.py:294
  48.8 3.2 %collective-permute-done.19 = f32[1,32,64]{2,1,0:T(8,128)S(1)} collective-permute-done((f32[1,32,64]{2,1,0:T(8,128)S(1)}, f32[1,32,64]{2,1,0:T(8,128)S(1)}, u32[]{:S(2)}, u32[]{:S(2)}) %collective-permute-start.19) | collective-permute-done | bytes 8224 | tf_op jit(solution)/shard_map/ppermute | solution.py:237
  56.3 3.6 %collective-permute-done.9.outer_in_ref = f32[3,32,256]{2,1,0:T(8,128)S(1)} collective-permute-done((f32[3,32,256]{2,1,0:T(8,128)S(1)}, f32[3,32,256]{2,1,0:T(8,128)S(1)}, u32[]{:S(2)}, u32[]{:S(2)}) %collective-permute-start.9) | collective-permute-done | bytes 98336 | tf_op jit(solution)/shard_map/ppermute | solution.py:245
  62.0 3.7 %collective-permute-done.11.outer_in_ref = f32[3,32,256]{2,1,0:T(8,128)S(1)} collective-permute-done((f32[3,32,256]{2,1,0:T(8,128)S(1)}, f32[3,32,256]{2,1,0:T(8,128)S(1)}, u32[]{:S(2)}, u32[]{:S(2)}) %collective-permute-start.11) | collective-permute-done | bytes 98336 | tf_op jit(solution)/shard_map/ppermute | solution.py:245
  68.6 3.9 %collective-permute-done.23 = f32[32,256]{1,0:T(8,128)S(1)} collective-permute-done((f32[32,256]{1,0:T(8,128)S(1)}, f32[32,256]{1,0:T(8,128)S(1)}, u32[]{:S(2)}, u32[]{:S(2)}) %collective-permute-start.23) | collective-permute-done | bytes 32800 | tf_op jit(solution)/shard_map/ppermute | solution.py:237
  72.5 4.8 %collective-permute-done.24 = f32[32,256]{1,0:T(8,128)S(1)} collective-permute-done((f32[32,256]{1,0:T(8,128)S(1)}, f32[32,256]{1,0:T(8,128)S(1)}, u32[]{:S(2)}, u32[]{:S(2)}) %collective-permute-start.24) | collective-permute-done | bytes 32800 | tf_op jit(solution)/shard_map/ppermute | solution.py:237
  77.3 3.0 %collective-permute-start.25 = (f32[32,256]{1,0:T(8,128)S(1)}, f32[32,256]{1,0:T(8,128)S(1)}, u32[]{:S(2)}, u32[]{:S(2)}) collective-permute-start(f32[32,256]{1,0:T(8,128)S(1)} %add.17), channel_id=1, source_target_pairs={{0,8},{1,9},{2,10},{3,11},{4,12},{5,13},{6,14},{7,15},{8,0},{9,1},... | collective-permute-start | bytes 98312 | tf_op jit(solution)/shard_map/ppermute | solution.py:237
  80.3 5.2 %collective-permute-done.25 = f32[32,256]{1,0:T(8,128)S(1)} collective-permute-done((f32[32,256]{1,0:T(8,128)S(1)}, f32[32,256]{1,0:T(8,128)S(1)}, u32[]{:S(2)}, u32[]{:S(2)}) %collective-permute-start.25) | collective-permute-done | bytes 32800 | tf_op jit(solution)/shard_map/ppermute | solution.py:237
  85.5 4.2 %collective-permute-start.26 = (f32[32,256]{1,0:T(8,128)S(1)}, f32[32,256]{1,0:T(8,128)S(1)}, u32[]{:S(2)}, u32[]{:S(2)}) collective-permute-start(f32[32,256]{1,0:T(8,128)S(1)} %add.18), channel_id=1, source_target_pairs={{0,128},{128,0},{1,129},{129,1},{2,130},{130,2},{3,131},{131,3},{4... | collective-permute-start | bytes 98312 | tf_op jit(solution)/shard_map/ppermute | solution.py:237
  89.7 2.6 %copy-done.1 = bf16[42,256,256]{2,1,0:T(8,128)(2,1)S(1)} copy-done((bf16[42,256,256]{2,1,0:T(8,128)(2,1)S(1)}, bf16[42,256,256]{2,1,0:T(8,128)(2,1)}, u32[]{:S(2)}) %copy-start.1) | copy-done | bytes 5505048
  92.2 2.6 %copy-done.3 = bf16[42,256,256]{2,1,0:T(8,128)(2,1)S(1)} copy-done((bf16[42,256,256]{2,1,0:T(8,128)(2,1)S(1)}, bf16[42,256,256]{2,1,0:T(8,128)(2,1)}, u32[]{:S(2)}) %copy-start.3) | copy-done | bytes 5505048
  96.9 3.8 %collective-permute-done.14.outer_in_ref = f32[3,32,256]{2,1,0:T(8,128)S(1)} collective-permute-done((f32[3,32,256]{2,1,0:T(8,128)S(1)}, f32[3,32,256]{2,1,0:T(8,128)S(1)}, u32[]{:S(2)}, u32[]{:S(2)}) %collective-permute-start.14) | collective-permute-done | bytes 98336 | tf_op jit(solution)/shard_map/ppermute | solution.py:245
  102.7 3.8 %collective-permute-done.16.outer_in_ref = f32[3,32,256]{2,1,0:T(8,128)S(1)} collective-permute-done((f32[3,32,256]{2,1,0:T(8,128)S(1)}, f32[3,32,256]{2,1,0:T(8,128)S(1)}, u32[]{:S(2)}, u32[]{:S(2)}) %collective-permute-start.16) | collective-permute-done | bytes 98336 | tf_op jit(solution)/shard_map/ppermute | solution.py:245
  106.6 1.9 %collective-permute-start.18 = (f32[6,32,128]{2,1,0:T(8,128)S(1)}, f32[6,32,128]{2,1,0:T(8,128)S(1)}, u32[]{:S(2)}, u32[]{:S(2)}) collective-permute-start(f32[6,32,128]{2,1,0:T(8,128)S(1)} %get-tuple-element.34), channel_id=1, source_target_pairs={{0,128},{1,129},{2,130},{3,131},{4,132},{5,133},{6,134},{7,135},{8... | collective-permute-start | bytes 294920 | tf_op jit(solution)/shard_map/ppermute | solution.py:319
  (82 shorter events, 29.6 us)
Async XLA Ops:
  1.6 16.0 %collective-permute-start = (f32[3,32,256]{2,1,0:T(8,128)S(1)}, f32[3,32,256]{2,1,0:T(8,128)S(1)}, u32[]{:S(2)}, u32[]{:S(2)}) collective-permute-start(f32[3,32,256]{2,1,0:T(8,128)S(1)} %get-tuple-element.43), channel_id=1, source_target_pairs={{0,15},{1,2},{2,1},{3,4},{4,3},{5,6},{6,5},{7,8},{8,7},{9,10},{10,... | collective-permute-start | bytes 294920 | tf_op jit(solution)/shard_map/ppermute | solution.py:245
  7.0 10.7 %collective-permute-start.1 = (f32[3,32,256]{2,1,0:T(8,128)S(1)}, f32[3,32,256]{2,1,0:T(8,128)S(1)}, u32[]{:S(2)}, u32[]{:S(2)}) collective-permute-start(f32[3,32,256]{2,1,0:T(8,128)S(1)} %get-tuple-element.42), channel_id=1, source_target_pairs={{0,1},{1,0},{2,3},{3,2},{4,5},{5,4},{6,7},{7,6},{8,9},{9,8},{10,11... | collective-permute-start | bytes 294920 | tf_op jit(solution)/shard_map/ppermute | solution.py:244
  18.7 5.3 %collective-permute-start.2 = (f32[3,32,256]{2,1,0:T(8,128)S(1)}, f32[3,32,256]{2,1,0:T(8,128)S(1)}, u32[]{:S(2)}, u32[]{:S(2)}) collective-permute-start(f32[3,32,256]{2,1,0:T(8,128)S(1)} %get-tuple-element.41), channel_id=1, source_target_pairs={{0,15},{1,2},{2,1},{3,4},{4,3},{5,6},{6,5},{7,8},{8,7},{9,10},{10,... | collective-permute-start | bytes 294920 | tf_op jit(solution)/shard_map/ppermute | solution.py:245
  19.9 4.1 %collective-permute-start.3 = (f32[3,32,256]{2,1,0:T(8,128)S(1)}, f32[3,32,256]{2,1,0:T(8,128)S(1)}, u32[]{:S(2)}, u32[]{:S(2)}) collective-permute-start(f32[3,32,256]{2,1,0:T(8,128)S(1)} %get-tuple-element.40), channel_id=1, source_target_pairs={{0,1},{1,0},{2,3},{3,2},{4,5},{5,4},{6,7},{7,6},{8,9},{9,8},{10,11... | collective-permute-start | bytes 294920 | tf_op jit(solution)/shard_map/ppermute | solution.py:244
  25.1 8.8 %collective-permute-start.4 = (f32[6,32,256]{2,1,0:T(8,128)S(1)}, f32[6,32,256]{2,1,0:T(8,128)S(1)}, u32[]{:S(2)}, u32[]{:S(2)}) collective-permute-start(f32[6,32,256]{2,1,0:T(8,128)S(1)} %tangent_edge.5.state0_ref), channel_id=1, source_target_pairs={{0,128},{1,129},{2,130},{3,131},{4,132},{5,133},{6,134},{7,135},{8... | collective-permute-start | bytes 589832 | tf_op jit(solution)/shard_map/ppermute | solution.py:310
  33.9 5.3 %collective-permute-start.5 = (f32[3,32,256]{2,1,0:T(8,128)S(1)}, f32[3,32,256]{2,1,0:T(8,128)S(1)}, u32[]{:S(2)}, u32[]{:S(2)}) collective-permute-start(f32[3,32,256]{2,1,0:T(8,128)S(1)} %get-tuple-element.39), channel_id=1, source_target_pairs={{0,15},{1,2},{2,1},{3,4},{4,3},{5,6},{6,5},{7,8},{8,7},{9,10},{10,... | collective-permute-start | bytes 294920 | tf_op jit(solution)/shard_map/ppermute | solution.py:245
  40.3 5.3 %collective-permute-start.7 = (f32[3,32,256]{2,1,0:T(8,128)S(1)}, f32[3,32,256]{2,1,0:T(8,128)S(1)}, u32[]{:S(2)}, u32[]{:S(2)}) collective-permute-start(f32[3,32,256]{2,1,0:T(8,128)S(1)} %get-tuple-element.37), channel_id=1, source_target_pairs={{0,15},{1,2},{2,1},{3,4},{4,3},{5,6},{6,5},{7,8},{8,7},{9,10},{10,... | collective-permute-start | bytes 294920 | tf_op jit(solution)/shard_map/ppermute | solution.py:245
  48.0 3.9 %collective-permute-start.19 = (f32[1,32,64]{2,1,0:T(8,128)S(1)}, f32[1,32,64]{2,1,0:T(8,128)S(1)}, u32[]{:S(2)}, u32[]{:S(2)}) collective-permute-start(f32[1,32,64]{2,1,0:T(8,128)S(1)} %bitcast.6), channel_id=1, source_target_pairs={{0,16},{16,0},{32,48},{48,32},{64,80},{80,64},{96,112},{112,96},{1... | collective-permute-start | bytes 24584 | tf_op jit(solution)/shard_map/ppermute | solution.py:237
  51.9 3.9 %collective-permute-start.20 = (f32[2,32,64]{2,1,0:T(8,128)S(1)}, f32[2,32,64]{2,1,0:T(8,128)S(1)}, u32[]{:S(2)}, u32[]{:S(2)}) collective-permute-start(f32[2,32,64]{2,1,0:T(8,128)S(1)} %pad_maximum_fusion.2), channel_id=1, source_target_pairs={{0,32},{16,48},{32,0},{48,16},{64,96},{80,112},{96,64},{112,80},{1... | collective-permute-start | bytes 49160 | tf_op jit(solution)/shard_map/ppermute | solution.py:237
  54.5 5.3 %collective-permute-start.9 = (f32[3,32,256]{2,1,0:T(8,128)S(1)}, f32[3,32,256]{2,1,0:T(8,128)S(1)}, u32[]{:S(2)}, u32[]{:S(2)}) collective-permute-start(f32[3,32,256]{2,1,0:T(8,128)S(1)} %get-tuple-element.22), channel_id=1, source_target_pairs={{0,15},{1,2},{2,1},{3,4},{4,3},{5,6},{6,5},{7,8},{8,7},{9,10},{10,... | collective-permute-start | bytes 294920 | tf_op jit(solution)/shard_map/ppermute | solution.py:245
  54.8 5.1 %collective-permute-start.10 = (f32[3,32,256]{2,1,0:T(8,128)S(1)}, f32[3,32,256]{2,1,0:T(8,128)S(1)}, u32[]{:S(2)}, u32[]{:S(2)}) collective-permute-start(f32[3,32,256]{2,1,0:T(8,128)S(1)} %get-tuple-element.23), channel_id=1, source_target_pairs={{0,1},{1,0},{2,3},{3,2},{4,5},{5,4},{6,7},{7,6},{8,9},{9,8},{10,11... | collective-permute-start | bytes 294920 | tf_op jit(solution)/shard_map/ppermute | solution.py:244
  55.8 11.2 %collective-permute-start.21 = (f32[4,32,64]{2,1,0:T(8,128)S(1)}, f32[4,32,64]{2,1,0:T(8,128)S(1)}, u32[]{:S(2)}, u32[]{:S(2)}) collective-permute-start(f32[4,32,64]{2,1,0:T(8,128)S(1)} %pad_maximum_fusion.1), channel_id=1, source_target_pairs={{0,64},{16,80},{32,96},{48,112},{64,0},{80,16},{96,32},{112,48},{1... | collective-permute-start | bytes 98312 | tf_op jit(solution)/shard_map/ppermute | solution.py:237
  60.4 5.3 %collective-permute-start.11 = (f32[3,32,256]{2,1,0:T(8,128)S(1)}, f32[3,32,256]{2,1,0:T(8,128)S(1)}, u32[]{:S(2)}, u32[]{:S(2)}) collective-permute-start(f32[3,32,256]{2,1,0:T(8,128)S(1)} %get-tuple-element.25), channel_id=1, source_target_pairs={{0,15},{1,2},{2,1},{3,4},{4,3},{5,6},{6,5},{7,8},{8,7},{9,10},{10,... | collective-permute-start | bytes 294920 | tf_op jit(solution)/shard_map/ppermute | solution.py:245
  60.7 5.1 %collective-permute-start.12 = (f32[3,32,256]{2,1,0:T(8,128)S(1)}, f32[3,32,256]{2,1,0:T(8,128)S(1)}, u32[]{:S(2)}, u32[]{:S(2)}) collective-permute-start(f32[3,32,256]{2,1,0:T(8,128)S(1)} %get-tuple-element.26), channel_id=1, source_target_pairs={{0,1},{1,0},{2,3},{3,2},{4,5},{5,4},{6,7},{7,6},{8,9},{9,8},{10,11... | collective-permute-start | bytes 294920 | tf_op jit(solution)/shard_map/ppermute | solution.py:244
  65.7 23.9 %collective-permute-start.13 = (f32[6,32,256]{2,1,0:T(8,128)S(1)}, f32[6,32,256]{2,1,0:T(8,128)S(1)}, u32[]{:S(2)}, u32[]{:S(2)}) collective-permute-start(f32[6,32,256]{2,1,0:T(8,128)S(1)} %adjoint_join.1), channel_id=1, source_target_pairs={{128,0},{129,1},{130,2},{131,3},{132,4},{133,5},{134,6},{135,7},{1... | collective-permute-start | bytes 589832 | tf_op jit(solution)/shard_map/ppermute | solution.py:316
  68.6 3.9 %collective-permute-start.23 = (f32[32,256]{1,0:T(8,128)S(1)}, f32[32,256]{1,0:T(8,128)S(1)}, u32[]{:S(2)}, u32[]{:S(2)}) collective-permute-start(f32[32,256]{1,0:T(8,128)S(1)} %add.15), channel_id=1, source_target_pairs={{0,2},{1,3},{2,0},{3,1},{4,6},{5,7},{6,4},{7,5},{8,10},{9,11},{10,... | collective-permute-start | bytes 98312 | tf_op jit(solution)/shard_map/ppermute | solution.py:237
  72.5 4.8 %collective-permute-start.24 = (f32[32,256]{1,0:T(8,128)S(1)}, f32[32,256]{1,0:T(8,128)S(1)}, u32[]{:S(2)}, u32[]{:S(2)}) collective-permute-start(f32[32,256]{1,0:T(8,128)S(1)} %add.16), channel_id=1, source_target_pairs={{0,4},{1,5},{2,6},{3,7},{4,0},{5,1},{6,2},{7,3},{8,12},{9,13},{10,... | collective-permute-start | bytes 98312 | tf_op jit(solution)/shard_map/ppermute | solution.py:237
  77.3 8.2 %collective-permute-start.25 = (f32[32,256]{1,0:T(8,128)S(1)}, f32[32,256]{1,0:T(8,128)S(1)}, u32[]{:S(2)}, u32[]{:S(2)}) collective-permute-start(f32[32,256]{1,0:T(8,128)S(1)} %add.17), channel_id=1, source_target_pairs={{0,8},{1,9},{2,10},{3,11},{4,12},{5,13},{6,14},{7,15},{8,0},{9,1},... | collective-permute-start | bytes 98312 | tf_op jit(solution)/shard_map/ppermute | solution.py:237
  85.5 23.0 %collective-permute-start.26 = (f32[32,256]{1,0:T(8,128)S(1)}, f32[32,256]{1,0:T(8,128)S(1)}, u32[]{:S(2)}, u32[]{:S(2)}) collective-permute-start(f32[32,256]{1,0:T(8,128)S(1)} %add.18), channel_id=1, source_target_pairs={{0,128},{128,0},{1,129},{129,1},{2,130},{130,2},{3,131},{131,3},{4... | collective-permute-start | bytes 98312 | tf_op jit(solution)/shard_map/ppermute | solution.py:237
  95.4 5.3 %collective-permute-start.14 = (f32[3,32,256]{2,1,0:T(8,128)S(1)}, f32[3,32,256]{2,1,0:T(8,128)S(1)}, u32[]{:S(2)}, u32[]{:S(2)}) collective-permute-start(f32[3,32,256]{2,1,0:T(8,128)S(1)} %get-tuple-element.28), channel_id=1, source_target_pairs={{0,15},{1,2},{2,1},{3,4},{4,3},{5,6},{6,5},{7,8},{8,7},{9,10},{10,... | collective-permute-start | bytes 294920 | tf_op jit(solution)/shard_map/ppermute | solution.py:245
  95.4 5.3 %collective-permute-start.15 = (f32[3,32,256]{2,1,0:T(8,128)S(1)}, f32[3,32,256]{2,1,0:T(8,128)S(1)}, u32[]{:S(2)}, u32[]{:S(2)}) collective-permute-start(f32[3,32,256]{2,1,0:T(8,128)S(1)} %get-tuple-element.29), channel_id=1, source_target_pairs={{0,1},{1,0},{2,3},{3,2},{4,5},{5,4},{6,7},{7,6},{8,9},{9,8},{10,11... | collective-permute-start | bytes 294920 | tf_op jit(solution)/shard_map/ppermute | solution.py:244
  101.3 5.3 %collective-permute-start.16 = (f32[3,32,256]{2,1,0:T(8,128)S(1)}, f32[3,32,256]{2,1,0:T(8,128)S(1)}, u32[]{:S(2)}, u32[]{:S(2)}) collective-permute-start(f32[3,32,256]{2,1,0:T(8,128)S(1)} %get-tuple-element.31), channel_id=1, source_target_pairs={{0,15},{1,2},{2,1},{3,4},{4,3},{5,6},{6,5},{7,8},{8,7},{9,10},{10,... | collective-permute-start | bytes 294920 | tf_op jit(solution)/shard_map/ppermute | solution.py:245
  101.3 5.3 %collective-permute-start.17 = (f32[3,32,256]{2,1,0:T(8,128)S(1)}, f32[3,32,256]{2,1,0:T(8,128)S(1)}, u32[]{:S(2)}, u32[]{:S(2)}) collective-permute-start(f32[3,32,256]{2,1,0:T(8,128)S(1)} %get-tuple-element.32), channel_id=1, source_target_pairs={{0,1},{1,0},{2,3},{3,2},{4,5},{5,4},{6,7},{7,6},{8,9},{9,8},{10,11... | collective-permute-start | bytes 294920 | tf_op jit(solution)/shard_map/ppermute | solution.py:244
  106.6 4.1 %collective-permute-start.18 = (f32[6,32,128]{2,1,0:T(8,128)S(1)}, f32[6,32,128]{2,1,0:T(8,128)S(1)}, u32[]{:S(2)}, u32[]{:S(2)}) collective-permute-start(f32[6,32,128]{2,1,0:T(8,128)S(1)} %get-tuple-element.34), channel_id=1, source_target_pairs={{0,128},{1,129},{2,130},{3,131},{4,132},{5,133},{6,134},{7,135},{8... | collective-permute-start | bytes 294920 | tf_op jit(solution)/shard_map/ppermute | solution.py:319
  (12 other events, 114.8 us)

commit v2 on v1

v2 whole, which is shorter than its diff:
```python
import functools

import jax
import jax.numpy as jnp
from jax import lax
from jax.experimental import pallas as pl
from jax.experimental.pallas import tpu as pltpu
from jax.sharding import PartitionSpec as P

NBRS = 7
RADIUS = 3
STEPS = 2
WORK = {
    "prepare": 30,
    "mirror": 30,
    "tangent_near": 30,
    "tangent_far": 30,
    "observe": 200,
    "adjoint_local": 100,
    "adjoint_outer": 400,
    "adjoint_inner": 100,
    "seen_outer": 100,
    "finish": 1000,
    "gram_part": 30,
}
PRECISE = lax.Precision.HIGHEST
BF16 = jnp.bfloat16
F32 = jnp.float32
NN = (((1,), (0,)), ((), ()))
NT = (((1,), (1,)), ((), ()))

IN_VMEM = pl.BlockSpec(memory_space=pltpu.VMEM)
IN_SMEM = pl.BlockSpec(memory_space=pltpu.SMEM)
IN_HBM = pl.BlockSpec(memory_space=pltpu.HBM)


def call(body, name, outs, in_specs, scratch=(), vmem=4 << 20, moved=10**5):
    single = not isinstance(outs, tuple)
    return pl.pallas_call(
        body,
        name=name,
        out_shape=outs,
        in_specs=in_specs,
        out_specs=IN_VMEM if single else (IN_VMEM,) * len(outs),
        scratch_shapes=list(scratch),
        compiler_params=pltpu.CompilerParams(vmem_limit_bytes=vmem),
        cost_estimate=pl.CostEstimate(flops=WORK[name] * 10**7, bytes_accessed=moved, transcendentals=0),
    )


def vmem(shape, dtype=F32):
    return pltpu.VMEM(shape, dtype)


def split(value):
    high = value.astype(BF16)
    low = (value - high.astype(F32)).astype(BF16)
    return high, low


def store_split(pair_ref, slot, value):
    rows = value.shape[0]
    high, low = split(value)
    pair_ref[slot, :rows] = high
    pair_ref[slot, rows:] = low


def product(pair_ref, slot, high_ref, low_ref, block, dims):
    rows = pair_ref.shape[1] // 2
    both = lax.dot_general(pair_ref[slot], high_ref[block], dims, preferred_element_type=F32)
    rest = lax.dot_general(
        pair_ref[slot, :rows], low_ref[block], dims, preferred_element_type=F32
    )
    return both[:rows] + both[rows:] + rest


def odd_device():
    return lax.rem(lax.axis_index("elem"), 2) == 1


def prepare_body(elem_total, nbr_ref, jac_ref, high_ref, low_ref, buffer, sems):
    elems = buffer.shape[0]
    copies = [
        [
            pltpu.make_async_copy(jac_ref.at[0, e, k], buffer.at[e, k], sems.at[e, k])
            for k in range(NBRS)
        ]
        for e in range(elems)
    ]
    for row in copies:
        for copy in row:
            copy.start()
    first = lax.axis_index("elem") * elems
    odd = odd_device()
    for e in range(elems):
        for k in range(NBRS):
            copies[e][k].wait()
            offset = lax.rem(nbr_ref[e, k] - (first + e) + RADIUS + elem_total, elem_total)
            slot = e * NBRS + offset
            slot = jnp.where(odd, elems * NBRS - 1 - slot, slot)
            high, low = split(buffer[e, k])
            high_ref[slot] = high
            low_ref[slot] = low


def mirror_body(field_ref, outer_ref, inner_ref):
    elems = field_ref.shape[0]
    odd = odd_device()
    for i in range(RADIUS):
        outer_ref[i] = field_ref[jnp.where(odd, elems - 1 - i, i)]
        inner_ref[i] = field_ref[jnp.where(odd, elems - 1 - RADIUS - i, RADIUS + i)]


def block(e, m):
    return e * NBRS + m - e + RADIUS


def tangent_near_body(
    outer_ref, inner_ref, halo_ref, high_ref, low_ref, outer_out, inner_out, pair_ref
):
    elems = 2 * RADIUS
    for i in range(RADIUS):
        store_split(pair_ref, i, outer_ref[i])
        store_split(pair_ref, RADIUS + i, inner_ref[i])
        store_split(pair_ref, elems + RADIUS - 1 - i, halo_ref[i])
    for e in range(elems):
        total = outer_ref[e] if e < RADIUS else inner_ref[e - RADIUS]
        for m in range(max(0, e - RADIUS), e + RADIUS + 1):
            total += product(pair_ref, m, high_ref, low_ref, block(e, m), NT)
        if e < RADIUS:
            outer_out[e] = total
        else:
            inner_out[e - RADIUS] = total


def tangent_far_body(outer_ref, halo_ref, high_ref, low_ref, outer_out, pair_ref):
    for i in range(RADIUS):
        store_split(pair_ref, i, halo_ref[i])
    for e in range(RADIUS):
        total = outer_ref[e]
        for i in range(RADIUS - e):
            total += product(pair_ref, i, high_ref, low_ref, block(e, -1 - i), NT)
        outer_out[e] = total


def outer_products(pair_ref, high_ref, low_ref, out_ref):
    for i in range(RADIUS):
        total = None
        for e in range(RADIUS - i):
            term = product(pair_ref, e, high_ref, low_ref, block(e, -1 - i), NN)
            total = term if total is None else total + term
        out_ref[i] = total


def inner_products(pair_ref, high_ref, low_ref, out_ref, base):
    elems = 2 * RADIUS
    for i in range(RADIUS):
        m = elems + RADIUS - 1 - i
        total = None
        for e in range(m - RADIUS, elems):
            term = product(
                pair_ref, e - RADIUS + base, high_ref, low_ref, block(e, m), NN
            )
            total = term if total is None else total + term
        out_ref[i] = total


def observe_body(
    outer0_ref, inner0_ref, outer1_ref, inner1_ref, stations_ref, weights_ref, high_ref, low_ref,
    outer_out, inner_out, readings_ref, inner_send, pair_ref, state_ref,
):
    elems, cols, dofs = state_ref.shape
    count = weights_ref.shape[0]
    section = lax.axis_index("sec")

    @pl.when(section == 0)
    def _():
        state_ref[:RADIUS] = outer0_ref[...]
        state_ref[RADIUS:] = inner0_ref[...]

    @pl.when(section != 0)
    def _():
        state_ref[:RADIUS] = outer1_ref[...]
        state_ref[RADIUS:] = inner1_ref[...]

    flat = state_ref[...].reshape(elems * cols, dofs)
    weights = weights_ref[...]
    raw = lax.dot_general(flat, weights, NT, precision=PRECISE, preferred_element_type=F32)
    local = stations_ref[...] - lax.axis_index("elem") * elems
    odd = odd_device()
    readings = jnp.zeros((cols, count), F32)
    for u in range(elems):
        here = local == jnp.where(odd, elems - 1 - u, u)
        part = jnp.where(here, raw[u * cols : (u + 1) * cols], 0.0)
        readings += part
        seen = lax.dot_general(part, weights, NN, precision=PRECISE, preferred_element_type=F32)
        if u < RADIUS:
            outer_out[u] = seen
        else:
            inner_out[u - RADIUS] = seen
            store_split(pair_ref, u - RADIUS, seen)
    readings_ref[...] = readings
    inner_products(pair_ref, high_ref, low_ref, inner_send, 0)


def seen_outer_body(value_ref, high_ref, low_ref, send_ref, pair_ref):
    for i in range(RADIUS):
        store_split(pair_ref, i, value_ref[i])
    outer_products(pair_ref, high_ref, low_ref, send_ref)


def adjoint_outer_body(total_ref, halo_ref, high_ref, low_ref, value_ref, send_ref, pair_ref):
    for i in range(RADIUS):
        value = total_ref[i] + halo_ref[i]
        value_ref[i] = value
        store_split(pair_ref, i, value)
    outer_products(pair_ref, high_ref, low_ref, send_ref)


def adjoint_inner_body(total_ref, halo_ref, high_ref, low_ref, value_ref, send_ref, pair_ref):
    for i in range(RADIUS):
        value = total_ref[i] + halo_ref[i]
        value_ref[i] = value
        store_split(pair_ref, i, value)
    inner_products(pair_ref, high_ref, low_ref, send_ref, 0)


def adjoint_local_body(outer_ref, inner_ref, high_ref, low_ref, outer_out, inner_out, pair_ref):
    elems = 2 * RADIUS
    for i in range(RADIUS):
        store_split(pair_ref, i, outer_ref[i])
        store_split(pair_ref, RADIUS + i, inner_ref[i])
    for m in range(elems):
        total = outer_ref[m] if m < RADIUS else inner_ref[m - RADIUS]
        for e in range(max(0, m - RADIUS), min(elems, m + RADIUS + 1)):
            total += product(pair_ref, e, high_ref, low_ref, block(e, m), NN)
        if m < RADIUS:
            outer_out[m] = total
        else:
            inner_out[m - RADIUS] = total


def finish_body(outer_ref, inner_ref, outer_up_ref, inner_up_ref, out_ref):
    elems, cols, half = out_ref.shape
    odd = odd_device()
    first = lax.axis_index("sec") == 0
    for u in range(elems):
        full, upper = (outer_ref, outer_up_ref) if u < RADIUS else (inner_ref, inner_up_ref)
        place = jnp.where(odd, elems - 1 - u, u)
        out_ref[place] = jnp.where(first, full[u % RADIUS, :, :half], upper[u % RADIUS])


def gram_body(stack_ref, out_ref):
    own = lax.axis_index("col")
    places = []
    for j in range(stack_ref.shape[0]):
        away = jnp.bitwise_xor(own, j)
        places.append(
            jnp.bitwise_xor(away, jnp.bitwise_and(lax.shift_right_logical(away, 1), 2))
        )
    total = None
    for core in range(stack_ref.shape[1]):
        every = jnp.concatenate([stack_ref[place, core] for place in places], axis=0)
        term = lax.dot_general(
            stack_ref[0, core], every, NT, precision=PRECISE, preferred_element_type=F32
        )
        total = term if total is None else total + term
    out_ref[...] = total


def swap(value, axis, mask):
    count = lax.axis_size(axis)
    return lax.ppermute(value, axis, [(i, i ^ mask) for i in range(count)])


def off_chip(value):
    count = lax.axis_size("elem")
    pairs = [(i, (i + (1 if i % 2 else -1)) % count) for i in range(count)]
    return lax.ppermute(value, "elem", pairs)


def on_chip(value):
    return swap(value, "elem", 1)


def after(value, *others):
    return lax.optimization_barrier((value, *others))[0]


def per_device(probes, jacobian, neighbors, stations, obs_weights):
    cols, elems, dofs = probes.shape
    elem_total = elems * lax.axis_size("elem")
    blocks = elems * NBRS
    edge = vmem((RADIUS, cols, dofs))
    count = obs_weights.shape[0]
    half = dofs // 2

    def pair(slots):
        return pltpu.VMEM((slots, 2 * cols, dofs), BF16)

    prepare = call(
        functools.partial(prepare_body, elem_total), "prepare",
        (vmem((blocks, dofs, dofs), BF16),) * 2, [IN_SMEM, IN_HBM],
        (pltpu.VMEM((elems, NBRS, dofs, dofs), F32), pltpu.SemaphoreType.DMA((elems, NBRS))),
        vmem=46 << 20, moved=2 * 10**7,
    )
    mirror = call(mirror_body, "mirror", (edge, edge), [IN_VMEM])
    tangent_near = call(
        tangent_near_body, "tangent_near", (edge, edge), [IN_VMEM] * 5, (pair(9),),
    )
    tangent_far = call(
        tangent_far_body, "tangent_far", edge, [IN_VMEM] * 4, (pair(RADIUS),)
    )
    observe = call(
        observe_body, "observe", (edge, edge, vmem((cols, count)), edge), [IN_VMEM] * 8,
        (pair(RADIUS), pltpu.VMEM((elems, cols, dofs), F32)),
    )
    adjoint_local = call(
        adjoint_local_body, "adjoint_local", (edge, edge), [IN_VMEM] * 4, (pair(elems),),
    )
    seen_products = call(
        seen_outer_body, "seen_outer", edge, [IN_VMEM] * 3, (pair(RADIUS),)
    )
    adjoint_outer = call(
        adjoint_outer_body, "adjoint_outer", (edge, edge), [IN_VMEM] * 4, (pair(RADIUS),),
    )
    adjoint_inner = call(
        adjoint_inner_body, "adjoint_inner", (edge, edge), [IN_VMEM] * 4, (pair(RADIUS),),
    )
    finish = call(
        finish_body, "finish", jax.ShapeDtypeStruct((elems, cols, half), F32), [IN_VMEM] * 4
    )
    col_count = lax.axis_size("col")
    gram_part = call(gram_body, "gram_part", vmem((cols, cols * col_count)), [IN_VMEM])

    def tangent(outer, inner, high, low):
        for _ in range(STEPS):
            inner_in = on_chip(inner)
            outer_in = off_chip(outer)
            outer, inner = tangent_near(outer, inner, inner_in, high, low)
            outer = tangent_far(outer, outer_in, high, low)
        return outer, inner

    def to_next(outer, inner):
        inner = lax.ppermute(inner, "sec", [(0, 1)])
        return lax.ppermute(outer, "sec", [(0, 1)]), inner

    high, low = prepare(neighbors, jacobian)
    state0 = tangent(*mirror(jnp.transpose(probes, (1, 0, 2))), high, low)
    state1 = tangent(*to_next(*state0), high, low)
    seen_outer, seen_inner, readings, inner_send = observe(
        *state0, *state1, stations.reshape(1, count), obs_weights, high, low
    )

    def gather(stack, mask, *others):
        return jnp.concatenate([stack, swap(after(stack, *others), "col", mask)], axis=0)

    inner_in = on_chip(inner_send)
    stack = jnp.stack([readings, on_chip(readings)])[None]
    outer_in = off_chip(seen_products(seen_outer, high, low))
    outer, inner = adjoint_local(seen_outer, seen_inner, high, low)
    inner, inner_send = adjoint_inner(inner, inner_in, high, low)
    inner_in = on_chip(inner_send)
    stack = gather(stack, 1, inner_in)
    outer, outer_send = adjoint_outer(after(outer, inner_in), outer_in, high, low)
    outer_in = off_chip(outer_send)
    outer, inner = adjoint_local(outer, inner, high, low)
    inner = inner + inner_in
    inner_back = lax.ppermute(after(inner, outer_in), "sec", [(1, 0)])
    stack = gather(stack, 2, inner)
    outer = after(outer, inner) + outer_in
    outer_back = lax.ppermute(outer, "sec", [(1, 0)])
    stack = gather(stack, 6, outer)
    inner, inner_send = adjoint_inner(seen_inner, inner_back, high, low)
    inner_in = on_chip(inner_send)
    gram = gram_part(stack)
    gram = gram + swap(gram, "elem", 2)
    outer, outer_send = adjoint_outer(after(seen_outer, inner_send), outer_back, high, low)
    outer_in = off_chip(outer_send)
    outer, inner = adjoint_local(outer, inner, high, low)
    inner, inner_send = adjoint_inner(inner, inner_in, high, low)
    inner_in = on_chip(inner_send)
    gram = gram + swap(after(gram, inner_in), "elem", 4)
    outer, outer_send = adjoint_outer(after(outer, inner_in), outer_in, high, low)
    outer_in = off_chip(outer_send)
    outer, inner = adjoint_local(outer, inner, high, low)
    inner = inner + inner_in
    inner_up = lax.ppermute(after(inner, outer_in)[:, :, half:], "sec", [(0, 1)])
    gram = gram + swap(after(gram, outer_in), "elem", 12)
    outer = after(outer, inner) + outer_in
    outer_up = lax.ppermute(outer[:, :, half:], "sec", [(0, 1)])
    gram = gram + swap(after(gram, outer), "sec", 1)
    hess = jnp.transpose(finish(outer, inner, outer_up, inner_up), (1, 0, 2))
    return hess, gram * (1.0 / (elem_total * dofs))


def solution(mesh):
    in_specs = (
        P("col", "elem", None),
        P("sec", "elem", None, None, None),
        P("elem", None),
        P("elem"),
        P("elem", None),
    )
    out_specs = (P("col", "elem", "sec"), P("col", None))
    return jax.shard_map(
        per_device, mesh=mesh, in_specs=in_specs, out_specs=out_specs, check_vma=False
    )
```

time: 113 us -> 92 us (0.81)
  waiting for transfers between devices: 43.8 us -> 22.8 us
  local copies, waits for them, and re-layouts: 11 us -> 1.21 us
  starting transfers between devices: 28.5 us -> 36 us
  Pallas kernels: 25.8 us -> 29 us
    ppermute x27 -> x30, waiting for transfers between devices: 43.8 us -> 22.8 us  [the longest x16 11.1 us: swap(): return lax.ppermute(value, axis, [(i, i ^ mask) for i in range(count)])]
    unnamed x18 -> x6, local copies, waits for them, and re-layouts: 10.9 us -> 1.2 us
    ppermute x27 -> x30, starting transfers between devices: 28.5 us -> 36 us  [the longest x8 17.2 us: off_chip(): return lax.ppermute(value, 'elem', pairs)]
    pallas_call x1, Pallas kernels: 3.37 us -> 5.24 us  [per_device(): high, low = prepare(neighbors, jacobian)]
    pallas_call x19 -> x22, Pallas kernels: 22.3 us -> 23.4 us  [the longest x4 11.5 us: tangent(): outer, inner = tangent_near(outer, inner, inner_in, high, low)]
  transfers between devices with their start and end apart: 27 -> 30, of which waited for: 15 -> 14; matrix products, arithmetic and copies ran while one was open for 1% -> 0% of each run, Pallas kernels for 18% -> 30%
where the time goes in v2:
time: 92 us; the launch traced here: 90.7 us
  starting transfers between devices  36 us (39%)
  Pallas kernels  29 us (32%)
  waiting for transfers between devices  22.8 us (25%)
  local copies, waits for them, and re-layouts  1.21 us (1%)
  between operations  0.95 us (1%)
    ppermute x8, starting transfers between devices, off_chip(): return lax.ppermute(value, 'elem', pairs)  17.2 us
    pallas_call x4, Pallas kernels, tangent(): outer, inner = tangent_near(outer, inner, inner_in, high, low)  11.5 us
    ppermute x16, waiting for transfers between devices, swap(): return lax.ppermute(value, axis, [(i, i ^ mask) for i in range(count)])  11.1 us
    ppermute x16, starting transfers between devices, swap(): return lax.ppermute(value, axis, [(i, i ^ mask) for i in range(count)])  7.28 us
    ppermute x1, waiting for transfers between devices, per_device(): inner_back = lax.ppermute(after(inner, outer_in), 'sec', [(1, 0)])  5.42 us
    pallas_call x1, Pallas kernels, per_device(): high, low = prepare(neighbors, jacobian)  5.24 us
    ppermute x1, starting transfers between devices, to_next(): inner = lax.ppermute(inner, 'sec', [(0, 1)])  4.94 us
    pallas_call x3, Pallas kernels, per_device(): outer, inner = adjoint_local(outer, inner, high, low)  4.05 us
  transfers between devices with their start and end apart: 30, of which 14 were waited for; matrix products, arithmetic and copies ran while one was open for 0% of the time, Pallas kernels for 30%

profile of v2, /device:TPU:16, one launch (start us, length us, event | category | flops | bytes accessed | tf_op | source)
XLA Modules:
  0.0 90.7 jit_solution(11660605202178481711)
XLA Ops:
  1.7 6.0 %collective-permute-start.1 = (f32[3,32,256]{2,1,0:T(8,128)S(1)}, f32[3,32,256]{2,1,0:T(8,128)S(1)}, u32[]{:S(2)}, u32[]{:S(2)}) collective-permute-start(f32[3,32,256]{2,1,0:T(8,128)S(1)} %get-tuple-element.51.outer_ref), channel_id=1, source_target_pairs={{0,15},{1,2},{2,1},{3,4},{4,3},{5,6},{6,5},{7,8},{8,7},{9,10},{10,... | collective-permute-start | bytes 294920 | tf_op jit(solution)/shard_map/ppermute | solution.py:279
  7.6 5.2 %prepare.1 = (bf16[42,256,256]{2,1,0:T(8,128)(2,1)S(1)}, bf16[42,256,256]{2,1,0:T(8,128)(2,1)S(1)}) custom-call(s32[6,7]{1,0:T(8,128)} %nbr_ref.1, f32[1,6,7,256,256]{4,3,2,1,0:T(8,128)} %jac_ref.1), custom_call_target="tpu_custom_call" | custom-call | flops 300000000 | bytes 20000000 | tf_op jit(solution)/shard_map/prepare/pallas_call | solution.py:348
  12.9 2.9 %tangent_near.4 = (f32[3,32,256]{2,1,0:T(8,128)S(1)}, f32[3,32,256]{2,1,0:T(8,128)S(1)}) custom-call(f32[3,32,256]{2,1,0:T(8,128)S(1)} %get-tuple-element.51.outer_ref, f32[3,32,256]{2,1,0:T(8,128)S(1)} %get-tuple-element.52.inner_ref, f32[3,32,256]{2,1,0:T(8,128)S(1)} %collective-permute-done.halo_ref, ...), custom_call_target="tpu_custom_call" | custom-call | flops 300000000 | bytes 100000 | tf_op jit(solution)/shard_map/tangent_near/pallas_call | solution.py:340
  17.5 2.9 %tangent_near.5 = (f32[3,32,256]{2,1,0:T(8,128)S(1)}, f32[3,32,256]{2,1,0:T(8,128)S(1)}) custom-call(f32[3,32,256]{2,1,0:T(8,128)S(1)} %tangent_far.4.outer_ref, f32[3,32,256]{2,1,0:T(8,128)S(1)} %get-tuple-element.56.inner_ref, f32[3,32,256]{2,1,0:T(8,128)S(1)} %collective-permute-done.2.halo_ref, bf16[42,256,256]{2,1,0:T(8,128)(2,1)S(1)} %get-tuple-element.53.high_ref, ...), custom_call_target="tpu_custom_call" | custom-call | flops 300000000 | bytes 100000 | tf_op jit(solution)/shard_map/tangent_near/pallas_call | solution.py:340
  20.4 4.9 %collective-permute-start.5 = (f32[3,32,256]{2,1,0:T(8,128)S(1)}, f32[3,32,256]{2,1,0:T(8,128)S(1)}, u32[]{:S(2)}, u32[]{:S(2)}) collective-permute-start(f32[3,32,256]{2,1,0:T(8,128)S(1)} %get-tuple-element.58.inner0_ref), channel_id=1, source_target_pairs={{0,128},{1,129},{2,130},{3,131},{4,132},{5,133},{6,134},{7,135},{8... | collective-permute-start | bytes 294920 | tf_op jit(solution)/shard_map/ppermute | solution.py:345
  27.9 1.6 %collective-permute-done.4.outer_ref = f32[3,32,256]{2,1,0:T(8,128)S(1)} collective-permute-done((f32[3,32,256]{2,1,0:T(8,128)S(1)}, f32[3,32,256]{2,1,0:T(8,128)S(1)}, u32[]{:S(2)}, u32[]{:S(2)}) %collective-permute-start.4) | collective-permute-done | bytes 98336 | tf_op jit(solution)/shard_map/ppermute | solution.py:346
  29.6 1.8 %collective-permute-start.7 = (f32[3,32,256]{2,1,0:T(8,128)S(1)}, f32[3,32,256]{2,1,0:T(8,128)S(1)}, u32[]{:S(2)}, u32[]{:S(2)}) collective-permute-start(f32[3,32,256]{2,1,0:T(8,128)S(1)} %collective-permute-done.4.outer_ref), channel_id=1, source_target_pairs={{0,15},{1,2},{2,1},{3,4},{4,3},{5,6},{6,5},{7,8},{8,7},{9,10},{10,... | collective-permute-start | bytes 294920 | tf_op jit(solution)/shard_map/ppermute | solution.py:279
  31.4 2.9 %tangent_near.6 = (f32[3,32,256]{2,1,0:T(8,128)S(1)}, f32[3,32,256]{2,1,0:T(8,128)S(1)}) custom-call(f32[3,32,256]{2,1,0:T(8,128)S(1)} %collective-permute-done.4.outer_ref, f32[3,32,256]{2,1,0:T(8,128)S(1)} %collective-permute-done.5.inner_ref, f32[3,32,256]{2,1,0:T(8,128)S(1)} %collective-permute-done.6.halo_ref, ...), custom_call_target="tpu_custom_call" | custom-call | flops 300000000 | bytes 100000 | tf_op jit(solution)/shard_map/tangent_near/pallas_call | solution.py:340
  35.4 2.0 %collective-permute-start.9 = (f32[3,32,256]{2,1,0:T(8,128)S(1)}, f32[3,32,256]{2,1,0:T(8,128)S(1)}, u32[]{:S(2)}, u32[]{:S(2)}) collective-permute-start(f32[3,32,256]{2,1,0:T(8,128)S(1)} %tangent_far.6.outer_ref), channel_id=1, source_target_pairs={{0,15},{1,2},{2,1},{3,4},{4,3},{5,6},{6,5},{7,8},{8,7},{9,10},{10,... | collective-permute-start | bytes 294920 | tf_op jit(solution)/shard_map/ppermute | solution.py:279
  37.4 2.9 %tangent_near.7 = (f32[3,32,256]{2,1,0:T(8,128)S(1)}, f32[3,32,256]{2,1,0:T(8,128)S(1)}) custom-call(f32[3,32,256]{2,1,0:T(8,128)S(1)} %tangent_far.6.outer_ref, f32[3,32,256]{2,1,0:T(8,128)S(1)} %get-tuple-element.60.inner_ref, f32[3,32,256]{2,1,0:T(8,128)S(1)} %collective-permute-done.8.halo_ref, bf16[42,256,256]{2,1,0:T(8,128)(2,1)S(1)} %get-tuple-element.53.high_ref, ...), custom_call_target="tpu_custom_call" | custom-call | flops 300000000 | bytes 100000 | tf_op jit(solution)/shard_map/tangent_near/pallas_call | solution.py:340
  43.7 1.8 %collective-permute-start.12 = (f32[3,32,256]{2,1,0:T(8,128)S(1)}, f32[3,32,256]{2,1,0:T(8,128)S(1)}, u32[]{:S(2)}, u32[]{:S(2)}) collective-permute-start(f32[3,32,256]{2,1,0:T(8,128)S(1)} %seen_outer.1), channel_id=1, source_target_pairs={{0,15},{1,2},{2,1},{3,4},{4,3},{5,6},{6,5},{7,8},{8,7},{9,10},{10,... | collective-permute-start | bytes 294920 | tf_op jit(solution)/shard_map/ppermute | solution.py:279
  45.6 1.3 %adjoint_local.4 = (f32[3,32,256]{2,1,0:T(8,128)S(1)}, f32[3,32,256]{2,1,0:T(8,128)S(1)}) custom-call(f32[3,32,256]{2,1,0:T(8,128)S(1)} %get-tuple-element.76.outer_ref.value_ref.total_ref, f32[3,32,256]{2,1,0:T(8,128)S(1)} %get-tuple-element.64.inner_ref.total_ref, bf16[42,256,256]{2,1,0:T(8,128)(2,1)S(1)} %get-tuple-element.53.high_ref, ...), custom_call_target="tpu_custom_call" | custom-call | flops 1000000000 | bytes 100000 | tf_op jit(solution)/shard_map/adjoint_local/pallas_call | solution.py:361
  49.6 1.6 %collective-permute-start.13 = (f32[3,32,256]{2,1,0:T(8,128)S(1)}, f32[3,32,256]{2,1,0:T(8,128)S(1)}, u32[]{:S(2)}, u32[]{:S(2)}) collective-permute-start(f32[3,32,256]{2,1,0:T(8,128)S(1)} %get-tuple-element.73), channel_id=1, source_target_pairs={{0,15},{1,2},{2,1},{3,4},{4,3},{5,6},{6,5},{7,8},{8,7},{9,10},{10,... | collective-permute-start | bytes 294920 | tf_op jit(solution)/shard_map/ppermute | solution.py:279
  51.2 1.3 %adjoint_local.5 = (f32[3,32,256]{2,1,0:T(8,128)S(1)}, f32[3,32,256]{2,1,0:T(8,128)S(1)}) custom-call(f32[3,32,256]{2,1,0:T(8,128)S(1)} %get-tuple-element.70.outer_ref, f32[3,32,256]{2,1,0:T(8,128)S(1)} %get-tuple-element.71.inner_ref, bf16[42,256,256]{2,1,0:T(8,128)(2,1)S(1)} %get-tuple-element.53.high_ref, bf16[42,256,256]{2,1,0:T(8,128)(2,1)S(1)} %get-tuple-element.54.low_ref), custom_call_target="tpu_custom_call" | custom-call | flops 1000000000 | bytes 100000 | tf_op jit(solution)/shard_map/adjoint_local/pallas_call | solution.py:367
  52.6 1.4 %collective-permute-start.24 = (f32[2,2,32,64]{3,2,1,0:T(8,128)S(1)}, f32[2,2,32,64]{3,2,1,0:T(8,128)S(1)}, u32[]{:S(2)}, u32[]{:S(2)}) collective-permute-start(f32[2,2,32,64]{3,2,1,0:T(8,128)S(1)} %pad_maximum_fusion.2), channel_id=1, source_target_pairs={{0,32},{16,48},{32,0},{48,16},{64,96},{80,112},{96,64},{112,80},{1... | collective-permute-start | bytes 98312 | tf_op jit(solution)/shard_map/ppermute | solution.py:273
  58.0 5.4 %collective-permute-done.14.halo_ref = f32[3,32,256]{2,1,0:T(8,128)S(1)} collective-permute-done((f32[3,32,256]{2,1,0:T(8,128)S(1)}, f32[3,32,256]{2,1,0:T(8,128)S(1)}, u32[]{:S(2)}, u32[]{:S(2)}) %collective-permute-start.14) | collective-permute-done | bytes 98336 | tf_op jit(solution)/shard_map/ppermute | solution.py:369
  64.9 1.4 %collective-permute-start.18 = (f32[3,32,256]{2,1,0:T(8,128)S(1)}, f32[3,32,256]{2,1,0:T(8,128)S(1)}, u32[]{:S(2)}, u32[]{:S(2)}) collective-permute-start(f32[3,32,256]{2,1,0:T(8,128)S(1)} %get-tuple-element.85), channel_id=1, source_target_pairs={{0,15},{1,2},{2,1},{3,4},{4,3},{5,6},{6,5},{7,8},{8,7},{9,10},{10,... | collective-permute-start | bytes 294920 | tf_op jit(solution)/shard_map/ppermute | solution.py:279
  66.2 1.3 %adjoint_local.6 = (f32[3,32,256]{2,1,0:T(8,128)S(1)}, f32[3,32,256]{2,1,0:T(8,128)S(1)}) custom-call(f32[3,32,256]{2,1,0:T(8,128)S(1)} %get-tuple-element.79.outer_ref, f32[3,32,256]{2,1,0:T(8,128)S(1)} %get-tuple-element.80.inner_ref, bf16[42,256,256]{2,1,0:T(8,128)(2,1)S(1)} %get-tuple-element.53.high_ref, bf16[42,256,256]{2,1,0:T(8,128)(2,1)S(1)} %get-tuple-element.54.low_ref), custom_call_target="tpu_custom_call" | custom-call | flops 1000000000 | bytes 100000 | tf_op jit(solution)/shard_map/adjoint_local/pallas_call | solution.py:380
  70.5 1.4 %collective-permute-start.19 = (f32[3,32,256]{2,1,0:T(8,128)S(1)}, f32[3,32,256]{2,1,0:T(8,128)S(1)}, u32[]{:S(2)}, u32[]{:S(2)}) collective-permute-start(f32[3,32,256]{2,1,0:T(8,128)S(1)} %get-tuple-element.91), channel_id=1, source_target_pairs={{0,15},{1,2},{2,1},{3,4},{4,3},{5,6},{6,5},{7,8},{8,7},{9,10},{10,... | collective-permute-start | bytes 294920 | tf_op jit(solution)/shard_map/ppermute | solution.py:279
  73.8 1.3 %adjoint_local.7 = (f32[3,32,256]{2,1,0:T(8,128)S(1)}, f32[3,32,256]{2,1,0:T(8,128)S(1)}) custom-call(f32[3,32,256]{2,1,0:T(8,128)S(1)} %get-tuple-element.86.outer_ref, f32[3,32,256]{2,1,0:T(8,128)S(1)} %get-tuple-element.87.inner_ref, bf16[42,256,256]{2,1,0:T(8,128)(2,1)S(1)} %get-tuple-element.53.high_ref, bf16[42,256,256]{2,1,0:T(8,128)(2,1)S(1)} %get-tuple-element.54.low_ref), custom_call_target="tpu_custom_call" | custom-call | flops 1000000000 | bytes 100000 | tf_op jit(solution)/shard_map/adjoint_local/pallas_call | solution.py:386
  75.8 1.4 %collective-permute-start.20 = (f32[3,32,128]{2,1,0:T(8,128)S(1)}, f32[3,32,128]{2,1,0:T(8,128)S(1)}, u32[]{:S(2)}, u32[]{:S(2)}) collective-permute-start(f32[3,32,128]{2,1,0:T(8,128)S(1)} %slice.8), channel_id=1, source_target_pairs={{0,128},{1,129},{2,130},{3,131},{4,132},{5,133},{6,134},{7,135},{8... | collective-permute-start | bytes 147464 | tf_op jit(solution)/shard_map/ppermute | solution.py:391
  78.6 2.4 %collective-permute-start.28 = (f32[32,256]{1,0:T(8,128)S(1)}, f32[32,256]{1,0:T(8,128)S(1)}, u32[]{:S(2)}, u32[]{:S(2)}) collective-permute-start(f32[32,256]{1,0:T(8,128)S(1)} %add.29), channel_id=1, source_target_pairs={{0,12},{1,13},{2,14},{3,15},{4,8},{5,9},{6,10},{7,11},{8,4},{9,5},... | collective-permute-start | bytes 98312 | tf_op jit(solution)/shard_map/ppermute | solution.py:273
  81.0 3.7 %collective-permute-done.28 = f32[32,256]{1,0:T(8,128)S(1)} collective-permute-done((f32[32,256]{1,0:T(8,128)S(1)}, f32[32,256]{1,0:T(8,128)S(1)}, u32[]{:S(2)}, u32[]{:S(2)}) %collective-permute-start.28) | collective-permute-done | bytes 32800 | tf_op jit(solution)/shard_map/ppermute | solution.py:273
  85.4 4.7 %collective-permute-done.29 = f32[32,256]{1,0:T(8,128)S(1)} collective-permute-done((f32[32,256]{1,0:T(8,128)S(1)}, f32[32,256]{1,0:T(8,128)S(1)}, u32[]{:S(2)}, u32[]{:S(2)}) %collective-permute-start.29) | collective-permute-done | bytes 32800 | tf_op jit(solution)/shard_map/ppermute | solution.py:273
  (80 shorter events, 26.0 us)
Async XLA Ops:
  1.6 11.3 %collective-permute-start = (f32[3,32,256]{2,1,0:T(8,128)S(1)}, f32[3,32,256]{2,1,0:T(8,128)S(1)}, u32[]{:S(2)}, u32[]{:S(2)}) collective-permute-start(f32[3,32,256]{2,1,0:T(8,128)S(1)} %get-tuple-element.52.inner_ref), channel_id=1, source_target_pairs={{0,1},{1,0},{2,3},{3,2},{4,5},{5,4},{6,7},{7,6},{8,9},{9,8},{10,11... | collective-permute-start | bytes 294920 | tf_op jit(solution)/shard_map/ppermute | solution.py:273
  1.7 14.2 %collective-permute-start.1 = (f32[3,32,256]{2,1,0:T(8,128)S(1)}, f32[3,32,256]{2,1,0:T(8,128)S(1)}, u32[]{:S(2)}, u32[]{:S(2)}) collective-permute-start(f32[3,32,256]{2,1,0:T(8,128)S(1)} %get-tuple-element.51.outer_ref), channel_id=1, source_target_pairs={{0,15},{1,2},{2,1},{3,4},{4,3},{5,6},{6,5},{7,8},{8,7},{9,10},{10,... | collective-permute-start | bytes 294920 | tf_op jit(solution)/shard_map/ppermute | solution.py:279
  16.4 9.0 %collective-permute-start.3 = (f32[3,32,256]{2,1,0:T(8,128)S(1)}, f32[3,32,256]{2,1,0:T(8,128)S(1)}, u32[]{:S(2)}, u32[]{:S(2)}) collective-permute-start(f32[3,32,256]{2,1,0:T(8,128)S(1)} %tangent_far.4.outer_ref), channel_id=1, source_target_pairs={{0,15},{1,2},{2,1},{3,4},{4,3},{5,6},{6,5},{7,8},{8,7},{9,10},{10,... | collective-permute-start | bytes 294920 | tf_op jit(solution)/shard_map/ppermute | solution.py:279
  20.4 7.5 %collective-permute-start.5 = (f32[3,32,256]{2,1,0:T(8,128)S(1)}, f32[3,32,256]{2,1,0:T(8,128)S(1)}, u32[]{:S(2)}, u32[]{:S(2)}) collective-permute-start(f32[3,32,256]{2,1,0:T(8,128)S(1)} %get-tuple-element.58.inner0_ref), channel_id=1, source_target_pairs={{0,128},{1,129},{2,130},{3,131},{4,132},{5,133},{6,134},{7,135},{8... | collective-permute-start | bytes 294920 | tf_op jit(solution)/shard_map/ppermute | solution.py:345
  29.6 5.3 %collective-permute-start.7 = (f32[3,32,256]{2,1,0:T(8,128)S(1)}, f32[3,32,256]{2,1,0:T(8,128)S(1)}, u32[]{:S(2)}, u32[]{:S(2)}) collective-permute-start(f32[3,32,256]{2,1,0:T(8,128)S(1)} %collective-permute-done.4.outer_ref), channel_id=1, source_target_pairs={{0,15},{1,2},{2,1},{3,4},{4,3},{5,6},{6,5},{7,8},{8,7},{9,10},{10,... | collective-permute-start | bytes 294920 | tf_op jit(solution)/shard_map/ppermute | solution.py:279
  35.4 5.5 %collective-permute-start.9 = (f32[3,32,256]{2,1,0:T(8,128)S(1)}, f32[3,32,256]{2,1,0:T(8,128)S(1)}, u32[]{:S(2)}, u32[]{:S(2)}) collective-permute-start(f32[3,32,256]{2,1,0:T(8,128)S(1)} %tangent_far.6.outer_ref), channel_id=1, source_target_pairs={{0,15},{1,2},{2,1},{3,4},{4,3},{5,6},{6,5},{7,8},{8,7},{9,10},{10,... | collective-permute-start | bytes 294920 | tf_op jit(solution)/shard_map/ppermute | solution.py:279
  42.8 4.5 %collective-permute-start.22 = (f32[32,64]{1,0:T(8,128)S(1)}, f32[32,64]{1,0:T(8,128)S(1)}, u32[]{:S(2)}, u32[]{:S(2)}) collective-permute-start(f32[32,64]{1,0:T(8,128)S(1)} %get-tuple-element.93), channel_id=1, source_target_pairs={{0,1},{1,0},{2,3},{3,2},{4,5},{5,4},{6,7},{7,6},{8,9},{9,8},{10,11... | collective-permute-start | bytes 24584 | tf_op jit(solution)/shard_map/ppermute | solution.py:273
  42.9 4.1 %collective-permute-start.10 = (f32[3,32,256]{2,1,0:T(8,128)S(1)}, f32[3,32,256]{2,1,0:T(8,128)S(1)}, u32[]{:S(2)}, u32[]{:S(2)}) collective-permute-start(f32[3,32,256]{2,1,0:T(8,128)S(1)} %get-tuple-element.67), channel_id=1, source_target_pairs={{0,1},{1,0},{2,3},{3,2},{4,5},{5,4},{6,7},{7,6},{8,9},{9,8},{10,11... | collective-permute-start | bytes 294920 | tf_op jit(solution)/shard_map/ppermute | solution.py:273
  43.7 5.5 %collective-permute-start.12 = (f32[3,32,256]{2,1,0:T(8,128)S(1)}, f32[3,32,256]{2,1,0:T(8,128)S(1)}, u32[]{:S(2)}, u32[]{:S(2)}) collective-permute-start(f32[3,32,256]{2,1,0:T(8,128)S(1)} %seen_outer.1), channel_id=1, source_target_pairs={{0,15},{1,2},{2,1},{3,4},{4,3},{5,6},{6,5},{7,8},{8,7},{9,10},{10,... | collective-permute-start | bytes 294920 | tf_op jit(solution)/shard_map/ppermute | solution.py:279
  48.6 4.0 %collective-permute-start.23 = (f32[1,2,32,64]{3,2,1,0:T(8,128)S(1)}, f32[1,2,32,64]{3,2,1,0:T(8,128)S(1)}, u32[]{:S(2)}, u32[]{:S(2)}) collective-permute-start(f32[1,2,32,64]{3,2,1,0:T(8,128)S(1)} %maximum_bitcast_fusion), channel_id=1, source_target_pairs={{0,16},{16,0},{32,48},{48,32},{64,80},{80,64},{96,112},{112,96},{1... | collective-permute-start | bytes 49160 | tf_op jit(solution)/shard_map/ppermute | solution.py:273
  49.6 5.3 %collective-permute-start.13 = (f32[3,32,256]{2,1,0:T(8,128)S(1)}, f32[3,32,256]{2,1,0:T(8,128)S(1)}, u32[]{:S(2)}, u32[]{:S(2)}) collective-permute-start(f32[3,32,256]{2,1,0:T(8,128)S(1)} %get-tuple-element.73), channel_id=1, source_target_pairs={{0,15},{1,2},{2,1},{3,4},{4,3},{5,6},{6,5},{7,8},{8,7},{9,10},{10,... | collective-permute-start | bytes 294920 | tf_op jit(solution)/shard_map/ppermute | solution.py:279
  52.6 4.9 %collective-permute-start.24 = (f32[2,2,32,64]{3,2,1,0:T(8,128)S(1)}, f32[2,2,32,64]{3,2,1,0:T(8,128)S(1)}, u32[]{:S(2)}, u32[]{:S(2)}) collective-permute-start(f32[2,2,32,64]{3,2,1,0:T(8,128)S(1)} %pad_maximum_fusion.2), channel_id=1, source_target_pairs={{0,32},{16,48},{32,0},{48,16},{64,96},{80,112},{96,64},{112,80},{1... | collective-permute-start | bytes 98312 | tf_op jit(solution)/shard_map/ppermute | solution.py:273
  54.8 8.6 %collective-permute-start.14 = (f32[3,32,256]{2,1,0:T(8,128)S(1)}, f32[3,32,256]{2,1,0:T(8,128)S(1)}, u32[]{:S(2)}, u32[]{:S(2)}) collective-permute-start(f32[3,32,256]{2,1,0:T(8,128)S(1)} %add.24), channel_id=1, source_target_pairs={{128,0},{129,1},{130,2},{131,3},{132,4},{133,5},{134,6},{135,7},{1... | collective-permute-start | bytes 294920 | tf_op jit(solution)/shard_map/ppermute | solution.py:369
  56.2 8.3 %collective-permute-start.15 = (f32[3,32,256]{2,1,0:T(8,128)S(1)}, f32[3,32,256]{2,1,0:T(8,128)S(1)}, u32[]{:S(2)}, u32[]{:S(2)}) collective-permute-start(f32[3,32,256]{2,1,0:T(8,128)S(1)} %add.25), channel_id=1, source_target_pairs={{128,0},{129,1},{130,2},{131,3},{132,4},{133,5},{134,6},{135,7},{1... | collective-permute-start | bytes 294920 | tf_op jit(solution)/shard_map/ppermute | solution.py:372
  57.5 10.7 %collective-permute-start.25 = (f32[4,2,32,64]{3,2,1,0:T(8,128)S(1)}, f32[4,2,32,64]{3,2,1,0:T(8,128)S(1)}, u32[]{:S(2)}, u32[]{:S(2)}) collective-permute-start(f32[4,2,32,64]{3,2,1,0:T(8,128)S(1)} %pad_maximum_fusion.1), channel_id=1, source_target_pairs={{0,96},{16,112},{32,64},{48,80},{64,32},{80,48},{96,0},{112,16},{1... | collective-permute-start | bytes 196616 | tf_op jit(solution)/shard_map/ppermute | solution.py:273
  63.8 3.8 %collective-permute-start.16 = (f32[3,32,256]{2,1,0:T(8,128)S(1)}, f32[3,32,256]{2,1,0:T(8,128)S(1)}, u32[]{:S(2)}, u32[]{:S(2)}) collective-permute-start(f32[3,32,256]{2,1,0:T(8,128)S(1)} %get-tuple-element.75), channel_id=1, source_target_pairs={{0,1},{1,0},{2,3},{3,2},{4,5},{5,4},{6,7},{7,6},{8,9},{9,8},{10,11... | collective-permute-start | bytes 294920 | tf_op jit(solution)/shard_map/ppermute | solution.py:273
  64.9 5.3 %collective-permute-start.18 = (f32[3,32,256]{2,1,0:T(8,128)S(1)}, f32[3,32,256]{2,1,0:T(8,128)S(1)}, u32[]{:S(2)}, u32[]{:S(2)}) collective-permute-start(f32[3,32,256]{2,1,0:T(8,128)S(1)} %get-tuple-element.85), channel_id=1, source_target_pairs={{0,15},{1,2},{2,1},{3,4},{4,3},{5,6},{6,5},{7,8},{8,7},{9,10},{10,... | collective-permute-start | bytes 294920 | tf_op jit(solution)/shard_map/ppermute | solution.py:279
  68.6 4.0 %collective-permute-start.26 = (f32[32,256]{1,0:T(8,128)S(1)}, f32[32,256]{1,0:T(8,128)S(1)}, u32[]{:S(2)}, u32[]{:S(2)}) collective-permute-start(f32[32,256]{1,0:T(8,128)S(1)} %gram_part.1), channel_id=1, source_target_pairs={{0,2},{1,3},{2,0},{3,1},{4,6},{5,7},{6,4},{7,5},{8,10},{9,11},{10,... | collective-permute-start | bytes 98312 | tf_op jit(solution)/shard_map/ppermute | solution.py:273
  70.5 5.3 %collective-permute-start.19 = (f32[3,32,256]{2,1,0:T(8,128)S(1)}, f32[3,32,256]{2,1,0:T(8,128)S(1)}, u32[]{:S(2)}, u32[]{:S(2)}) collective-permute-start(f32[3,32,256]{2,1,0:T(8,128)S(1)} %get-tuple-element.91), channel_id=1, source_target_pairs={{0,15},{1,2},{2,1},{3,4},{4,3},{5,6},{6,5},{7,8},{8,7},{9,10},{10,... | collective-permute-start | bytes 294920 | tf_op jit(solution)/shard_map/ppermute | solution.py:279
  72.6 6.0 %collective-permute-start.27 = (f32[32,256]{1,0:T(8,128)S(1)}, f32[32,256]{1,0:T(8,128)S(1)}, u32[]{:S(2)}, u32[]{:S(2)}) collective-permute-start(f32[32,256]{1,0:T(8,128)S(1)} %add.28), channel_id=1, source_target_pairs={{0,4},{1,5},{2,6},{3,7},{4,0},{5,1},{6,2},{7,3},{8,12},{9,13},{10,... | collective-permute-start | bytes 98312 | tf_op jit(solution)/shard_map/ppermute | solution.py:273
  75.8 8.9 %collective-permute-start.20 = (f32[3,32,128]{2,1,0:T(8,128)S(1)}, f32[3,32,128]{2,1,0:T(8,128)S(1)}, u32[]{:S(2)}, u32[]{:S(2)}) collective-permute-start(f32[3,32,128]{2,1,0:T(8,128)S(1)} %slice.8), channel_id=1, source_target_pairs={{0,128},{1,129},{2,130},{3,131},{4,132},{5,133},{6,134},{7,135},{8... | collective-permute-start | bytes 147464 | tf_op jit(solution)/shard_map/ppermute | solution.py:391
  77.3 7.5 %collective-permute-start.21 = (f32[3,32,128]{2,1,0:T(8,128)S(1)}, f32[3,32,128]{2,1,0:T(8,128)S(1)}, u32[]{:S(2)}, u32[]{:S(2)}) collective-permute-start(f32[3,32,128]{2,1,0:T(8,128)S(1)} %slice.7), channel_id=1, source_target_pairs={{0,128},{1,129},{2,130},{3,131},{4,132},{5,133},{6,134},{7,135},{8... | collective-permute-start | bytes 147464 | tf_op jit(solution)/shard_map/ppermute | solution.py:388
  78.6 6.1 %collective-permute-start.28 = (f32[32,256]{1,0:T(8,128)S(1)}, f32[32,256]{1,0:T(8,128)S(1)}, u32[]{:S(2)}, u32[]{:S(2)}) collective-permute-start(f32[32,256]{1,0:T(8,128)S(1)} %add.29), channel_id=1, source_target_pairs={{0,12},{1,13},{2,14},{3,15},{4,8},{5,9},{6,10},{7,11},{8,4},{9,5},... | collective-permute-start | bytes 98312 | tf_op jit(solution)/shard_map/ppermute | solution.py:273
  84.7 5.4 %collective-permute-start.29 = (f32[32,256]{1,0:T(8,128)S(1)}, f32[32,256]{1,0:T(8,128)S(1)}, u32[]{:S(2)}, u32[]{:S(2)}) collective-permute-start(f32[32,256]{1,0:T(8,128)S(1)} %add.30), channel_id=1, source_target_pairs={{0,128},{128,0},{1,129},{129,1},{2,130},{130,2},{3,131},{131,3},{4... | collective-permute-start | bytes 98312 | tf_op jit(solution)/shard_map/ppermute | solution.py:273
  (9 other events, 17.5 us)

commit v3 on v2

--- a/solution.py
+++ b/solution.py
@@ -240,14 +240,14 @@
             inner_out[m - RADIUS] = total
 
 
-def finish_body(outer_ref, inner_ref, outer_up_ref, inner_up_ref, out_ref):
+def finish_body(scale, field_ref, upper_ref, gram_ref, rest_ref, out_ref, gram_out):
     elems, cols, half = out_ref.shape
     odd = odd_device()
     first = lax.axis_index("sec") == 0
     for u in range(elems):
-        full, upper = (outer_ref, outer_up_ref) if u < RADIUS else (inner_ref, inner_up_ref)
         place = jnp.where(odd, elems - 1 - u, u)
-        out_ref[place] = jnp.where(first, full[u % RADIUS, :, :half], upper[u % RADIUS])
+        out_ref[place] = jnp.where(first, field_ref[u, :, :half], upper_ref[u])
+    gram_out[...] = (gram_ref[...] + rest_ref[...]) * scale
 
 
 def gram_body(stack_ref, out_ref):
@@ -294,6 +294,7 @@
     edge = vmem((RADIUS, cols, dofs))
     count = obs_weights.shape[0]
     half = dofs // 2
+    col_count = lax.axis_size("col")
 
     def pair(slots):
         return pltpu.VMEM((slots, 2 * cols, dofs), BF16)
@@ -328,9 +329,13 @@
         adjoint_inner_body, "adjoint_inner", (edge, edge), [IN_VMEM] * 4, (pair(RADIUS),),
     )
     finish = call(
-        finish_body, "finish", jax.ShapeDtypeStruct((elems, cols, half), F32), [IN_VMEM] * 4
-    )
-    col_count = lax.axis_size("col")
+        functools.partial(finish_body, 1.0 / (elem_total * dofs)), "finish",
+        (
+            jax.ShapeDtypeStruct((elems, cols, half), F32),
+            jax.ShapeDtypeStruct((cols, cols * col_count), F32),
+        ),
+        [IN_VMEM] * 4,
+    )
     gram_part = call(gram_body, "gram_part", vmem((cols, cols * col_count)), [IN_VMEM])
 
     def tangent(outer, inner, high, low):
@@ -385,13 +390,12 @@
     outer_in = off_chip(outer_send)
     outer, inner = adjoint_local(outer, inner, high, low)
     inner = inner + inner_in
-    inner_up = lax.ppermute(after(inner, outer_in)[:, :, half:], "sec", [(0, 1)])
     gram = gram + swap(after(gram, outer_in), "elem", 12)
     outer = after(outer, inner) + outer_in
-    outer_up = lax.ppermute(outer[:, :, half:], "sec", [(0, 1)])
-    gram = gram + swap(after(gram, outer), "sec", 1)
-    hess = jnp.transpose(finish(outer, inner, outer_up, inner_up), (1, 0, 2))
-    return hess, gram * (1.0 / (elem_total * dofs))
+    field = jnp.concatenate([outer, inner])
+    upper = lax.ppermute(field[:, :, half:], "sec", [(0, 1)])
+    hess, gram = finish(field, upper, gram, swap(gram, "sec", 1))
+    return jnp.transpose(hess, (1, 0, 2)), gram
 
 
 def solution(mesh):

time: 92 us -> 89.9 us (0.977); the launches traced: 90.7 us -> 89.6 us
  starting transfers between devices: 36 us -> 34 us
  waiting for transfers between devices: 22.8 us -> 24.3 us
    ppermute x16, waiting for transfers between devices: 11.1 us -> 13.3 us  [swap(): return lax.ppermute(value, axis, [(i, i ^ mask) for i in range(count)])]
    ppermute x2 -> x1, starting transfers between devices: 2.74 us -> 1.46 us  [per_device(): upper = lax.ppermute(field[:, :, half:], 'sec', [(0, 1)])]
  transfers between devices with their start and end apart: 30 -> 29, of which waited for: 14 -> 14; matrix products, arithmetic and copies ran while one was open for 0% -> 0% of each run, Pallas kernels for 30% -> 30%
where the time goes in v3:
time: 89.9 us; the launch traced here: 89.6 us
  starting transfers between devices  34 us (38%)
  Pallas kernels  29 us (32%)
  waiting for transfers between devices  24.3 us (27%)
  local copies, waits for them, and re-layouts  1.2 us (1%)
  between operations  0.92 us (1%)
    ppermute x8, starting transfers between devices, off_chip(): return lax.ppermute(value, 'elem', pairs)  17.2 us
    ppermute x16, waiting for transfers between devices, swap(): return lax.ppermute(value, axis, [(i, i ^ mask) for i in range(count)])  13.3 us
    pallas_call x4, Pallas kernels, tangent(): outer, inner = tangent_near(outer, inner, inner_in, high, low)  11.5 us
    ppermute x16, starting transfers between devices, swap(): return lax.ppermute(value, axis, [(i, i ^ mask) for i in range(count)])  6.54 us
    ppermute x1, waiting for transfers between devices, per_device(): inner_back = lax.ppermute(after(inner, outer_in), 'sec', [(1, 0)])  5.42 us
    pallas_call x1, Pallas kernels, per_device(): high, low = prepare(neighbors, jacobian)  5.24 us
    ppermute x1, starting transfers between devices, to_next(): inner = lax.ppermute(inner, 'sec', [(0, 1)])  4.94 us
    pallas_call x3, Pallas kernels, per_device(): outer, inner = adjoint_local(outer, inner, high, low)  4.05 us
  transfers between devices with their start and end apart: 29, of which 14 were waited for; matrix products, arithmetic and copies ran while one was open for 0% of the time, Pallas kernels for 30%

profile of v3, /device:TPU:16, one launch (start us, length us, event | category | flops | bytes accessed | tf_op | source)
XLA Modules:
  0.0 89.6 jit_solution(8167021671309859852)
XLA Ops:
  1.7 6.0 %collective-permute-start.1 = (f32[3,32,256]{2,1,0:T(8,128)S(1)}, f32[3,32,256]{2,1,0:T(8,128)S(1)}, u32[]{:S(2)}, u32[]{:S(2)}) collective-permute-start(f32[3,32,256]{2,1,0:T(8,128)S(1)} %get-tuple-element.51.outer_ref), channel_id=1, source_target_pairs={{0,15},{1,2},{2,1},{3,4},{4,3},{5,6},{6,5},{7,8},{8,7},{9,10},{10,... | collective-permute-start | bytes 294920 | tf_op jit(solution)/shard_map/ppermute | solution.py:279
  7.6 5.2 %prepare.1 = (bf16[42,256,256]{2,1,0:T(8,128)(2,1)S(1)}, bf16[42,256,256]{2,1,0:T(8,128)(2,1)S(1)}) custom-call(s32[6,7]{1,0:T(8,128)} %nbr_ref.1, f32[1,6,7,256,256]{4,3,2,1,0:T(8,128)} %jac_ref.1), custom_call_target="tpu_custom_call" | custom-call | flops 300000000 | bytes 20000000 | tf_op jit(solution)/shard_map/prepare/pallas_call | solution.py:353
  12.9 2.9 %tangent_near.4 = (f32[3,32,256]{2,1,0:T(8,128)S(1)}, f32[3,32,256]{2,1,0:T(8,128)S(1)}) custom-call(f32[3,32,256]{2,1,0:T(8,128)S(1)} %get-tuple-element.51.outer_ref, f32[3,32,256]{2,1,0:T(8,128)S(1)} %get-tuple-element.52.inner_ref, f32[3,32,256]{2,1,0:T(8,128)S(1)} %collective-permute-done.halo_ref, ...), custom_call_target="tpu_custom_call" | custom-call | flops 300000000 | bytes 100000 | tf_op jit(solution)/shard_map/tangent_near/pallas_call | solution.py:345
  17.5 2.9 %tangent_near.5 = (f32[3,32,256]{2,1,0:T(8,128)S(1)}, f32[3,32,256]{2,1,0:T(8,128)S(1)}) custom-call(f32[3,32,256]{2,1,0:T(8,128)S(1)} %tangent_far.4.outer_ref, f32[3,32,256]{2,1,0:T(8,128)S(1)} %get-tuple-element.56.inner_ref, f32[3,32,256]{2,1,0:T(8,128)S(1)} %collective-permute-done.2.halo_ref, bf16[42,256,256]{2,1,0:T(8,128)(2,1)S(1)} %get-tuple-element.53.high_ref, ...), custom_call_target="tpu_custom_call" | custom-call | flops 300000000 | bytes 100000 | tf_op jit(solution)/shard_map/tangent_near/pallas_call | solution.py:345
  20.4 4.9 %collective-permute-start.5 = (f32[3,32,256]{2,1,0:T(8,128)S(1)}, f32[3,32,256]{2,1,0:T(8,128)S(1)}, u32[]{:S(2)}, u32[]{:S(2)}) collective-permute-start(f32[3,32,256]{2,1,0:T(8,128)S(1)} %get-tuple-element.58.inner0_ref), channel_id=1, source_target_pairs={{0,128},{1,129},{2,130},{3,131},{4,132},{5,133},{6,134},{7,135},{8... | collective-permute-start | bytes 294920 | tf_op jit(solution)/shard_map/ppermute | solution.py:350
  27.9 1.6 %collective-permute-done.4.outer_ref = f32[3,32,256]{2,1,0:T(8,128)S(1)} collective-permute-done((f32[3,32,256]{2,1,0:T(8,128)S(1)}, f32[3,32,256]{2,1,0:T(8,128)S(1)}, u32[]{:S(2)}, u32[]{:S(2)}) %collective-permute-start.4) | collective-permute-done | bytes 98336 | tf_op jit(solution)/shard_map/ppermute | solution.py:351
  29.6 1.8 %collective-permute-start.7 = (f32[3,32,256]{2,1,0:T(8,128)S(1)}, f32[3,32,256]{2,1,0:T(8,128)S(1)}, u32[]{:S(2)}, u32[]{:S(2)}) collective-permute-start(f32[3,32,256]{2,1,0:T(8,128)S(1)} %collective-permute-done.4.outer_ref), channel_id=1, source_target_pairs={{0,15},{1,2},{2,1},{3,4},{4,3},{5,6},{6,5},{7,8},{8,7},{9,10},{10,... | collective-permute-start | bytes 294920 | tf_op jit(solution)/shard_map/ppermute | solution.py:279
  31.4 2.9 %tangent_near.6 = (f32[3,32,256]{2,1,0:T(8,128)S(1)}, f32[3,32,256]{2,1,0:T(8,128)S(1)}) custom-call(f32[3,32,256]{2,1,0:T(8,128)S(1)} %collective-permute-done.4.outer_ref, f32[3,32,256]{2,1,0:T(8,128)S(1)} %collective-permute-done.5.inner_ref, f32[3,32,256]{2,1,0:T(8,128)S(1)} %collective-permute-done.6.halo_ref, ...), custom_call_target="tpu_custom_call" | custom-call | flops 300000000 | bytes 100000 | tf_op jit(solution)/shard_map/tangent_near/pallas_call | solution.py:345
  35.4 2.0 %collective-permute-start.9 = (f32[3,32,256]{2,1,0:T(8,128)S(1)}, f32[3,32,256]{2,1,0:T(8,128)S(1)}, u32[]{:S(2)}, u32[]{:S(2)}) collective-permute-start(f32[3,32,256]{2,1,0:T(8,128)S(1)} %tangent_far.6.outer_ref), channel_id=1, source_target_pairs={{0,15},{1,2},{2,1},{3,4},{4,3},{5,6},{6,5},{7,8},{8,7},{9,10},{10,... | collective-permute-start | bytes 294920 | tf_op jit(solution)/shard_map/ppermute | solution.py:279
  37.4 2.9 %tangent_near.7 = (f32[3,32,256]{2,1,0:T(8,128)S(1)}, f32[3,32,256]{2,1,0:T(8,128)S(1)}) custom-call(f32[3,32,256]{2,1,0:T(8,128)S(1)} %tangent_far.6.outer_ref, f32[3,32,256]{2,1,0:T(8,128)S(1)} %get-tuple-element.60.inner_ref, f32[3,32,256]{2,1,0:T(8,128)S(1)} %collective-permute-done.8.halo_ref, bf16[42,256,256]{2,1,0:T(8,128)(2,1)S(1)} %get-tuple-element.53.high_ref, ...), custom_call_target="tpu_custom_call" | custom-call | flops 300000000 | bytes 100000 | tf_op jit(solution)/shard_map/tangent_near/pallas_call | solution.py:345
  43.7 1.8 %collective-permute-start.12 = (f32[3,32,256]{2,1,0:T(8,128)S(1)}, f32[3,32,256]{2,1,0:T(8,128)S(1)}, u32[]{:S(2)}, u32[]{:S(2)}) collective-permute-start(f32[3,32,256]{2,1,0:T(8,128)S(1)} %seen_outer.1), channel_id=1, source_target_pairs={{0,15},{1,2},{2,1},{3,4},{4,3},{5,6},{6,5},{7,8},{8,7},{9,10},{10,... | collective-permute-start | bytes 294920 | tf_op jit(solution)/shard_map/ppermute | solution.py:279
  45.6 1.3 %adjoint_local.4 = (f32[3,32,256]{2,1,0:T(8,128)S(1)}, f32[3,32,256]{2,1,0:T(8,128)S(1)}) custom-call(f32[3,32,256]{2,1,0:T(8,128)S(1)} %get-tuple-element.76.outer_ref.value_ref.total_ref, f32[3,32,256]{2,1,0:T(8,128)S(1)} %get-tuple-element.64.inner_ref.total_ref, bf16[42,256,256]{2,1,0:T(8,128)(2,1)S(1)} %get-tuple-element.53.high_ref, ...), custom_call_target="tpu_custom_call" | custom-call | flops 1000000000 | bytes 100000 | tf_op jit(solution)/shard_map/adjoint_local/pallas_call | solution.py:366
  49.6 1.6 %collective-permute-start.13 = (f32[3,32,256]{2,1,0:T(8,128)S(1)}, f32[3,32,256]{2,1,0:T(8,128)S(1)}, u32[]{:S(2)}, u32[]{:S(2)}) collective-permute-start(f32[3,32,256]{2,1,0:T(8,128)S(1)} %get-tuple-element.73), channel_id=1, source_target_pairs={{0,15},{1,2},{2,1},{3,4},{4,3},{5,6},{6,5},{7,8},{8,7},{9,10},{10,... | collective-permute-start | bytes 294920 | tf_op jit(solution)/shard_map/ppermute | solution.py:279
  51.2 1.3 %adjoint_local.5 = (f32[3,32,256]{2,1,0:T(8,128)S(1)}, f32[3,32,256]{2,1,0:T(8,128)S(1)}) custom-call(f32[3,32,256]{2,1,0:T(8,128)S(1)} %get-tuple-element.70.outer_ref, f32[3,32,256]{2,1,0:T(8,128)S(1)} %get-tuple-element.71.inner_ref, bf16[42,256,256]{2,1,0:T(8,128)(2,1)S(1)} %get-tuple-element.53.high_ref, bf16[42,256,256]{2,1,0:T(8,128)(2,1)S(1)} %get-tuple-element.54.low_ref), custom_call_target="tpu_custom_call" | custom-call | flops 1000000000 | bytes 100000 | tf_op jit(solution)/shard_map/adjoint_local/pallas_call | solution.py:372
  52.6 1.4 %collective-permute-start.23 = (f32[2,2,32,64]{3,2,1,0:T(8,128)S(1)}, f32[2,2,32,64]{3,2,1,0:T(8,128)S(1)}, u32[]{:S(2)}, u32[]{:S(2)}) collective-permute-start(f32[2,2,32,64]{3,2,1,0:T(8,128)S(1)} %pad_maximum_fusion.3), channel_id=1, source_target_pairs={{0,32},{16,48},{32,0},{48,16},{64,96},{80,112},{96,64},{112,80},{1... | collective-permute-start | bytes 98312 | tf_op jit(solution)/shard_map/ppermute | solution.py:273
  58.0 5.4 %collective-permute-done.14.halo_ref = f32[3,32,256]{2,1,0:T(8,128)S(1)} collective-permute-done((f32[3,32,256]{2,1,0:T(8,128)S(1)}, f32[3,32,256]{2,1,0:T(8,128)S(1)}, u32[]{:S(2)}, u32[]{:S(2)}) %collective-permute-start.14) | collective-permute-done | bytes 98336 | tf_op jit(solution)/shard_map/ppermute | solution.py:374
  64.9 1.4 %collective-permute-start.18 = (f32[3,32,256]{2,1,0:T(8,128)S(1)}, f32[3,32,256]{2,1,0:T(8,128)S(1)}, u32[]{:S(2)}, u32[]{:S(2)}) collective-permute-start(f32[3,32,256]{2,1,0:T(8,128)S(1)} %get-tuple-element.85), channel_id=1, source_target_pairs={{0,15},{1,2},{2,1},{3,4},{4,3},{5,6},{6,5},{7,8},{8,7},{9,10},{10,... | collective-permute-start | bytes 294920 | tf_op jit(solution)/shard_map/ppermute | solution.py:279
  66.2 1.3 %adjoint_local.6 = (f32[3,32,256]{2,1,0:T(8,128)S(1)}, f32[3,32,256]{2,1,0:T(8,128)S(1)}) custom-call(f32[3,32,256]{2,1,0:T(8,128)S(1)} %get-tuple-element.79.outer_ref, f32[3,32,256]{2,1,0:T(8,128)S(1)} %get-tuple-element.80.inner_ref, bf16[42,256,256]{2,1,0:T(8,128)(2,1)S(1)} %get-tuple-element.53.high_ref, bf16[42,256,256]{2,1,0:T(8,128)(2,1)S(1)} %get-tuple-element.54.low_ref), custom_call_target="tpu_custom_call" | custom-call | flops 1000000000 | bytes 100000 | tf_op jit(solution)/shard_map/adjoint_local/pallas_call | solution.py:385
  70.5 1.4 %collective-permute-start.19 = (f32[3,32,256]{2,1,0:T(8,128)S(1)}, f32[3,32,256]{2,1,0:T(8,128)S(1)}, u32[]{:S(2)}, u32[]{:S(2)}) collective-permute-start(f32[3,32,256]{2,1,0:T(8,128)S(1)} %get-tuple-element.91), channel_id=1, source_target_pairs={{0,15},{1,2},{2,1},{3,4},{4,3},{5,6},{6,5},{7,8},{8,7},{9,10},{10,... | collective-permute-start | bytes 294920 | tf_op jit(solution)/shard_map/ppermute | solution.py:279
  75.2 2.2 %collective-permute-done.26 = f32[32,256]{1,0:T(8,128)S(1)} collective-permute-done((f32[32,256]{1,0:T(8,128)S(1)}, f32[32,256]{1,0:T(8,128)S(1)}, u32[]{:S(2)}, u32[]{:S(2)}) %collective-permute-start.26) | collective-permute-done | bytes 32800 | tf_op jit(solution)/shard_map/ppermute | solution.py:273
  77.4 1.6 %collective-permute-start.27 = (f32[32,256]{1,0:T(8,128)S(1)}, f32[32,256]{1,0:T(8,128)S(1)}, u32[]{:S(2)}, u32[]{:S(2)}) collective-permute-start(f32[32,256]{1,0:T(8,128)S(1)} %add.26), channel_id=1, source_target_pairs={{0,12},{1,13},{2,14},{3,15},{4,8},{5,9},{6,10},{7,11},{8,4},{9,5},... | collective-permute-start | bytes 98312 | tf_op jit(solution)/shard_map/ppermute | solution.py:273
  79.1 1.5 %collective-permute-start.20 = (f32[6,32,128]{2,1,0:T(8,128)S(1)}, f32[6,32,128]{2,1,0:T(8,128)S(1)}, u32[]{:S(2)}, u32[]{:S(2)}) collective-permute-start(f32[6,32,128]{2,1,0:T(8,128)S(1)} %fusion), channel_id=1, source_target_pairs={{0,128},{1,129},{2,130},{3,131},{4,132},{5,133},{6,134},{7,135},{8... | collective-permute-start | bytes 294920 | tf_op jit(solution)/shard_map/ppermute | solution.py:396
  80.6 3.0 %collective-permute-done.27 = f32[32,256]{1,0:T(8,128)S(1)} collective-permute-done((f32[32,256]{1,0:T(8,128)S(1)}, f32[32,256]{1,0:T(8,128)S(1)}, u32[]{:S(2)}, u32[]{:S(2)}) %collective-permute-start.27) | collective-permute-done | bytes 32800 | tf_op jit(solution)/shard_map/ppermute | solution.py:273
  83.6 5.4 %collective-permute-done.28.rest_ref = f32[32,256]{1,0:T(8,128)S(1)} collective-permute-done((f32[32,256]{1,0:T(8,128)S(1)}, f32[32,256]{1,0:T(8,128)S(1)}, u32[]{:S(2)}, u32[]{:S(2)}) %collective-permute-start.28) | collective-permute-done | bytes 32800 | tf_op jit(solution)/shard_map/ppermute | solution.py:273
  (77 shorter events, 24.8 us)
Async XLA Ops:
  1.6 11.3 %collective-permute-start = (f32[3,32,256]{2,1,0:T(8,128)S(1)}, f32[3,32,256]{2,1,0:T(8,128)S(1)}, u32[]{:S(2)}, u32[]{:S(2)}) collective-permute-start(f32[3,32,256]{2,1,0:T(8,128)S(1)} %get-tuple-element.52.inner_ref), channel_id=1, source_target_pairs={{0,1},{1,0},{2,3},{3,2},{4,5},{5,4},{6,7},{7,6},{8,9},{9,8},{10,11... | collective-permute-start | bytes 294920 | tf_op jit(solution)/shard_map/ppermute | solution.py:273
  1.7 14.2 %collective-permute-start.1 = (f32[3,32,256]{2,1,0:T(8,128)S(1)}, f32[3,32,256]{2,1,0:T(8,128)S(1)}, u32[]{:S(2)}, u32[]{:S(2)}) collective-permute-start(f32[3,32,256]{2,1,0:T(8,128)S(1)} %get-tuple-element.51.outer_ref), channel_id=1, source_target_pairs={{0,15},{1,2},{2,1},{3,4},{4,3},{5,6},{6,5},{7,8},{8,7},{9,10},{10,... | collective-permute-start | bytes 294920 | tf_op jit(solution)/shard_map/ppermute | solution.py:279
  16.4 9.0 %collective-permute-start.3 = (f32[3,32,256]{2,1,0:T(8,128)S(1)}, f32[3,32,256]{2,1,0:T(8,128)S(1)}, u32[]{:S(2)}, u32[]{:S(2)}) collective-permute-start(f32[3,32,256]{2,1,0:T(8,128)S(1)} %tangent_far.4.outer_ref), channel_id=1, source_target_pairs={{0,15},{1,2},{2,1},{3,4},{4,3},{5,6},{6,5},{7,8},{8,7},{9,10},{10,... | collective-permute-start | bytes 294920 | tf_op jit(solution)/shard_map/ppermute | solution.py:279
  20.4 7.5 %collective-permute-start.5 = (f32[3,32,256]{2,1,0:T(8,128)S(1)}, f32[3,32,256]{2,1,0:T(8,128)S(1)}, u32[]{:S(2)}, u32[]{:S(2)}) collective-permute-start(f32[3,32,256]{2,1,0:T(8,128)S(1)} %get-tuple-element.58.inner0_ref), channel_id=1, source_target_pairs={{0,128},{1,129},{2,130},{3,131},{4,132},{5,133},{6,134},{7,135},{8... | collective-permute-start | bytes 294920 | tf_op jit(solution)/shard_map/ppermute | solution.py:350
  25.9 3.6 %collective-permute-start.4 = (f32[3,32,256]{2,1,0:T(8,128)S(1)}, f32[3,32,256]{2,1,0:T(8,128)S(1)}, u32[]{:S(2)}, u32[]{:S(2)}) collective-permute-start(f32[3,32,256]{2,1,0:T(8,128)S(1)} %tangent_far.5.outer0_ref), channel_id=1, source_target_pairs={{0,128},{1,129},{2,130},{3,131},{4,132},{5,133},{6,134},{7,135},{8... | collective-permute-start | bytes 294920 | tf_op jit(solution)/shard_map/ppermute | solution.py:351
  29.6 5.3 %collective-permute-start.7 = (f32[3,32,256]{2,1,0:T(8,128)S(1)}, f32[3,32,256]{2,1,0:T(8,128)S(1)}, u32[]{:S(2)}, u32[]{:S(2)}) collective-permute-start(f32[3,32,256]{2,1,0:T(8,128)S(1)} %collective-permute-done.4.outer_ref), channel_id=1, source_target_pairs={{0,15},{1,2},{2,1},{3,4},{4,3},{5,6},{6,5},{7,8},{8,7},{9,10},{10,... | collective-permute-start | bytes 294920 | tf_op jit(solution)/shard_map/ppermute | solution.py:279
  35.4 5.5 %collective-permute-start.9 = (f32[3,32,256]{2,1,0:T(8,128)S(1)}, f32[3,32,256]{2,1,0:T(8,128)S(1)}, u32[]{:S(2)}, u32[]{:S(2)}) collective-permute-start(f32[3,32,256]{2,1,0:T(8,128)S(1)} %tangent_far.6.outer_ref), channel_id=1, source_target_pairs={{0,15},{1,2},{2,1},{3,4},{4,3},{5,6},{6,5},{7,8},{8,7},{9,10},{10,... | collective-permute-start | bytes 294920 | tf_op jit(solution)/shard_map/ppermute | solution.py:279
  42.8 4.5 %collective-permute-start.21 = (f32[32,64]{1,0:T(8,128)S(1)}, f32[32,64]{1,0:T(8,128)S(1)}, u32[]{:S(2)}, u32[]{:S(2)}) collective-permute-start(f32[32,64]{1,0:T(8,128)S(1)} %get-tuple-element.92), channel_id=1, source_target_pairs={{0,1},{1,0},{2,3},{3,2},{4,5},{5,4},{6,7},{7,6},{8,9},{9,8},{10,11... | collective-permute-start | bytes 24584 | tf_op jit(solution)/shard_map/ppermute | solution.py:273
  42.9 4.1 %collective-permute-start.10 = (f32[3,32,256]{2,1,0:T(8,128)S(1)}, f32[3,32,256]{2,1,0:T(8,128)S(1)}, u32[]{:S(2)}, u32[]{:S(2)}) collective-permute-start(f32[3,32,256]{2,1,0:T(8,128)S(1)} %get-tuple-element.67), channel_id=1, source_target_pairs={{0,1},{1,0},{2,3},{3,2},{4,5},{5,4},{6,7},{7,6},{8,9},{9,8},{10,11... | collective-permute-start | bytes 294920 | tf_op jit(solution)/shard_map/ppermute | solution.py:273
  43.7 5.5 %collective-permute-start.12 = (f32[3,32,256]{2,1,0:T(8,128)S(1)}, f32[3,32,256]{2,1,0:T(8,128)S(1)}, u32[]{:S(2)}, u32[]{:S(2)}) collective-permute-start(f32[3,32,256]{2,1,0:T(8,128)S(1)} %seen_outer.1), channel_id=1, source_target_pairs={{0,15},{1,2},{2,1},{3,4},{4,3},{5,6},{6,5},{7,8},{8,7},{9,10},{10,... | collective-permute-start | bytes 294920 | tf_op jit(solution)/shard_map/ppermute | solution.py:279
  48.6 4.0 %collective-permute-start.22 = (f32[1,2,32,64]{3,2,1,0:T(8,128)S(1)}, f32[1,2,32,64]{3,2,1,0:T(8,128)S(1)}, u32[]{:S(2)}, u32[]{:S(2)}) collective-permute-start(f32[1,2,32,64]{3,2,1,0:T(8,128)S(1)} %maximum_bitcast_fusion), channel_id=1, source_target_pairs={{0,16},{16,0},{32,48},{48,32},{64,80},{80,64},{96,112},{112,96},{1... | collective-permute-start | bytes 49160 | tf_op jit(solution)/shard_map/ppermute | solution.py:273
  49.6 5.3 %collective-permute-start.13 = (f32[3,32,256]{2,1,0:T(8,128)S(1)}, f32[3,32,256]{2,1,0:T(8,128)S(1)}, u32[]{:S(2)}, u32[]{:S(2)}) collective-permute-start(f32[3,32,256]{2,1,0:T(8,128)S(1)} %get-tuple-element.73), channel_id=1, source_target_pairs={{0,15},{1,2},{2,1},{3,4},{4,3},{5,6},{6,5},{7,8},{8,7},{9,10},{10,... | collective-permute-start | bytes 294920 | tf_op jit(solution)/shard_map/ppermute | solution.py:279
  52.6 4.9 %collective-permute-start.23 = (f32[2,2,32,64]{3,2,1,0:T(8,128)S(1)}, f32[2,2,32,64]{3,2,1,0:T(8,128)S(1)}, u32[]{:S(2)}, u32[]{:S(2)}) collective-permute-start(f32[2,2,32,64]{3,2,1,0:T(8,128)S(1)} %pad_maximum_fusion.3), channel_id=1, source_target_pairs={{0,32},{16,48},{32,0},{48,16},{64,96},{80,112},{96,64},{112,80},{1... | collective-permute-start | bytes 98312 | tf_op jit(solution)/shard_map/ppermute | solution.py:273
  54.8 8.6 %collective-permute-start.14 = (f32[3,32,256]{2,1,0:T(8,128)S(1)}, f32[3,32,256]{2,1,0:T(8,128)S(1)}, u32[]{:S(2)}, u32[]{:S(2)}) collective-permute-start(f32[3,32,256]{2,1,0:T(8,128)S(1)} %add.21), channel_id=1, source_target_pairs={{128,0},{129,1},{130,2},{131,3},{132,4},{133,5},{134,6},{135,7},{1... | collective-permute-start | bytes 294920 | tf_op jit(solution)/shard_map/ppermute | solution.py:374
  56.2 8.3 %collective-permute-start.15 = (f32[3,32,256]{2,1,0:T(8,128)S(1)}, f32[3,32,256]{2,1,0:T(8,128)S(1)}, u32[]{:S(2)}, u32[]{:S(2)}) collective-permute-start(f32[3,32,256]{2,1,0:T(8,128)S(1)} %add.22), channel_id=1, source_target_pairs={{128,0},{129,1},{130,2},{131,3},{132,4},{133,5},{134,6},{135,7},{1... | collective-permute-start | bytes 294920 | tf_op jit(solution)/shard_map/ppermute | solution.py:377
  57.5 10.7 %collective-permute-start.24 = (f32[4,2,32,64]{3,2,1,0:T(8,128)S(1)}, f32[4,2,32,64]{3,2,1,0:T(8,128)S(1)}, u32[]{:S(2)}, u32[]{:S(2)}) collective-permute-start(f32[4,2,32,64]{3,2,1,0:T(8,128)S(1)} %pad_maximum_fusion.2), channel_id=1, source_target_pairs={{0,96},{16,112},{32,64},{48,80},{64,32},{80,48},{96,0},{112,16},{1... | collective-permute-start | bytes 196616 | tf_op jit(solution)/shard_map/ppermute | solution.py:273
  63.8 3.8 %collective-permute-start.16 = (f32[3,32,256]{2,1,0:T(8,128)S(1)}, f32[3,32,256]{2,1,0:T(8,128)S(1)}, u32[]{:S(2)}, u32[]{:S(2)}) collective-permute-start(f32[3,32,256]{2,1,0:T(8,128)S(1)} %get-tuple-element.75), channel_id=1, source_target_pairs={{0,1},{1,0},{2,3},{3,2},{4,5},{5,4},{6,7},{7,6},{8,9},{9,8},{10,11... | collective-permute-start | bytes 294920 | tf_op jit(solution)/shard_map/ppermute | solution.py:273
  64.9 5.3 %collective-permute-start.18 = (f32[3,32,256]{2,1,0:T(8,128)S(1)}, f32[3,32,256]{2,1,0:T(8,128)S(1)}, u32[]{:S(2)}, u32[]{:S(2)}) collective-permute-start(f32[3,32,256]{2,1,0:T(8,128)S(1)} %get-tuple-element.85), channel_id=1, source_target_pairs={{0,15},{1,2},{2,1},{3,4},{4,3},{5,6},{6,5},{7,8},{8,7},{9,10},{10,... | collective-permute-start | bytes 294920 | tf_op jit(solution)/shard_map/ppermute | solution.py:279
  68.6 4.0 %collective-permute-start.25 = (f32[32,256]{1,0:T(8,128)S(1)}, f32[32,256]{1,0:T(8,128)S(1)}, u32[]{:S(2)}, u32[]{:S(2)}) collective-permute-start(f32[32,256]{1,0:T(8,128)S(1)} %gram_part.1), channel_id=1, source_target_pairs={{0,2},{1,3},{2,0},{3,1},{4,6},{5,7},{6,4},{7,5},{8,10},{9,11},{10,... | collective-permute-start | bytes 98312 | tf_op jit(solution)/shard_map/ppermute | solution.py:273
  70.5 6.9 %collective-permute-start.19 = (f32[3,32,256]{2,1,0:T(8,128)S(1)}, f32[3,32,256]{2,1,0:T(8,128)S(1)}, u32[]{:S(2)}, u32[]{:S(2)}) collective-permute-start(f32[3,32,256]{2,1,0:T(8,128)S(1)} %get-tuple-element.91), channel_id=1, source_target_pairs={{0,15},{1,2},{2,1},{3,4},{4,3},{5,6},{6,5},{7,8},{8,7},{9,10},{10,... | collective-permute-start | bytes 294920 | tf_op jit(solution)/shard_map/ppermute | solution.py:279
  72.6 4.8 %collective-permute-start.26 = (f32[32,256]{1,0:T(8,128)S(1)}, f32[32,256]{1,0:T(8,128)S(1)}, u32[]{:S(2)}, u32[]{:S(2)}) collective-permute-start(f32[32,256]{1,0:T(8,128)S(1)} %add.25), channel_id=1, source_target_pairs={{0,4},{1,5},{2,6},{3,7},{4,0},{5,1},{6,2},{7,3},{8,12},{9,13},{10,... | collective-permute-start | bytes 98312 | tf_op jit(solution)/shard_map/ppermute | solution.py:273
  77.4 6.1 %collective-permute-start.27 = (f32[32,256]{1,0:T(8,128)S(1)}, f32[32,256]{1,0:T(8,128)S(1)}, u32[]{:S(2)}, u32[]{:S(2)}) collective-permute-start(f32[32,256]{1,0:T(8,128)S(1)} %add.26), channel_id=1, source_target_pairs={{0,12},{1,13},{2,14},{3,15},{4,8},{5,9},{6,10},{7,11},{8,4},{9,5},... | collective-permute-start | bytes 98312 | tf_op jit(solution)/shard_map/ppermute | solution.py:273
  79.1 9.9 %collective-permute-start.20 = (f32[6,32,128]{2,1,0:T(8,128)S(1)}, f32[6,32,128]{2,1,0:T(8,128)S(1)}, u32[]{:S(2)}, u32[]{:S(2)}) collective-permute-start(f32[6,32,128]{2,1,0:T(8,128)S(1)} %fusion), channel_id=1, source_target_pairs={{0,128},{1,129},{2,130},{3,131},{4,132},{5,133},{6,134},{7,135},{8... | collective-permute-start | bytes 294920 | tf_op jit(solution)/shard_map/ppermute | solution.py:396
  83.5 5.4 %collective-permute-start.28 = (f32[32,256]{1,0:T(8,128)S(1)}, f32[32,256]{1,0:T(8,128)S(1)}, u32[]{:S(2)}, u32[]{:S(2)}) collective-permute-start(f32[32,256]{1,0:T(8,128)S(1)} %add.27.gram_ref), channel_id=1, source_target_pairs={{0,128},{128,0},{1,129},{129,1},{2,130},{130,2},{3,131},{131,3},{4... | collective-permute-start | bytes 98312 | tf_op jit(solution)/shard_map/ppermute | solution.py:273
  (8 other events, 13.8 us)

commit v4 on v3

--- a/solution.py
+++ b/solution.py
@@ -111,6 +111,22 @@
         inner_ref[i] = field_ref[jnp.where(odd, elems - 1 - RADIUS - i, RADIUS + i)]
 
 
+def only(section, copies, body):
+    def guarded(*refs):
+        active = lax.axis_index("sec") == section
+
+        @pl.when(active)
+        def _():
+            body(*refs)
+
+        @pl.when(jnp.logical_not(active))
+        def _():
+            for source, target in copies:
+                refs[target][...] = refs[source][...]
+
+    return guarded
+
+
 def block(e, m):
     return e * NBRS + m - e + RADIUS
 
@@ -189,11 +205,17 @@
     local = stations_ref[...] - lax.axis_index("elem") * elems
     odd = odd_device()
     readings = jnp.zeros((cols, count), F32)
+    parts = []
     for u in range(elems):
         here = local == jnp.where(odd, elems - 1 - u, u)
         part = jnp.where(here, raw[u * cols : (u + 1) * cols], 0.0)
         readings += part
-        seen = lax.dot_general(part, weights, NN, precision=PRECISE, preferred_element_type=F32)
+        parts.append(part)
+    every = lax.dot_general(
+        jnp.concatenate(parts, axis=0), weights, NN, precision=PRECISE, preferred_element_type=F32
+    )
+    for u in range(elems):
+        seen = every[u * cols : (u + 1) * cols]
         if u < RADIUS:
             outer_out[u] = seen
         else:
@@ -306,28 +328,48 @@
         vmem=46 << 20, moved=2 * 10**7,
     )
     mirror = call(mirror_body, "mirror", (edge, edge), [IN_VMEM])
-    tangent_near = call(
-        tangent_near_body, "tangent_near", (edge, edge), [IN_VMEM] * 5, (pair(9),),
-    )
-    tangent_far = call(
-        tangent_far_body, "tangent_far", edge, [IN_VMEM] * 4, (pair(RADIUS),)
-    )
+    def make_tangent_near(body):
+        return call(
+            body, "tangent_near", (edge, edge), [IN_VMEM] * 5, (pair(9),),
+        )
+
+    tangent_near = make_tangent_near(tangent_near_body)
+    tangent_near_first = make_tangent_near(only(0, ((0, 5), (1, 6)), tangent_near_body))
+    def make_tangent_far(body):
+        return call(
+            body, "tangent_far", edge, [IN_VMEM] * 4, (pair(RADIUS),)
+        )
+
+    tangent_far = make_tangent_far(tangent_far_body)
+    tangent_far_first = make_tangent_far(only(0, ((0, 4),), tangent_far_body))
     observe = call(
         observe_body, "observe", (edge, edge, vmem((cols, count)), edge), [IN_VMEM] * 8,
         (pair(RADIUS), pltpu.VMEM((elems, cols, dofs), F32)),
     )
-    adjoint_local = call(
-        adjoint_local_body, "adjoint_local", (edge, edge), [IN_VMEM] * 4, (pair(elems),),
-    )
+    def make_adjoint_local(body):
+        return call(
+            body, "adjoint_local", (edge, edge), [IN_VMEM] * 4, (pair(elems),),
+        )
+
+    adjoint_local = make_adjoint_local(adjoint_local_body)
+    adjoint_local_last = make_adjoint_local(only(0, ((0, 4), (1, 5)), adjoint_local_body))
     seen_products = call(
         seen_outer_body, "seen_outer", edge, [IN_VMEM] * 3, (pair(RADIUS),)
     )
-    adjoint_outer = call(
-        adjoint_outer_body, "adjoint_outer", (edge, edge), [IN_VMEM] * 4, (pair(RADIUS),),
-    )
-    adjoint_inner = call(
-        adjoint_inner_body, "adjoint_inner", (edge, edge), [IN_VMEM] * 4, (pair(RADIUS),),
-    )
+    def make_adjoint_outer(body):
+        return call(
+            body, "adjoint_outer", (edge, edge), [IN_VMEM] * 4, (pair(RADIUS),),
+        )
+
+    adjoint_outer = make_adjoint_outer(adjoint_outer_body)
+    adjoint_outer_last = make_adjoint_outer(only(0, ((0, 4), (1, 5)), adjoint_outer_body))
+    def make_adjoint_inner(body):
+        return call(
+            body, "adjoint_inner", (edge, edge), [IN_VMEM] * 4, (pair(RADIUS),),
+        )
+
+    adjoint_inner = make_adjoint_inner(adjoint_inner_body)
+    adjoint_inner_last = make_adjoint_inner(only(0, ((0, 4), (1, 5)), adjoint_inner_body))
     finish = call(
         functools.partial(finish_body, 1.0 / (elem_total * dofs)), "finish",
         (
@@ -338,12 +380,12 @@
     )
     gram_part = call(gram_body, "gram_part", vmem((cols, cols * col_count)), [IN_VMEM])
 
-    def tangent(outer, inner, high, low):
+    def tangent(outer, inner, high, low, near, far):
         for _ in range(STEPS):
             inner_in = on_chip(inner)
             outer_in = off_chip(outer)
-            outer, inner = tangent_near(outer, inner, inner_in, high, low)
-            outer = tangent_far(outer, outer_in, high, low)
+            outer, inner = near(outer, inner, inner_in, high, low)
+            outer = far(outer, outer_in, high, low)
         return outer, inner
 
     def to_next(outer, inner):
@@ -351,8 +393,9 @@
         return lax.ppermute(outer, "sec", [(0, 1)]), inner
 
     high, low = prepare(neighbors, jacobian)
-    state0 = tangent(*mirror(jnp.transpose(probes, (1, 0, 2))), high, low)
-    state1 = tangent(*to_next(*state0), high, low)
+    start = mirror(jnp.transpose(probes, (1, 0, 2)))
+    state0 = tangent(*start, high, low, tangent_near_first, tangent_far_first)
+    state1 = tangent(*to_next(*state0), high, low, tangent_near, tangent_far)
     seen_outer, seen_inner, readings, inner_send = observe(
         *state0, *state1, stations.reshape(1, count), obs_weights, high, low
     )
@@ -376,19 +419,19 @@
     outer = after(outer, inner) + outer_in
     outer_back = lax.ppermute(outer, "sec", [(1, 0)])
     stack = gather(stack, 6, outer)
-    inner, inner_send = adjoint_inner(seen_inner, inner_back, high, low)
+    inner, inner_send = adjoint_inner_last(seen_inner, inner_back, high, low)
     inner_in = on_chip(inner_send)
     gram = gram_part(stack)
     gram = gram + swap(gram, "elem", 2)
-    outer, outer_send = adjoint_outer(after(seen_outer, inner_send), outer_back, high, low)
+    outer, outer_send = adjoint_outer_last(after(seen_outer, inner_send), outer_back, high, low)
     outer_in = off_chip(outer_send)
-    outer, inner = adjoint_local(outer, inner, high, low)
-    inner, inner_send = adjoint_inner(inner, inner_in, high, low)
+    outer, inner = adjoint_local_last(outer, inner, high, low)
+    inner, inner_send = adjoint_inner_last(inner, inner_in, high, low)
     inner_in = on_chip(inner_send)
     gram = gram + swap(after(gram, inner_in), "elem", 4)
-    outer, outer_send = adjoint_outer(after(outer, inner_in), outer_in, high, low)
+    outer, outer_send = adjoint_outer_last(after(outer, inner_in), outer_in, high, low)
     outer_in = off_chip(outer_send)
-    outer, inner = adjoint_local(outer, inner, high, low)
+    outer, inner = adjoint_local_last(outer, inner, high, low)
     inner = inner + inner_in
     gram = gram + swap(after(gram, outer_in), "elem", 12)
     outer = after(outer, inner) + outer_in

time: 89.9 us -> 87.3 us (0.971)
  starting transfers between devices: 34 us -> 30.5 us
  waiting for transfers between devices: 24.3 us -> 25.2 us
    ppermute x1, starting transfers between devices: 4.94 us -> 1.31 us  [to_next(): inner = lax.ppermute(inner, 'sec', [(0, 1)])]
    pallas_call x11 -> x15, Pallas kernels: 14.5 us -> 17.9 us  [the longest x4 11.5 us: tangent(): outer, inner = near(outer, inner, inner_in, high, low)]
    pallas_call x3 -> x1, Pallas kernels: 4.05 us -> 1.35 us  [per_device(): outer, inner = adjoint_local(outer, inner, high, low)]
  transfers between devices with their start and end apart: 29 -> 29, of which waited for: 14 -> 14; matrix products, arithmetic and copies ran while one was open for 0% -> 0% of each run, Pallas kernels for 30% -> 31%
where the time goes in v4:
time: 87.3 us; the launch traced here: 87.1 us
  starting transfers between devices  30.5 us (35%)
  Pallas kernels  29.1 us (33%)
  waiting for transfers between devices  25.2 us (29%)
  local copies, waits for them, and re-layouts  1.2 us (1%)
  between operations  0.92 us (1%)
    ppermute x8, starting transfers between devices, off_chip(): return lax.ppermute(value, 'elem', pairs)  16.6 us
    ppermute x16, waiting for transfers between devices, swap(): return lax.ppermute(value, axis, [(i, i ^ mask) for i in range(count)])  13.5 us
    pallas_call x4, Pallas kernels, tangent(): outer, inner = near(outer, inner, inner_in, high, low)  11.5 us
    ppermute x16, starting transfers between devices, swap(): return lax.ppermute(value, axis, [(i, i ^ mask) for i in range(count)])  7.4 us
    ppermute x1, waiting for transfers between devices, per_device(): inner_back = lax.ppermute(after(inner, outer_in), 'sec', [(1, 0)])  5.34 us
    pallas_call x1, Pallas kernels, per_device(): high, low = prepare(neighbors, jacobian)  5.24 us
    ppermute x8, waiting for transfers between devices, off_chip(): return lax.ppermute(value, 'elem', pairs)  3.23 us
    pallas_call x2, Pallas kernels, per_device(): outer, inner = adjoint_local_last(outer, inner, high, low)  2.7 us
  transfers between devices with their start and end apart: 29, of which 14 were waited for; matrix products, arithmetic and copies ran while one was open for 0% of the time, Pallas kernels for 31%

profile of v4, /device:TPU:16, one launch (start us, length us, event | category | flops | bytes accessed | tf_op | source)
XLA Modules:
  0.0 87.1 jit_solution(13575833331289404334)
XLA Ops:
  1.7 6.0 %collective-permute-start.1 = (f32[3,32,256]{2,1,0:T(8,128)S(1)}, f32[3,32,256]{2,1,0:T(8,128)S(1)}, u32[]{:S(2)}, u32[]{:S(2)}) collective-permute-start(f32[3,32,256]{2,1,0:T(8,128)S(1)} %get-tuple-element.51.refs_0_), channel_id=1, source_target_pairs={{0,15},{1,2},{2,1},{3,4},{4,3},{5,6},{6,5},{7,8},{8,7},{9,10},{10,... | collective-permute-start | bytes 294920 | tf_op jit(solution)/shard_map/ppermute | solution.py:301
  7.6 5.2 %prepare.1 = (bf16[42,256,256]{2,1,0:T(8,128)(2,1)S(1)}, bf16[42,256,256]{2,1,0:T(8,128)(2,1)S(1)}) custom-call(s32[6,7]{1,0:T(8,128)} %nbr_ref.1, f32[1,6,7,256,256]{4,3,2,1,0:T(8,128)} %jac_ref.1), custom_call_target="tpu_custom_call" | custom-call | flops 300000000 | bytes 20000000 | tf_op jit(solution)/shard_map/prepare/pallas_call | solution.py:395
  12.9 2.9 %tangent_near.4 = (f32[3,32,256]{2,1,0:T(8,128)S(1)}, f32[3,32,256]{2,1,0:T(8,128)S(1)}) custom-call(f32[3,32,256]{2,1,0:T(8,128)S(1)} %get-tuple-element.51.refs_0_, f32[3,32,256]{2,1,0:T(8,128)S(1)} %get-tuple-element.52.refs_1_, f32[3,32,256]{2,1,0:T(8,128)S(1)} %collective-permute-done.refs_2_, ...), custom_call_target="tpu_custom_call" | custom-call | flops 300000000 | bytes 100000 | tf_op jit(solution)/shard_map/tangent_near/pallas_call | solution.py:387
  17.6 2.9 %tangent_near.5 = (f32[3,32,256]{2,1,0:T(8,128)S(1)}, f32[3,32,256]{2,1,0:T(8,128)S(1)}) custom-call(f32[3,32,256]{2,1,0:T(8,128)S(1)} %tangent_far.4.refs_0_, f32[3,32,256]{2,1,0:T(8,128)S(1)} %get-tuple-element.56.refs_1_, f32[3,32,256]{2,1,0:T(8,128)S(1)} %collective-permute-done.2.refs_2_, ...), custom_call_target="tpu_custom_call" | custom-call | flops 300000000 | bytes 100000 | tf_op jit(solution)/shard_map/tangent_near/pallas_call | solution.py:387
  24.2 1.9 %collective-permute-done.4.outer_ref = f32[3,32,256]{2,1,0:T(8,128)S(1)} collective-permute-done((f32[3,32,256]{2,1,0:T(8,128)S(1)}, f32[3,32,256]{2,1,0:T(8,128)S(1)}, u32[]{:S(2)}, u32[]{:S(2)}) %collective-permute-start.4) | collective-permute-done | bytes 98336 | tf_op jit(solution)/shard_map/ppermute | solution.py:393
  26.1 1.7 %collective-permute-start.7 = (f32[3,32,256]{2,1,0:T(8,128)S(1)}, f32[3,32,256]{2,1,0:T(8,128)S(1)}, u32[]{:S(2)}, u32[]{:S(2)}) collective-permute-start(f32[3,32,256]{2,1,0:T(8,128)S(1)} %collective-permute-done.4.outer_ref), channel_id=1, source_target_pairs={{0,15},{1,2},{2,1},{3,4},{4,3},{5,6},{6,5},{7,8},{8,7},{9,10},{10,... | collective-permute-start | bytes 294920 | tf_op jit(solution)/shard_map/ppermute | solution.py:301
  27.8 2.9 %tangent_near.6 = (f32[3,32,256]{2,1,0:T(8,128)S(1)}, f32[3,32,256]{2,1,0:T(8,128)S(1)}) custom-call(f32[3,32,256]{2,1,0:T(8,128)S(1)} %collective-permute-done.4.outer_ref, f32[3,32,256]{2,1,0:T(8,128)S(1)} %collective-permute-done.5.inner_ref, f32[3,32,256]{2,1,0:T(8,128)S(1)} %collective-permute-done.6.halo_ref, ...), custom_call_target="tpu_custom_call" | custom-call | flops 300000000 | bytes 100000 | tf_op jit(solution)/shard_map/tangent_near/pallas_call | solution.py:387
  31.9 1.9 %collective-permute-start.9 = (f32[3,32,256]{2,1,0:T(8,128)S(1)}, f32[3,32,256]{2,1,0:T(8,128)S(1)}, u32[]{:S(2)}, u32[]{:S(2)}) collective-permute-start(f32[3,32,256]{2,1,0:T(8,128)S(1)} %tangent_far.6.outer_ref), channel_id=1, source_target_pairs={{0,15},{1,2},{2,1},{3,4},{4,3},{5,6},{6,5},{7,8},{8,7},{9,10},{10,... | collective-permute-start | bytes 294920 | tf_op jit(solution)/shard_map/ppermute | solution.py:301
  33.8 2.9 %tangent_near.7 = (f32[3,32,256]{2,1,0:T(8,128)S(1)}, f32[3,32,256]{2,1,0:T(8,128)S(1)}) custom-call(f32[3,32,256]{2,1,0:T(8,128)S(1)} %tangent_far.6.outer_ref, f32[3,32,256]{2,1,0:T(8,128)S(1)} %get-tuple-element.60.inner_ref, f32[3,32,256]{2,1,0:T(8,128)S(1)} %collective-permute-done.8.halo_ref, ...), custom_call_target="tpu_custom_call" | custom-call | flops 300000000 | bytes 100000 | tf_op jit(solution)/shard_map/tangent_near/pallas_call | solution.py:387
  40.2 1.7 %collective-permute-start.12 = (f32[3,32,256]{2,1,0:T(8,128)S(1)}, f32[3,32,256]{2,1,0:T(8,128)S(1)}, u32[]{:S(2)}, u32[]{:S(2)}) collective-permute-start(f32[3,32,256]{2,1,0:T(8,128)S(1)} %seen_outer.1), channel_id=1, source_target_pairs={{0,15},{1,2},{2,1},{3,4},{4,3},{5,6},{6,5},{7,8},{8,7},{9,10},{10,... | collective-permute-start | bytes 294920 | tf_op jit(solution)/shard_map/ppermute | solution.py:301
  42.0 1.3 %adjoint_local.4 = (f32[3,32,256]{2,1,0:T(8,128)S(1)}, f32[3,32,256]{2,1,0:T(8,128)S(1)}) custom-call(f32[3,32,256]{2,1,0:T(8,128)S(1)} %get-tuple-element.76.outer_ref.value_ref.refs_0_, f32[3,32,256]{2,1,0:T(8,128)S(1)} %get-tuple-element.64.inner_ref.refs_0_, bf16[42,256,256]{2,1,0:T(8,128)(2,1)S(1)} %get-tuple-element.53.refs_3_.refs_2_.high_ref, ...), custom_call_target="tpu_custom_call" | custom-call | flops 1000000000 | bytes 100000 | tf_op jit(solution)/shard_map/adjoint_local/pallas_call | solution.py:409
  45.0 1.5 %collective-permute-start.22 = (f32[1,2,32,64]{3,2,1,0:T(8,128)S(1)}, f32[1,2,32,64]{3,2,1,0:T(8,128)S(1)}, u32[]{:S(2)}, u32[]{:S(2)}) collective-permute-start(f32[1,2,32,64]{3,2,1,0:T(8,128)S(1)} %maximum_bitcast_fusion), channel_id=1, source_target_pairs={{0,16},{16,0},{32,48},{48,32},{64,80},{80,64},{96,112},{112,96},{1... | collective-permute-start | bytes 49160 | tf_op jit(solution)/shard_map/ppermute | solution.py:295
  47.8 1.3 %adjoint_local.5 = (f32[3,32,256]{2,1,0:T(8,128)S(1)}, f32[3,32,256]{2,1,0:T(8,128)S(1)}) custom-call(f32[3,32,256]{2,1,0:T(8,128)S(1)} %get-tuple-element.70.outer_ref, f32[3,32,256]{2,1,0:T(8,128)S(1)} %get-tuple-element.71.inner_ref, bf16[42,256,256]{2,1,0:T(8,128)(2,1)S(1)} %get-tuple-element.53.refs_3_.refs_2_.high_ref, ...), custom_call_target="tpu_custom_call" | custom-call | flops 1000000000 | bytes 100000 | tf_op jit(solution)/shard_map/adjoint_local/pallas_call | solution.py:415
  49.2 1.4 %collective-permute-start.23 = (f32[2,2,32,64]{3,2,1,0:T(8,128)S(1)}, f32[2,2,32,64]{3,2,1,0:T(8,128)S(1)}, u32[]{:S(2)}, u32[]{:S(2)}) collective-permute-start(f32[2,2,32,64]{3,2,1,0:T(8,128)S(1)} %pad_maximum_fusion.3), channel_id=1, source_target_pairs={{0,32},{16,48},{32,0},{48,16},{64,96},{80,112},{96,64},{112,80},{1... | collective-permute-start | bytes 98312 | tf_op jit(solution)/shard_map/ppermute | solution.py:295
  50.6 1.5 %collective-permute-done.13 = f32[3,32,256]{2,1,0:T(8,128)S(1)} collective-permute-done((f32[3,32,256]{2,1,0:T(8,128)S(1)}, f32[3,32,256]{2,1,0:T(8,128)S(1)}, u32[]{:S(2)}, u32[]{:S(2)}) %collective-permute-start.13) | collective-permute-done | bytes 98336 | tf_op jit(solution)/shard_map/ppermute | solution.py:301
  55.3 5.3 %collective-permute-done.14.refs_1_ = f32[3,32,256]{2,1,0:T(8,128)S(1)} collective-permute-done((f32[3,32,256]{2,1,0:T(8,128)S(1)}, f32[3,32,256]{2,1,0:T(8,128)S(1)}, u32[]{:S(2)}, u32[]{:S(2)}) %collective-permute-start.14) | collective-permute-done | bytes 98336 | tf_op jit(solution)/shard_map/ppermute | solution.py:417
  62.1 1.6 %collective-permute-start.18 = (f32[3,32,256]{2,1,0:T(8,128)S(1)}, f32[3,32,256]{2,1,0:T(8,128)S(1)}, u32[]{:S(2)}, u32[]{:S(2)}) collective-permute-start(f32[3,32,256]{2,1,0:T(8,128)S(1)} %get-tuple-element.85), channel_id=1, source_target_pairs={{0,15},{1,2},{2,1},{3,4},{4,3},{5,6},{6,5},{7,8},{8,7},{9,10},{10,... | collective-permute-start | bytes 294920 | tf_op jit(solution)/shard_map/ppermute | solution.py:301
  63.6 1.3 %adjoint_local.6 = (f32[3,32,256]{2,1,0:T(8,128)S(1)}, f32[3,32,256]{2,1,0:T(8,128)S(1)}) custom-call(f32[3,32,256]{2,1,0:T(8,128)S(1)} %get-tuple-element.79.refs_0_, f32[3,32,256]{2,1,0:T(8,128)S(1)} %get-tuple-element.80.refs_1_, bf16[42,256,256]{2,1,0:T(8,128)(2,1)S(1)} %get-tuple-element.53.refs_3_.refs_2_.high_ref, ...), custom_call_target="tpu_custom_call" | custom-call | flops 1000000000 | bytes 100000 | tf_op jit(solution)/shard_map/adjoint_local/pallas_call | solution.py:428
  67.7 1.6 %collective-permute-start.19 = (f32[3,32,256]{2,1,0:T(8,128)S(1)}, f32[3,32,256]{2,1,0:T(8,128)S(1)}, u32[]{:S(2)}, u32[]{:S(2)}) collective-permute-start(f32[3,32,256]{2,1,0:T(8,128)S(1)} %get-tuple-element.91), channel_id=1, source_target_pairs={{0,15},{1,2},{2,1},{3,4},{4,3},{5,6},{6,5},{7,8},{8,7},{9,10},{10,... | collective-permute-start | bytes 294920 | tf_op jit(solution)/shard_map/ppermute | solution.py:301
  71.2 1.3 %adjoint_local.7 = (f32[3,32,256]{2,1,0:T(8,128)S(1)}, f32[3,32,256]{2,1,0:T(8,128)S(1)}) custom-call(f32[3,32,256]{2,1,0:T(8,128)S(1)} %get-tuple-element.86.refs_0_, f32[3,32,256]{2,1,0:T(8,128)S(1)} %get-tuple-element.87.refs_1_, bf16[42,256,256]{2,1,0:T(8,128)(2,1)S(1)} %get-tuple-element.53.refs_3_.refs_2_.high_ref, ...), custom_call_target="tpu_custom_call" | custom-call | flops 1000000000 | bytes 100000 | tf_op jit(solution)/shard_map/adjoint_local/pallas_call | solution.py:434
  72.5 2.3 %collective-permute-done.26 = f32[32,256]{1,0:T(8,128)S(1)} collective-permute-done((f32[32,256]{1,0:T(8,128)S(1)}, f32[32,256]{1,0:T(8,128)S(1)}, u32[]{:S(2)}, u32[]{:S(2)}) %collective-permute-start.26) | collective-permute-done | bytes 32800 | tf_op jit(solution)/shard_map/ppermute | solution.py:295
  74.8 1.7 %collective-permute-start.27 = (f32[32,256]{1,0:T(8,128)S(1)}, f32[32,256]{1,0:T(8,128)S(1)}, u32[]{:S(2)}, u32[]{:S(2)}) collective-permute-start(f32[32,256]{1,0:T(8,128)S(1)} %add.26), channel_id=1, source_target_pairs={{0,12},{1,13},{2,14},{3,15},{4,8},{5,9},{6,10},{7,11},{8,4},{9,5},... | collective-permute-start | bytes 98312 | tf_op jit(solution)/shard_map/ppermute | solution.py:295
  77.9 3.1 %collective-permute-done.27 = f32[32,256]{1,0:T(8,128)S(1)} collective-permute-done((f32[32,256]{1,0:T(8,128)S(1)}, f32[32,256]{1,0:T(8,128)S(1)}, u32[]{:S(2)}, u32[]{:S(2)}) %collective-permute-start.27) | collective-permute-done | bytes 32800 | tf_op jit(solution)/shard_map/ppermute | solution.py:295
  81.0 5.4 %collective-permute-done.28.rest_ref = f32[32,256]{1,0:T(8,128)S(1)} collective-permute-done((f32[32,256]{1,0:T(8,128)S(1)}, f32[32,256]{1,0:T(8,128)S(1)}, u32[]{:S(2)}, u32[]{:S(2)}) %collective-permute-start.28) | collective-permute-done | bytes 32800 | tf_op jit(solution)/shard_map/ppermute | solution.py:295
  (77 shorter events, 25.5 us)
Async XLA Ops:
  1.6 11.3 %collective-permute-start = (f32[3,32,256]{2,1,0:T(8,128)S(1)}, f32[3,32,256]{2,1,0:T(8,128)S(1)}, u32[]{:S(2)}, u32[]{:S(2)}) collective-permute-start(f32[3,32,256]{2,1,0:T(8,128)S(1)} %get-tuple-element.52.refs_1_), channel_id=1, source_target_pairs={{0,1},{1,0},{2,3},{3,2},{4,5},{5,4},{6,7},{7,6},{8,9},{9,8},{10,11... | collective-permute-start | bytes 294920 | tf_op jit(solution)/shard_map/ppermute | solution.py:295
  1.7 14.2 %collective-permute-start.1 = (f32[3,32,256]{2,1,0:T(8,128)S(1)}, f32[3,32,256]{2,1,0:T(8,128)S(1)}, u32[]{:S(2)}, u32[]{:S(2)}) collective-permute-start(f32[3,32,256]{2,1,0:T(8,128)S(1)} %get-tuple-element.51.refs_0_), channel_id=1, source_target_pairs={{0,15},{1,2},{2,1},{3,4},{4,3},{5,6},{6,5},{7,8},{8,7},{9,10},{10,... | collective-permute-start | bytes 294920 | tf_op jit(solution)/shard_map/ppermute | solution.py:301
  16.4 5.3 %collective-permute-start.3 = (f32[3,32,256]{2,1,0:T(8,128)S(1)}, f32[3,32,256]{2,1,0:T(8,128)S(1)}, u32[]{:S(2)}, u32[]{:S(2)}) collective-permute-start(f32[3,32,256]{2,1,0:T(8,128)S(1)} %tangent_far.4.refs_0_), channel_id=1, source_target_pairs={{0,15},{1,2},{2,1},{3,4},{4,3},{5,6},{6,5},{7,8},{8,7},{9,10},{10,... | collective-permute-start | bytes 294920 | tf_op jit(solution)/shard_map/ppermute | solution.py:301
  20.4 3.7 %collective-permute-start.5 = (f32[3,32,256]{2,1,0:T(8,128)S(1)}, f32[3,32,256]{2,1,0:T(8,128)S(1)}, u32[]{:S(2)}, u32[]{:S(2)}) collective-permute-start(f32[3,32,256]{2,1,0:T(8,128)S(1)} %get-tuple-element.58.inner0_ref), channel_id=1, source_target_pairs={{0,128},{1,129},{2,130},{3,131},{4,132},{5,133},{6,134},{7,135},{8... | collective-permute-start | bytes 294920 | tf_op jit(solution)/shard_map/ppermute | solution.py:392
  22.3 3.7 %collective-permute-start.4 = (f32[3,32,256]{2,1,0:T(8,128)S(1)}, f32[3,32,256]{2,1,0:T(8,128)S(1)}, u32[]{:S(2)}, u32[]{:S(2)}) collective-permute-start(f32[3,32,256]{2,1,0:T(8,128)S(1)} %tangent_far.5.outer0_ref), channel_id=1, source_target_pairs={{0,128},{1,129},{2,130},{3,131},{4,132},{5,133},{6,134},{7,135},{8... | collective-permute-start | bytes 294920 | tf_op jit(solution)/shard_map/ppermute | solution.py:393
  26.1 5.3 %collective-permute-start.7 = (f32[3,32,256]{2,1,0:T(8,128)S(1)}, f32[3,32,256]{2,1,0:T(8,128)S(1)}, u32[]{:S(2)}, u32[]{:S(2)}) collective-permute-start(f32[3,32,256]{2,1,0:T(8,128)S(1)} %collective-permute-done.4.outer_ref), channel_id=1, source_target_pairs={{0,15},{1,2},{2,1},{3,4},{4,3},{5,6},{6,5},{7,8},{8,7},{9,10},{10,... | collective-permute-start | bytes 294920 | tf_op jit(solution)/shard_map/ppermute | solution.py:301
  31.9 5.5 %collective-permute-start.9 = (f32[3,32,256]{2,1,0:T(8,128)S(1)}, f32[3,32,256]{2,1,0:T(8,128)S(1)}, u32[]{:S(2)}, u32[]{:S(2)}) collective-permute-start(f32[3,32,256]{2,1,0:T(8,128)S(1)} %tangent_far.6.outer_ref), channel_id=1, source_target_pairs={{0,15},{1,2},{2,1},{3,4},{4,3},{5,6},{6,5},{7,8},{8,7},{9,10},{10,... | collective-permute-start | bytes 294920 | tf_op jit(solution)/shard_map/ppermute | solution.py:301
  39.3 4.3 %collective-permute-start.21 = (f32[32,64]{1,0:T(8,128)S(1)}, f32[32,64]{1,0:T(8,128)S(1)}, u32[]{:S(2)}, u32[]{:S(2)}) collective-permute-start(f32[32,64]{1,0:T(8,128)S(1)} %get-tuple-element.92), channel_id=1, source_target_pairs={{0,1},{1,0},{2,3},{3,2},{4,5},{5,4},{6,7},{7,6},{8,9},{9,8},{10,11... | collective-permute-start | bytes 24584 | tf_op jit(solution)/shard_map/ppermute | solution.py:295
  39.3 4.0 %collective-permute-start.10 = (f32[3,32,256]{2,1,0:T(8,128)S(1)}, f32[3,32,256]{2,1,0:T(8,128)S(1)}, u32[]{:S(2)}, u32[]{:S(2)}) collective-permute-start(f32[3,32,256]{2,1,0:T(8,128)S(1)} %get-tuple-element.67), channel_id=1, source_target_pairs={{0,1},{1,0},{2,3},{3,2},{4,5},{5,4},{6,7},{7,6},{8,9},{9,8},{10,11... | collective-permute-start | bytes 294920 | tf_op jit(solution)/shard_map/ppermute | solution.py:295
  40.2 6.3 %collective-permute-start.12 = (f32[3,32,256]{2,1,0:T(8,128)S(1)}, f32[3,32,256]{2,1,0:T(8,128)S(1)}, u32[]{:S(2)}, u32[]{:S(2)}) collective-permute-start(f32[3,32,256]{2,1,0:T(8,128)S(1)} %seen_outer.1), channel_id=1, source_target_pairs={{0,15},{1,2},{2,1},{3,4},{4,3},{5,6},{6,5},{7,8},{8,7},{9,10},{10,... | collective-permute-start | bytes 294920 | tf_op jit(solution)/shard_map/ppermute | solution.py:301
  45.0 4.2 %collective-permute-start.22 = (f32[1,2,32,64]{3,2,1,0:T(8,128)S(1)}, f32[1,2,32,64]{3,2,1,0:T(8,128)S(1)}, u32[]{:S(2)}, u32[]{:S(2)}) collective-permute-start(f32[1,2,32,64]{3,2,1,0:T(8,128)S(1)} %maximum_bitcast_fusion), channel_id=1, source_target_pairs={{0,16},{16,0},{32,48},{48,32},{64,80},{80,64},{96,112},{112,96},{1... | collective-permute-start | bytes 49160 | tf_op jit(solution)/shard_map/ppermute | solution.py:295
  46.8 5.3 %collective-permute-start.13 = (f32[3,32,256]{2,1,0:T(8,128)S(1)}, f32[3,32,256]{2,1,0:T(8,128)S(1)}, u32[]{:S(2)}, u32[]{:S(2)}) collective-permute-start(f32[3,32,256]{2,1,0:T(8,128)S(1)} %get-tuple-element.73), channel_id=1, source_target_pairs={{0,15},{1,2},{2,1},{3,4},{4,3},{5,6},{6,5},{7,8},{8,7},{9,10},{10,... | collective-permute-start | bytes 294920 | tf_op jit(solution)/shard_map/ppermute | solution.py:301
  49.2 5.5 %collective-permute-start.23 = (f32[2,2,32,64]{3,2,1,0:T(8,128)S(1)}, f32[2,2,32,64]{3,2,1,0:T(8,128)S(1)}, u32[]{:S(2)}, u32[]{:S(2)}) collective-permute-start(f32[2,2,32,64]{3,2,1,0:T(8,128)S(1)} %pad_maximum_fusion.3), channel_id=1, source_target_pairs={{0,32},{16,48},{32,0},{48,16},{64,96},{80,112},{96,64},{112,80},{1... | collective-permute-start | bytes 98312 | tf_op jit(solution)/shard_map/ppermute | solution.py:295
  52.1 8.5 %collective-permute-start.14 = (f32[3,32,256]{2,1,0:T(8,128)S(1)}, f32[3,32,256]{2,1,0:T(8,128)S(1)}, u32[]{:S(2)}, u32[]{:S(2)}) collective-permute-start(f32[3,32,256]{2,1,0:T(8,128)S(1)} %add.21), channel_id=1, source_target_pairs={{128,0},{129,1},{130,2},{131,3},{132,4},{133,5},{134,6},{135,7},{1... | collective-permute-start | bytes 294920 | tf_op jit(solution)/shard_map/ppermute | solution.py:417
  53.4 8.3 %collective-permute-start.15 = (f32[3,32,256]{2,1,0:T(8,128)S(1)}, f32[3,32,256]{2,1,0:T(8,128)S(1)}, u32[]{:S(2)}, u32[]{:S(2)}) collective-permute-start(f32[3,32,256]{2,1,0:T(8,128)S(1)} %add.22), channel_id=1, source_target_pairs={{128,0},{129,1},{130,2},{131,3},{132,4},{133,5},{134,6},{135,7},{1... | collective-permute-start | bytes 294920 | tf_op jit(solution)/shard_map/ppermute | solution.py:420
  54.8 10.8 %collective-permute-start.24 = (f32[4,2,32,64]{3,2,1,0:T(8,128)S(1)}, f32[4,2,32,64]{3,2,1,0:T(8,128)S(1)}, u32[]{:S(2)}, u32[]{:S(2)}) collective-permute-start(f32[4,2,32,64]{3,2,1,0:T(8,128)S(1)} %pad_maximum_fusion.2), channel_id=1, source_target_pairs={{0,96},{16,112},{32,64},{48,80},{64,32},{80,48},{96,0},{112,16},{1... | collective-permute-start | bytes 196616 | tf_op jit(solution)/shard_map/ppermute | solution.py:295
  61.0 4.0 %collective-permute-start.16 = (f32[3,32,256]{2,1,0:T(8,128)S(1)}, f32[3,32,256]{2,1,0:T(8,128)S(1)}, u32[]{:S(2)}, u32[]{:S(2)}) collective-permute-start(f32[3,32,256]{2,1,0:T(8,128)S(1)} %get-tuple-element.75), channel_id=1, source_target_pairs={{0,1},{1,0},{2,3},{3,2},{4,5},{5,4},{6,7},{7,6},{8,9},{9,8},{10,11... | collective-permute-start | bytes 294920 | tf_op jit(solution)/shard_map/ppermute | solution.py:295
  62.1 5.3 %collective-permute-start.18 = (f32[3,32,256]{2,1,0:T(8,128)S(1)}, f32[3,32,256]{2,1,0:T(8,128)S(1)}, u32[]{:S(2)}, u32[]{:S(2)}) collective-permute-start(f32[3,32,256]{2,1,0:T(8,128)S(1)} %get-tuple-element.85), channel_id=1, source_target_pairs={{0,15},{1,2},{2,1},{3,4},{4,3},{5,6},{6,5},{7,8},{8,7},{9,10},{10,... | collective-permute-start | bytes 294920 | tf_op jit(solution)/shard_map/ppermute | solution.py:301
  66.0 4.0 %collective-permute-start.25 = (f32[32,256]{1,0:T(8,128)S(1)}, f32[32,256]{1,0:T(8,128)S(1)}, u32[]{:S(2)}, u32[]{:S(2)}) collective-permute-start(f32[32,256]{1,0:T(8,128)S(1)} %gram_part.1), channel_id=1, source_target_pairs={{0,2},{1,3},{2,0},{3,1},{4,6},{5,7},{6,4},{7,5},{8,10},{9,11},{10,... | collective-permute-start | bytes 98312 | tf_op jit(solution)/shard_map/ppermute | solution.py:295
  67.7 7.1 %collective-permute-start.19 = (f32[3,32,256]{2,1,0:T(8,128)S(1)}, f32[3,32,256]{2,1,0:T(8,128)S(1)}, u32[]{:S(2)}, u32[]{:S(2)}) collective-permute-start(f32[3,32,256]{2,1,0:T(8,128)S(1)} %get-tuple-element.91), channel_id=1, source_target_pairs={{0,15},{1,2},{2,1},{3,4},{4,3},{5,6},{6,5},{7,8},{8,7},{9,10},{10,... | collective-permute-start | bytes 294920 | tf_op jit(solution)/shard_map/ppermute | solution.py:301
  70.0 4.8 %collective-permute-start.26 = (f32[32,256]{1,0:T(8,128)S(1)}, f32[32,256]{1,0:T(8,128)S(1)}, u32[]{:S(2)}, u32[]{:S(2)}) collective-permute-start(f32[32,256]{1,0:T(8,128)S(1)} %add.25), channel_id=1, source_target_pairs={{0,4},{1,5},{2,6},{3,7},{4,0},{5,1},{6,2},{7,3},{8,12},{9,13},{10,... | collective-permute-start | bytes 98312 | tf_op jit(solution)/shard_map/ppermute | solution.py:295
  74.8 6.1 %collective-permute-start.27 = (f32[32,256]{1,0:T(8,128)S(1)}, f32[32,256]{1,0:T(8,128)S(1)}, u32[]{:S(2)}, u32[]{:S(2)}) collective-permute-start(f32[32,256]{1,0:T(8,128)S(1)} %add.26), channel_id=1, source_target_pairs={{0,12},{1,13},{2,14},{3,15},{4,8},{5,9},{6,10},{7,11},{8,4},{9,5},... | collective-permute-start | bytes 98312 | tf_op jit(solution)/shard_map/ppermute | solution.py:295
  76.6 9.8 %collective-permute-start.20 = (f32[6,32,128]{2,1,0:T(8,128)S(1)}, f32[6,32,128]{2,1,0:T(8,128)S(1)}, u32[]{:S(2)}, u32[]{:S(2)}) collective-permute-start(f32[6,32,128]{2,1,0:T(8,128)S(1)} %fusion), channel_id=1, source_target_pairs={{0,128},{1,129},{2,130},{3,131},{4,132},{5,133},{6,134},{7,135},{8... | collective-permute-start | bytes 294920 | tf_op jit(solution)/shard_map/ppermute | solution.py:439
  81.0 5.4 %collective-permute-start.28 = (f32[32,256]{1,0:T(8,128)S(1)}, f32[32,256]{1,0:T(8,128)S(1)}, u32[]{:S(2)}, u32[]{:S(2)}) collective-permute-start(f32[32,256]{1,0:T(8,128)S(1)} %add.27.gram_ref), channel_id=1, source_target_pairs={{0,128},{128,0},{1,129},{129,1},{2,130},{130,2},{3,131},{131,3},{4... | collective-permute-start | bytes 98312 | tf_op jit(solution)/shard_map/ppermute | solution.py:295
  (8 other events, 14.0 us)

commit v5 on v4

--- a/solution.py
+++ b/solution.py
@@ -333,14 +333,14 @@
             body, "tangent_near", (edge, edge), [IN_VMEM] * 5, (pair(9),),
         )
 
-    tangent_near = make_tangent_near(tangent_near_body)
+    tangent_near = make_tangent_near(only(1, ((0, 5), (1, 6)), tangent_near_body))
     tangent_near_first = make_tangent_near(only(0, ((0, 5), (1, 6)), tangent_near_body))
     def make_tangent_far(body):
         return call(
             body, "tangent_far", edge, [IN_VMEM] * 4, (pair(RADIUS),)
         )
 
-    tangent_far = make_tangent_far(tangent_far_body)
+    tangent_far = make_tangent_far(only(1, ((0, 4),), tangent_far_body))
     tangent_far_first = make_tangent_far(only(0, ((0, 4),), tangent_far_body))
     observe = call(
         observe_body, "observe", (edge, edge, vmem((cols, count)), edge), [IN_VMEM] * 8,
@@ -351,7 +351,7 @@
             body, "adjoint_local", (edge, edge), [IN_VMEM] * 4, (pair(elems),),
         )
 
-    adjoint_local = make_adjoint_local(adjoint_local_body)
+    adjoint_local = make_adjoint_local(only(1, ((0, 4), (1, 5)), adjoint_local_body))
     adjoint_local_last = make_adjoint_local(only(0, ((0, 4), (1, 5)), adjoint_local_body))
     seen_products = call(
         seen_outer_body, "seen_outer", edge, [IN_VMEM] * 3, (pair(RADIUS),)
@@ -361,14 +361,14 @@
             body, "adjoint_outer", (edge, edge), [IN_VMEM] * 4, (pair(RADIUS),),
         )
 
-    adjoint_outer = make_adjoint_outer(adjoint_outer_body)
+    adjoint_outer = make_adjoint_outer(only(1, ((0, 4), (1, 5)), adjoint_outer_body))
     adjoint_outer_last = make_adjoint_outer(only(0, ((0, 4), (1, 5)), adjoint_outer_body))
     def make_adjoint_inner(body):
         return call(
             body, "adjoint_inner", (edge, edge), [IN_VMEM] * 4, (pair(RADIUS),),
         )
 
-    adjoint_inner = make_adjoint_inner(adjoint_inner_body)
+    adjoint_inner = make_adjoint_inner(only(1, ((0, 4), (1, 5)), adjoint_inner_body))
     adjoint_inner_last = make_adjoint_inner(only(0, ((0, 4), (1, 5)), adjoint_inner_body))
     finish = call(
         functools.partial(finish_body, 1.0 / (elem_total * dofs)), "finish",

time: 87.3 us -> 87.2 us (level)
  Pallas kernels: 29.1 us -> 19 us
  waiting for transfers between devices: 25.2 us -> 33.8 us
    ppermute x8, waiting for transfers between devices: 3.23 us -> 10.1 us  [off_chip(): return lax.ppermute(value, 'elem', pairs)]
    pallas_call x4, Pallas kernels: 11.5 us -> 5.79 us  [tangent(): outer, inner = near(outer, inner, inner_in, high, low)]
    ppermute x1, waiting for transfers between devices: 5.34 us -> 7.12 us  [per_device(): inner_back = lax.ppermute(after(inner, outer_in), 'sec', [(1, 0)])]
    pallas_call x1, Pallas kernels: 1.35 us -> 0.01 us  [per_device(): outer, inner = adjoint_local(outer, inner, high, low)]
    pallas_call x1, Pallas kernels: 1.35 us -> 0.01 us  [per_device(): outer, inner = adjoint_local(seen_outer, seen_inner, high, low)]
    pallas_call x4, Pallas kernels: 2.26 us -> 1.16 us  [tangent(): outer = far(outer, outer_in, high, low)]
  transfers between devices with their start and end apart: 29 -> 29, of which waited for: 14 -> 15; matrix products, arithmetic and copies ran while one was open for 0% -> 0% of each run, Pallas kernels for 31% -> 20%
where the time goes in v5:
time: 87.2 us; the launch traced here: 86.9 us
  waiting for transfers between devices  33.8 us (39%)
  starting transfers between devices  31.3 us (36%)
  Pallas kernels  19 us (22%)
  local copies, waits for them, and re-layouts  1.75 us (2%)
  between operations  0.96 us (1%)
    ppermute x8, starting transfers between devices, off_chip(): return lax.ppermute(value, 'elem', pairs)  17.3 us
    ppermute x16, waiting for transfers between devices, swap(): return lax.ppermute(value, axis, [(i, i ^ mask) for i in range(count)])  13.5 us
    ppermute x8, waiting for transfers between devices, off_chip(): return lax.ppermute(value, 'elem', pairs)  10.1 us
    ppermute x16, starting transfers between devices, swap(): return lax.ppermute(value, axis, [(i, i ^ mask) for i in range(count)])  7.51 us
    ppermute x1, waiting for transfers between devices, per_device(): inner_back = lax.ppermute(after(inner, outer_in), 'sec', [(1, 0)])  7.12 us
    pallas_call x4, Pallas kernels, tangent(): outer, inner = near(outer, inner, inner_in, high, low)  5.79 us
    pallas_call x1, Pallas kernels, per_device(): high, low = prepare(neighbors, jacobian)  5.24 us
    pallas_call x2, Pallas kernels, per_device(): outer, inner = adjoint_local_last(outer, inner, high, low)  2.7 us
  transfers between devices with their start and end apart: 29, of which 15 were waited for; matrix products, arithmetic and copies ran while one was open for 0% of the time, Pallas kernels for 20%

profile of v5, /device:TPU:16, one launch (start us, length us, event | category | flops | bytes accessed | tf_op | source)
XLA Modules:
  0.0 86.9 jit_solution(10659426633532730421)
XLA Ops:
  1.7 6.0 %collective-permute-start.1 = (f32[3,32,256]{2,1,0:T(8,128)S(1)}, f32[3,32,256]{2,1,0:T(8,128)S(1)}, u32[]{:S(2)}, u32[]{:S(2)}) collective-permute-start(f32[3,32,256]{2,1,0:T(8,128)S(1)} %get-tuple-element.51.refs_0_), channel_id=1, source_target_pairs={{0,15},{1,2},{2,1},{3,4},{4,3},{5,6},{6,5},{7,8},{8,7},{9,10},{10,... | collective-permute-start | bytes 294920 | tf_op jit(solution)/shard_map/ppermute | solution.py:301
  7.6 5.2 %prepare.1 = (bf16[42,256,256]{2,1,0:T(8,128)(2,1)S(1)}, bf16[42,256,256]{2,1,0:T(8,128)(2,1)S(1)}) custom-call(s32[6,7]{1,0:T(8,128)} %nbr_ref.1, f32[1,6,7,256,256]{4,3,2,1,0:T(8,128)} %jac_ref.1), custom_call_target="tpu_custom_call" | custom-call | flops 300000000 | bytes 20000000 | tf_op jit(solution)/shard_map/prepare/pallas_call | solution.py:395
  12.9 2.9 %tangent_near.4 = (f32[3,32,256]{2,1,0:T(8,128)S(1)}, f32[3,32,256]{2,1,0:T(8,128)S(1)}) custom-call(f32[3,32,256]{2,1,0:T(8,128)S(1)} %get-tuple-element.51.refs_0_, f32[3,32,256]{2,1,0:T(8,128)S(1)} %get-tuple-element.52.refs_1_, f32[3,32,256]{2,1,0:T(8,128)S(1)} %collective-permute-done.refs_2_, ...), custom_call_target="tpu_custom_call" | custom-call | flops 300000000 | bytes 100000 | tf_op jit(solution)/shard_map/tangent_near/pallas_call | solution.py:387
  17.6 2.9 %tangent_near.5 = (f32[3,32,256]{2,1,0:T(8,128)S(1)}, f32[3,32,256]{2,1,0:T(8,128)S(1)}) custom-call(f32[3,32,256]{2,1,0:T(8,128)S(1)} %tangent_far.4.refs_0_, f32[3,32,256]{2,1,0:T(8,128)S(1)} %get-tuple-element.56.refs_1_, f32[3,32,256]{2,1,0:T(8,128)S(1)} %collective-permute-done.2.refs_2_, ...), custom_call_target="tpu_custom_call" | custom-call | flops 300000000 | bytes 100000 | tf_op jit(solution)/shard_map/tangent_near/pallas_call | solution.py:387
  20.4 1.3 %collective-permute-start.5 = (f32[3,32,256]{2,1,0:T(8,128)S(1)}, f32[3,32,256]{2,1,0:T(8,128)S(1)}, u32[]{:S(2)}, u32[]{:S(2)}) collective-permute-start(f32[3,32,256]{2,1,0:T(8,128)S(1)} %get-tuple-element.58.inner0_ref), channel_id=1, source_target_pairs={{0,128},{1,129},{2,130},{3,131},{4,132},{5,133},{6,134},{7,135},{8... | collective-permute-start | bytes 294920 | tf_op jit(solution)/shard_map/ppermute | solution.py:392
  24.2 1.9 %collective-permute-done.4.refs_0_ = f32[3,32,256]{2,1,0:T(8,128)S(1)} collective-permute-done((f32[3,32,256]{2,1,0:T(8,128)S(1)}, f32[3,32,256]{2,1,0:T(8,128)S(1)}, u32[]{:S(2)}, u32[]{:S(2)}) %collective-permute-start.4) | collective-permute-done | bytes 98336 | tf_op jit(solution)/shard_map/ppermute | solution.py:393
  26.1 1.7 %collective-permute-start.7 = (f32[3,32,256]{2,1,0:T(8,128)S(1)}, f32[3,32,256]{2,1,0:T(8,128)S(1)}, u32[]{:S(2)}, u32[]{:S(2)}) collective-permute-start(f32[3,32,256]{2,1,0:T(8,128)S(1)} %collective-permute-done.4.refs_0_), channel_id=1, source_target_pairs={{0,15},{1,2},{2,1},{3,4},{4,3},{5,6},{6,5},{7,8},{8,7},{9,10},{10,... | collective-permute-start | bytes 294920 | tf_op jit(solution)/shard_map/ppermute | solution.py:301
  27.9 3.4 %collective-permute-done.7.refs_1_ = f32[3,32,256]{2,1,0:T(8,128)S(1)} collective-permute-done((f32[3,32,256]{2,1,0:T(8,128)S(1)}, f32[3,32,256]{2,1,0:T(8,128)S(1)}, u32[]{:S(2)}, u32[]{:S(2)}) %collective-permute-start.7) | collective-permute-done | bytes 98336 | tf_op jit(solution)/shard_map/ppermute | solution.py:301
  31.3 1.8 %collective-permute-start.9 = (f32[3,32,256]{2,1,0:T(8,128)S(1)}, f32[3,32,256]{2,1,0:T(8,128)S(1)}, u32[]{:S(2)}, u32[]{:S(2)}) collective-permute-start(f32[3,32,256]{2,1,0:T(8,128)S(1)} %tangent_far.6.refs_0_), channel_id=1, source_target_pairs={{0,15},{1,2},{2,1},{3,4},{4,3},{5,6},{6,5},{7,8},{8,7},{9,10},{10,... | collective-permute-start | bytes 294920 | tf_op jit(solution)/shard_map/ppermute | solution.py:301
  33.1 3.5 %collective-permute-done.9.refs_1_ = f32[3,32,256]{2,1,0:T(8,128)S(1)} collective-permute-done((f32[3,32,256]{2,1,0:T(8,128)S(1)}, f32[3,32,256]{2,1,0:T(8,128)S(1)}, u32[]{:S(2)}, u32[]{:S(2)}) %collective-permute-start.9) | collective-permute-done | bytes 98336 | tf_op jit(solution)/shard_map/ppermute | solution.py:301
  39.5 1.7 %collective-permute-start.12 = (f32[3,32,256]{2,1,0:T(8,128)S(1)}, f32[3,32,256]{2,1,0:T(8,128)S(1)}, u32[]{:S(2)}, u32[]{:S(2)}) collective-permute-start(f32[3,32,256]{2,1,0:T(8,128)S(1)} %seen_outer.1), channel_id=1, source_target_pairs={{0,15},{1,2},{2,1},{3,4},{4,3},{5,6},{6,5},{7,8},{8,7},{9,10},{10,... | collective-permute-start | bytes 294920 | tf_op jit(solution)/shard_map/ppermute | solution.py:301
  42.7 1.5 %collective-permute-start.22 = (f32[1,2,32,64]{3,2,1,0:T(8,128)S(1)}, f32[1,2,32,64]{3,2,1,0:T(8,128)S(1)}, u32[]{:S(2)}, u32[]{:S(2)}) collective-permute-start(f32[1,2,32,64]{3,2,1,0:T(8,128)S(1)} %maximum_bitcast_fusion), channel_id=1, source_target_pairs={{0,16},{16,0},{32,48},{48,32},{64,80},{80,64},{96,112},{112,96},{1... | collective-permute-start | bytes 49160 | tf_op jit(solution)/shard_map/ppermute | solution.py:295
  44.8 1.8 %collective-permute-start.13 = (f32[3,32,256]{2,1,0:T(8,128)S(1)}, f32[3,32,256]{2,1,0:T(8,128)S(1)}, u32[]{:S(2)}, u32[]{:S(2)}) collective-permute-start(f32[3,32,256]{2,1,0:T(8,128)S(1)} %get-tuple-element.73), channel_id=1, source_target_pairs={{0,15},{1,2},{2,1},{3,4},{4,3},{5,6},{6,5},{7,8},{8,7},{9,10},{10,... | collective-permute-start | bytes 294920 | tf_op jit(solution)/shard_map/ppermute | solution.py:301
  46.7 1.4 %collective-permute-start.23 = (f32[2,2,32,64]{3,2,1,0:T(8,128)S(1)}, f32[2,2,32,64]{3,2,1,0:T(8,128)S(1)}, u32[]{:S(2)}, u32[]{:S(2)}) collective-permute-start(f32[2,2,32,64]{3,2,1,0:T(8,128)S(1)} %pad_maximum_fusion.3), channel_id=1, source_target_pairs={{0,32},{16,48},{32,0},{48,16},{64,96},{80,112},{96,64},{112,80},{1... | collective-permute-start | bytes 98312 | tf_op jit(solution)/shard_map/ppermute | solution.py:295
  48.1 2.1 %collective-permute-done.13 = f32[3,32,256]{2,1,0:T(8,128)S(1)} collective-permute-done((f32[3,32,256]{2,1,0:T(8,128)S(1)}, f32[3,32,256]{2,1,0:T(8,128)S(1)}, u32[]{:S(2)}, u32[]{:S(2)}) %collective-permute-start.13) | collective-permute-done | bytes 98336 | tf_op jit(solution)/shard_map/ppermute | solution.py:301
  53.4 7.1 %collective-permute-done.14.refs_1_ = f32[3,32,256]{2,1,0:T(8,128)S(1)} collective-permute-done((f32[3,32,256]{2,1,0:T(8,128)S(1)}, f32[3,32,256]{2,1,0:T(8,128)S(1)}, u32[]{:S(2)}, u32[]{:S(2)}) %collective-permute-start.14) | collective-permute-done | bytes 98336 | tf_op jit(solution)/shard_map/ppermute | solution.py:417
  61.9 1.6 %collective-permute-start.18 = (f32[3,32,256]{2,1,0:T(8,128)S(1)}, f32[3,32,256]{2,1,0:T(8,128)S(1)}, u32[]{:S(2)}, u32[]{:S(2)}) collective-permute-start(f32[3,32,256]{2,1,0:T(8,128)S(1)} %get-tuple-element.85), channel_id=1, source_target_pairs={{0,15},{1,2},{2,1},{3,4},{4,3},{5,6},{6,5},{7,8},{8,7},{9,10},{10,... | collective-permute-start | bytes 294920 | tf_op jit(solution)/shard_map/ppermute | solution.py:301
  63.5 1.4 %adjoint_local.6 = (f32[3,32,256]{2,1,0:T(8,128)S(1)}, f32[3,32,256]{2,1,0:T(8,128)S(1)}) custom-call(f32[3,32,256]{2,1,0:T(8,128)S(1)} %get-tuple-element.79.refs_0_, f32[3,32,256]{2,1,0:T(8,128)S(1)} %get-tuple-element.80.refs_1_, bf16[42,256,256]{2,1,0:T(8,128)(2,1)S(1)} %get-tuple-element.53.refs_3_.refs_2_.high_ref, ...), custom_call_target="tpu_custom_call" | custom-call | flops 1000000000 | bytes 100000 | tf_op jit(solution)/shard_map/adjoint_local/pallas_call | solution.py:428
  67.5 1.6 %collective-permute-start.19 = (f32[3,32,256]{2,1,0:T(8,128)S(1)}, f32[3,32,256]{2,1,0:T(8,128)S(1)}, u32[]{:S(2)}, u32[]{:S(2)}) collective-permute-start(f32[3,32,256]{2,1,0:T(8,128)S(1)} %get-tuple-element.91), channel_id=1, source_target_pairs={{0,15},{1,2},{2,1},{3,4},{4,3},{5,6},{6,5},{7,8},{8,7},{9,10},{10,... | collective-permute-start | bytes 294920 | tf_op jit(solution)/shard_map/ppermute | solution.py:301
  71.0 1.3 %adjoint_local.7 = (f32[3,32,256]{2,1,0:T(8,128)S(1)}, f32[3,32,256]{2,1,0:T(8,128)S(1)}) custom-call(f32[3,32,256]{2,1,0:T(8,128)S(1)} %get-tuple-element.86.refs_0_, f32[3,32,256]{2,1,0:T(8,128)S(1)} %get-tuple-element.87.refs_1_, bf16[42,256,256]{2,1,0:T(8,128)(2,1)S(1)} %get-tuple-element.53.refs_3_.refs_2_.high_ref, ...), custom_call_target="tpu_custom_call" | custom-call | flops 1000000000 | bytes 100000 | tf_op jit(solution)/shard_map/adjoint_local/pallas_call | solution.py:434
  72.4 2.3 %collective-permute-done.26 = f32[32,256]{1,0:T(8,128)S(1)} collective-permute-done((f32[32,256]{1,0:T(8,128)S(1)}, f32[32,256]{1,0:T(8,128)S(1)}, u32[]{:S(2)}, u32[]{:S(2)}) %collective-permute-start.26) | collective-permute-done | bytes 32800 | tf_op jit(solution)/shard_map/ppermute | solution.py:295
  74.7 1.7 %collective-permute-start.27 = (f32[32,256]{1,0:T(8,128)S(1)}, f32[32,256]{1,0:T(8,128)S(1)}, u32[]{:S(2)}, u32[]{:S(2)}) collective-permute-start(f32[32,256]{1,0:T(8,128)S(1)} %add.26), channel_id=1, source_target_pairs={{0,12},{1,13},{2,14},{3,15},{4,8},{5,9},{6,10},{7,11},{8,4},{9,5},... | collective-permute-start | bytes 98312 | tf_op jit(solution)/shard_map/ppermute | solution.py:295
  77.7 3.1 %collective-permute-done.27 = f32[32,256]{1,0:T(8,128)S(1)} collective-permute-done((f32[32,256]{1,0:T(8,128)S(1)}, f32[32,256]{1,0:T(8,128)S(1)}, u32[]{:S(2)}, u32[]{:S(2)}) %collective-permute-start.27) | collective-permute-done | bytes 32800 | tf_op jit(solution)/shard_map/ppermute | solution.py:295
  80.8 5.4 %collective-permute-done.28.rest_ref = f32[32,256]{1,0:T(8,128)S(1)} collective-permute-done((f32[32,256]{1,0:T(8,128)S(1)}, f32[32,256]{1,0:T(8,128)S(1)}, u32[]{:S(2)}, u32[]{:S(2)}) %collective-permute-start.28) | collective-permute-done | bytes 32800 | tf_op jit(solution)/shard_map/ppermute | solution.py:295
  (77 shorter events, 21.4 us)
Async XLA Ops:
  1.6 11.3 %collective-permute-start = (f32[3,32,256]{2,1,0:T(8,128)S(1)}, f32[3,32,256]{2,1,0:T(8,128)S(1)}, u32[]{:S(2)}, u32[]{:S(2)}) collective-permute-start(f32[3,32,256]{2,1,0:T(8,128)S(1)} %get-tuple-element.52.refs_1_), channel_id=1, source_target_pairs={{0,1},{1,0},{2,3},{3,2},{4,5},{5,4},{6,7},{7,6},{8,9},{9,8},{10,11... | collective-permute-start | bytes 294920 | tf_op jit(solution)/shard_map/ppermute | solution.py:295
  1.7 14.2 %collective-permute-start.1 = (f32[3,32,256]{2,1,0:T(8,128)S(1)}, f32[3,32,256]{2,1,0:T(8,128)S(1)}, u32[]{:S(2)}, u32[]{:S(2)}) collective-permute-start(f32[3,32,256]{2,1,0:T(8,128)S(1)} %get-tuple-element.51.refs_0_), channel_id=1, source_target_pairs={{0,15},{1,2},{2,1},{3,4},{4,3},{5,6},{6,5},{7,8},{8,7},{9,10},{10,... | collective-permute-start | bytes 294920 | tf_op jit(solution)/shard_map/ppermute | solution.py:301
  16.4 5.3 %collective-permute-start.3 = (f32[3,32,256]{2,1,0:T(8,128)S(1)}, f32[3,32,256]{2,1,0:T(8,128)S(1)}, u32[]{:S(2)}, u32[]{:S(2)}) collective-permute-start(f32[3,32,256]{2,1,0:T(8,128)S(1)} %tangent_far.4.refs_0_), channel_id=1, source_target_pairs={{0,15},{1,2},{2,1},{3,4},{4,3},{5,6},{6,5},{7,8},{8,7},{9,10},{10,... | collective-permute-start | bytes 294920 | tf_op jit(solution)/shard_map/ppermute | solution.py:301
  20.4 3.7 %collective-permute-start.5 = (f32[3,32,256]{2,1,0:T(8,128)S(1)}, f32[3,32,256]{2,1,0:T(8,128)S(1)}, u32[]{:S(2)}, u32[]{:S(2)}) collective-permute-start(f32[3,32,256]{2,1,0:T(8,128)S(1)} %get-tuple-element.58.inner0_ref), channel_id=1, source_target_pairs={{0,128},{1,129},{2,130},{3,131},{4,132},{5,133},{6,134},{7,135},{8... | collective-permute-start | bytes 294920 | tf_op jit(solution)/shard_map/ppermute | solution.py:392
  22.3 3.7 %collective-permute-start.4 = (f32[3,32,256]{2,1,0:T(8,128)S(1)}, f32[3,32,256]{2,1,0:T(8,128)S(1)}, u32[]{:S(2)}, u32[]{:S(2)}) collective-permute-start(f32[3,32,256]{2,1,0:T(8,128)S(1)} %tangent_far.5.outer0_ref), channel_id=1, source_target_pairs={{0,128},{1,129},{2,130},{3,131},{4,132},{5,133},{6,134},{7,135},{8... | collective-permute-start | bytes 294920 | tf_op jit(solution)/shard_map/ppermute | solution.py:393
  24.2 3.6 %collective-permute-start.6 = (f32[3,32,256]{2,1,0:T(8,128)S(1)}, f32[3,32,256]{2,1,0:T(8,128)S(1)}, u32[]{:S(2)}, u32[]{:S(2)}) collective-permute-start(f32[3,32,256]{2,1,0:T(8,128)S(1)} %collective-permute-done.5.refs_1_), channel_id=1, source_target_pairs={{0,1},{1,0},{2,3},{3,2},{4,5},{5,4},{6,7},{7,6},{8,9},{9,8},{10,11... | collective-permute-start | bytes 294920 | tf_op jit(solution)/shard_map/ppermute | solution.py:295
  26.1 5.3 %collective-permute-start.7 = (f32[3,32,256]{2,1,0:T(8,128)S(1)}, f32[3,32,256]{2,1,0:T(8,128)S(1)}, u32[]{:S(2)}, u32[]{:S(2)}) collective-permute-start(f32[3,32,256]{2,1,0:T(8,128)S(1)} %collective-permute-done.4.refs_0_), channel_id=1, source_target_pairs={{0,15},{1,2},{2,1},{3,4},{4,3},{5,6},{6,5},{7,8},{8,7},{9,10},{10,... | collective-permute-start | bytes 294920 | tf_op jit(solution)/shard_map/ppermute | solution.py:301
  27.8 5.3 %collective-permute-start.8 = (f32[3,32,256]{2,1,0:T(8,128)S(1)}, f32[3,32,256]{2,1,0:T(8,128)S(1)}, u32[]{:S(2)}, u32[]{:S(2)}) collective-permute-start(f32[3,32,256]{2,1,0:T(8,128)S(1)} %get-tuple-element.60.refs_1_), channel_id=1, source_target_pairs={{0,1},{1,0},{2,3},{3,2},{4,5},{5,4},{6,7},{7,6},{8,9},{9,8},{10,11... | collective-permute-start | bytes 294920 | tf_op jit(solution)/shard_map/ppermute | solution.py:295
  31.3 5.3 %collective-permute-start.9 = (f32[3,32,256]{2,1,0:T(8,128)S(1)}, f32[3,32,256]{2,1,0:T(8,128)S(1)}, u32[]{:S(2)}, u32[]{:S(2)}) collective-permute-start(f32[3,32,256]{2,1,0:T(8,128)S(1)} %tangent_far.6.refs_0_), channel_id=1, source_target_pairs={{0,15},{1,2},{2,1},{3,4},{4,3},{5,6},{6,5},{7,8},{8,7},{9,10},{10,... | collective-permute-start | bytes 294920 | tf_op jit(solution)/shard_map/ppermute | solution.py:301
  39.5 5.3 %collective-permute-start.12 = (f32[3,32,256]{2,1,0:T(8,128)S(1)}, f32[3,32,256]{2,1,0:T(8,128)S(1)}, u32[]{:S(2)}, u32[]{:S(2)}) collective-permute-start(f32[3,32,256]{2,1,0:T(8,128)S(1)} %seen_outer.1), channel_id=1, source_target_pairs={{0,15},{1,2},{2,1},{3,4},{4,3},{5,6},{6,5},{7,8},{8,7},{9,10},{10,... | collective-permute-start | bytes 294920 | tf_op jit(solution)/shard_map/ppermute | solution.py:301
  42.7 3.9 %collective-permute-start.22 = (f32[1,2,32,64]{3,2,1,0:T(8,128)S(1)}, f32[1,2,32,64]{3,2,1,0:T(8,128)S(1)}, u32[]{:S(2)}, u32[]{:S(2)}) collective-permute-start(f32[1,2,32,64]{3,2,1,0:T(8,128)S(1)} %maximum_bitcast_fusion), channel_id=1, source_target_pairs={{0,16},{16,0},{32,48},{48,32},{64,80},{80,64},{96,112},{112,96},{1... | collective-permute-start | bytes 49160 | tf_op jit(solution)/shard_map/ppermute | solution.py:295
  44.8 5.3 %collective-permute-start.13 = (f32[3,32,256]{2,1,0:T(8,128)S(1)}, f32[3,32,256]{2,1,0:T(8,128)S(1)}, u32[]{:S(2)}, u32[]{:S(2)}) collective-permute-start(f32[3,32,256]{2,1,0:T(8,128)S(1)} %get-tuple-element.73), channel_id=1, source_target_pairs={{0,15},{1,2},{2,1},{3,4},{4,3},{5,6},{6,5},{7,8},{8,7},{9,10},{10,... | collective-permute-start | bytes 294920 | tf_op jit(solution)/shard_map/ppermute | solution.py:301
  46.7 6.1 %collective-permute-start.23 = (f32[2,2,32,64]{3,2,1,0:T(8,128)S(1)}, f32[2,2,32,64]{3,2,1,0:T(8,128)S(1)}, u32[]{:S(2)}, u32[]{:S(2)}) collective-permute-start(f32[2,2,32,64]{3,2,1,0:T(8,128)S(1)} %pad_maximum_fusion.3), channel_id=1, source_target_pairs={{0,32},{16,48},{32,0},{48,16},{64,96},{80,112},{96,64},{112,80},{1... | collective-permute-start | bytes 98312 | tf_op jit(solution)/shard_map/ppermute | solution.py:295
  50.2 10.3 %collective-permute-start.14 = (f32[3,32,256]{2,1,0:T(8,128)S(1)}, f32[3,32,256]{2,1,0:T(8,128)S(1)}, u32[]{:S(2)}, u32[]{:S(2)}) collective-permute-start(f32[3,32,256]{2,1,0:T(8,128)S(1)} %add.21), channel_id=1, source_target_pairs={{128,0},{129,1},{130,2},{131,3},{132,4},{133,5},{134,6},{135,7},{1... | collective-permute-start | bytes 294920 | tf_op jit(solution)/shard_map/ppermute | solution.py:417
  51.5 10.0 %collective-permute-start.15 = (f32[3,32,256]{2,1,0:T(8,128)S(1)}, f32[3,32,256]{2,1,0:T(8,128)S(1)}, u32[]{:S(2)}, u32[]{:S(2)}) collective-permute-start(f32[3,32,256]{2,1,0:T(8,128)S(1)} %add.22), channel_id=1, source_target_pairs={{128,0},{129,1},{130,2},{131,3},{132,4},{133,5},{134,6},{135,7},{1... | collective-permute-start | bytes 294920 | tf_op jit(solution)/shard_map/ppermute | solution.py:420
  52.8 12.6 %collective-permute-start.24 = (f32[4,2,32,64]{3,2,1,0:T(8,128)S(1)}, f32[4,2,32,64]{3,2,1,0:T(8,128)S(1)}, u32[]{:S(2)}, u32[]{:S(2)}) collective-permute-start(f32[4,2,32,64]{3,2,1,0:T(8,128)S(1)} %pad_maximum_fusion.2), channel_id=1, source_target_pairs={{0,96},{16,112},{32,64},{48,80},{64,32},{80,48},{96,0},{112,16},{1... | collective-permute-start | bytes 196616 | tf_op jit(solution)/shard_map/ppermute | solution.py:295
  60.8 4.0 %collective-permute-start.16 = (f32[3,32,256]{2,1,0:T(8,128)S(1)}, f32[3,32,256]{2,1,0:T(8,128)S(1)}, u32[]{:S(2)}, u32[]{:S(2)}) collective-permute-start(f32[3,32,256]{2,1,0:T(8,128)S(1)} %get-tuple-element.75), channel_id=1, source_target_pairs={{0,1},{1,0},{2,3},{3,2},{4,5},{5,4},{6,7},{7,6},{8,9},{9,8},{10,11... | collective-permute-start | bytes 294920 | tf_op jit(solution)/shard_map/ppermute | solution.py:295
  61.9 5.3 %collective-permute-start.18 = (f32[3,32,256]{2,1,0:T(8,128)S(1)}, f32[3,32,256]{2,1,0:T(8,128)S(1)}, u32[]{:S(2)}, u32[]{:S(2)}) collective-permute-start(f32[3,32,256]{2,1,0:T(8,128)S(1)} %get-tuple-element.85), channel_id=1, source_target_pairs={{0,15},{1,2},{2,1},{3,4},{4,3},{5,6},{6,5},{7,8},{8,7},{9,10},{10,... | collective-permute-start | bytes 294920 | tf_op jit(solution)/shard_map/ppermute | solution.py:301
  65.8 4.0 %collective-permute-start.25 = (f32[32,256]{1,0:T(8,128)S(1)}, f32[32,256]{1,0:T(8,128)S(1)}, u32[]{:S(2)}, u32[]{:S(2)}) collective-permute-start(f32[32,256]{1,0:T(8,128)S(1)} %gram_part.1), channel_id=1, source_target_pairs={{0,2},{1,3},{2,0},{3,1},{4,6},{5,7},{6,4},{7,5},{8,10},{9,11},{10,... | collective-permute-start | bytes 98312 | tf_op jit(solution)/shard_map/ppermute | solution.py:295
  67.5 7.1 %collective-permute-start.19 = (f32[3,32,256]{2,1,0:T(8,128)S(1)}, f32[3,32,256]{2,1,0:T(8,128)S(1)}, u32[]{:S(2)}, u32[]{:S(2)}) collective-permute-start(f32[3,32,256]{2,1,0:T(8,128)S(1)} %get-tuple-element.91), channel_id=1, source_target_pairs={{0,15},{1,2},{2,1},{3,4},{4,3},{5,6},{6,5},{7,8},{8,7},{9,10},{10,... | collective-permute-start | bytes 294920 | tf_op jit(solution)/shard_map/ppermute | solution.py:301
  69.9 4.8 %collective-permute-start.26 = (f32[32,256]{1,0:T(8,128)S(1)}, f32[32,256]{1,0:T(8,128)S(1)}, u32[]{:S(2)}, u32[]{:S(2)}) collective-permute-start(f32[32,256]{1,0:T(8,128)S(1)} %add.25), channel_id=1, source_target_pairs={{0,4},{1,5},{2,6},{3,7},{4,0},{5,1},{6,2},{7,3},{8,12},{9,13},{10,... | collective-permute-start | bytes 98312 | tf_op jit(solution)/shard_map/ppermute | solution.py:295
  74.7 6.1 %collective-permute-start.27 = (f32[32,256]{1,0:T(8,128)S(1)}, f32[32,256]{1,0:T(8,128)S(1)}, u32[]{:S(2)}, u32[]{:S(2)}) collective-permute-start(f32[32,256]{1,0:T(8,128)S(1)} %add.26), channel_id=1, source_target_pairs={{0,12},{1,13},{2,14},{3,15},{4,8},{5,9},{6,10},{7,11},{8,4},{9,5},... | collective-permute-start | bytes 98312 | tf_op jit(solution)/shard_map/ppermute | solution.py:295
  76.4 9.8 %collective-permute-start.20 = (f32[6,32,128]{2,1,0:T(8,128)S(1)}, f32[6,32,128]{2,1,0:T(8,128)S(1)}, u32[]{:S(2)}, u32[]{:S(2)}) collective-permute-start(f32[6,32,128]{2,1,0:T(8,128)S(1)} %fusion), channel_id=1, source_target_pairs={{0,128},{1,129},{2,130},{3,131},{4,132},{5,133},{6,134},{7,135},{8... | collective-permute-start | bytes 294920 | tf_op jit(solution)/shard_map/ppermute | solution.py:439
  80.8 5.4 %collective-permute-start.28 = (f32[32,256]{1,0:T(8,128)S(1)}, f32[32,256]{1,0:T(8,128)S(1)}, u32[]{:S(2)}, u32[]{:S(2)}) collective-permute-start(f32[32,256]{1,0:T(8,128)S(1)} %add.27.gram_ref), channel_id=1, source_target_pairs={{0,128},{128,0},{1,129},{129,1},{2,130},{130,2},{3,131},{131,3},{4... | collective-permute-start | bytes 98312 | tf_op jit(solution)/shard_map/ppermute | solution.py:295
  (8 other events, 12.7 us)
